TPU v7x, 256 devices: a whole 4x4x8 slice. The times are simulated.
256 devices in a mesh: replica: 2 (over z_lo), segment: 4 (over z_hi), tensor: 32 (over x, y, core).
Axes of the slice: x: 4, y: 4, z: 8 (z_hi: 4, z_lo: 2; z = z_hi * 2 + z_lo), core: 2. Of those that a mesh axis runs over, the one named last changes fastest.
Arguments:
- x_in: bfloat16 [256, 8192], P('replica', 'tensor'), parts along dimension 0, may hold values from -6 to 6
- norm_gain: float32 [4, 8192], P('segment'), may hold values from 0.5 to 1.5
- in_index: int32 [4, 224, 72], P('segment', 'tensor'), may hold values from -1 to 127, as said below
- gate_blocks: bfloat16 [4, 224, 72, 4096], P('segment', 'tensor'), may hold values from -0.09375 to 0.09375
- up_blocks: bfloat16 [4, 224, 72, 4096], P('segment', 'tensor'), may hold values from -0.09375 to 0.09375
- out_index: int32 [4, 128, 126], P('segment', 'tensor'), may hold values from -1 to 223, as said below
- down_blocks: bfloat16 [4, 128, 126, 4096], P('segment', 'tensor'), may hold values from -0.0625 to 0.0625
Outputs:
- sections: bfloat16 [4, 256, 8192], P('segment', 'replica', 'tensor'), parts along dimension 1
There are 2 independent parts, one for each index of `replica`. A program takes and returns all parts, laid end to end along the dimension named above; an argument that names none is the same for every part. Nothing has to cross between parts.
Inputs may be any that keep to these rules, and one draw needn't show every extreme that they name: `in_index`: for each section and column block the entries name distinct row blocks, the kept ones first and -1 in the remaining slots; between 3 * 128 / 8 (rounded down) and 72 slots are kept, and in every section some column block keeps exactly 72 and another exactly the least. `out_index`: for each section and column block the entries name distinct row blocks, the kept ones first and -1 in the remaining slots; between 3 * 224 / 8 (rounded down) and 126 slots are kept, and in every section some column block keeps exactly 126 and another exactly the least.
All inputs are finite; a program needn't handle non-finite values.
Results may differ from a plain program's by a relative error of at most 0.0095.
Values may be sent and summed in bfloat16 or wider, within the bound.
No kernel may reach another device: no remote copies, remote signals or barrier semaphores. Data moves between devices by JAX's collectives and lax.ppermute only.
A program may use at most 128 MiB of HBM per device.

v0:
```python
import jax
import jax.numpy as jnp
from jax import lax
from jax.sharding import PartitionSpec as P

D = 8192
FFW = 14336
BS = 64


def shifted(value, axis, by):
    length = lax.axis_size(axis)
    pairs = [(i, i + by) for i in range(length) if 0 <= i + by < length]
    return lax.ppermute(value, axis, pairs)


def densify(index, blocks, row_blocks):
    tile_count = index.shape[0]
    picks = (index[:, None, :] == jnp.arange(row_blocks, dtype=jnp.int32)[None, :, None]).astype(
        jnp.bfloat16
    )
    dense = jnp.einsum("crm,cmq->crq", picks, blocks, preferred_element_type=jnp.bfloat16)
    dense = dense.reshape(tile_count, row_blocks, BS, BS)
    return jnp.transpose(dense, (1, 2, 0, 3)).reshape(row_blocks * BS, tile_count * BS)


def local(x_in, norm_gain, in_index, gate_blocks, up_blocks, out_index, down_blocks):
    segment_count = lax.axis_size("segment")
    segment_at = lax.axis_index("segment")
    tokens, local_cols = x_in.shape
    gain_row = norm_gain[0]
    index_in = in_index[0]
    index_out = out_index[0]
    gate_dense = densify(index_in, gate_blocks[0], D // BS)
    up_dense = densify(index_in, up_blocks[0], D // BS)
    down_dense = densify(index_out, down_blocks[0], FFW // BS)
    rows_micro = tokens // 2
    group_count = tokens // rows_micro
    tick_count = group_count + segment_count - 1
    result = jnp.zeros((tokens, local_cols), jnp.bfloat16)
    carried = jnp.zeros((rows_micro, local_cols), jnp.bfloat16)
    for tick_now in range(tick_count):
        first_group = min(tick_now, group_count - 1)
        first_rows = x_in[first_group * rows_micro : (first_group + 1) * rows_micro]
        incoming = jnp.where(segment_at == 0, first_rows, carried)
        whole = lax.all_gather(incoming, "tensor", axis=1, tiled=True)
        wide = whole.astype(jnp.float32)
        stat = jnp.mean(wide * wide, axis=1, keepdims=True)
        section_normed = (wide * lax.rsqrt(stat + 1e-05) * gain_row[None, :]).astype(jnp.bfloat16)
        gate = jnp.dot(section_normed, gate_dense, preferred_element_type=jnp.float32)
        up_part = jnp.dot(section_normed, up_dense, preferred_element_type=jnp.float32)
        section_hidden = (jax.nn.silu(gate) * up_part).astype(jnp.bfloat16)
        mixed = jnp.dot(
            lax.all_gather(section_hidden, "tensor", axis=1, tiled=True),
            down_dense,
            preferred_element_type=jnp.float32,
        )
        produced = (incoming.astype(jnp.float32) + mixed).astype(jnp.bfloat16)
        micro_id = tick_now - segment_at
        is_valid = jnp.logical_and(micro_id >= 0, micro_id < group_count)
        offset = jnp.clip(micro_id, 0, group_count - 1) * rows_micro
        previous = lax.dynamic_slice_in_dim(result, offset, rows_micro, 0)
        result = lax.dynamic_update_slice_in_dim(
            result, jnp.where(is_valid, produced, previous), offset, 0
        )
        if tick_now + 1 < tick_count:
            carried = shifted(produced, "segment", 1)
    return result[None]


def solution(mesh):
    placed = (
        P("replica", "tensor"),
        P("segment", None),
        P("segment", "tensor", None),
        P("segment", "tensor", None, None),
        P("segment", "tensor", None, None),
        P("segment", "tensor", None),
        P("segment", "tensor", None, None),
    )
    return jax.shard_map(
        local,
        mesh=mesh,
        in_specs=placed,
        out_specs=P("segment", "replica", "tensor"),
        check_vma=False,
    )
```

profile of v0, /device:TPU:65, one launch (start us, length us, event | category | flops | bytes accessed | tf_op | source)
XLA Modules:
  0.0 694.7 jit_solution(13553117329584117888)
XLA Ops:
  8.7 7.7 %fusion.4 = bf16[7,128,4096]{1,2,0:T(8,128)(2,1)} fusion(bf16[1,7,72,4096]{3,2,1,0:T(8,128)(2,1)} %param.10, s32[7,72]{1,0:T(8,128)S(1)} %bitcast.103), kind=kOutput, calls=%fused_computation.4 | convolution fusion | flops 528546816 | bytes 11470816 | tf_op jit(solution)/shard_map/crm,cmq->crq/dot_general | solution.py:22
  16.4 15.6 %copy.22 = bf16[128,64,7,64]{1,0,3,2:T(8,128)(2,1)} copy(bf16[128,64,7,64]{0,3,1,2:T(8,128)(2,1)} %bitcast.90) | data formatting | bytes 14680064 | tf_op jit(solution)/shard_map/transpose | solution.py:24
  32.0 20.0 %reshape.63 = bf16[8192,448]{0,1:T(8,128)(2,1)} reshape(bf16[128,64,7,64]{1,0,3,2:T(8,128)(2,1)} %copy.22) | data formatting | bytes 14680064 | tf_op jit(solution)/shard_map/reshape | solution.py:24
  52.0 7.8 %fusion.2 = bf16[7,128,4096]{1,2,0:T(8,128)(2,1)} fusion(bf16[1,7,72,4096]{3,2,1,0:T(8,128)(2,1)} %param.11, s32[7,72]{1,0:T(8,128)S(1)} %bitcast.104), kind=kOutput, calls=%fused_computation.2 | convolution fusion | flops 528546816 | bytes 11470816 | tf_op jit(solution)/shard_map/crm,cmq->crq/dot_general | solution.py:22
  59.8 15.6 %copy.24 = bf16[128,64,7,64]{1,0,3,2:T(8,128)(2,1)} copy(bf16[128,64,7,64]{0,3,1,2:T(8,128)(2,1)} %bitcast.89) | data formatting | bytes 14680064 | tf_op jit(solution)/shard_map/transpose | solution.py:24
  75.4 20.0 %reshape.65 = bf16[8192,448]{0,1:T(8,128)(2,1)} reshape(bf16[128,64,7,64]{1,0,3,2:T(8,128)(2,1)} %copy.24) | data formatting | bytes 14680064 | tf_op jit(solution)/shard_map/reshape | solution.py:24
  97.0 5.8 fusion.41
  105.9 9.4 %fusion = bf16[4,224,4096]{1,2,0:T(8,128)(2,1)} fusion(bf16[4,126,4096]{2,0,1:T(4,128)(2,1)} %bitcast.91, s32[4,126]{1,0:T(4,128)S(1)} %bitcast.105), kind=kOutput, calls=%fused_computation | convolution fusion | flops 924956928 | bytes 11470816 | tf_op jit(solution)/shard_map/crm,cmq->crq/dot_general | solution.py:22
  115.3 17.4 %copy.28 = bf16[224,64,4,64]{1,0,3,2:T(8,128)(2,1)} copy(bf16[224,64,4,64]{0,3,1,2:T(8,128)(2,1)} %bitcast.88) | data formatting | bytes 14680064 | tf_op jit(solution)/shard_map/transpose | solution.py:24
  132.7 18.6 %reshape.67 = bf16[14336,256]{0,1:T(8,128)(2,1)} reshape(bf16[224,64,4,64]{1,0,3,2:T(8,128)(2,1)} %copy.28) | data formatting | bytes 14680064 | tf_op jit(solution)/shard_map/reshape | solution.py:24
  151.3 5.7 all-gather.26.cloned.1.call-done
  163.1 6.0 select_dynamic-update-slice_fusion.3
  176.4 48.6 %all-gather.18.cloned.1.call-done = bf16[64,8192]{1,0:T(8,128)(2,1)} async-done(((bf16[64,256]{1,0:T(8,128)(2,1)}), bf16[64,8192]{1,0:T(8,128)(2,1)}) %all-gather.18.cloned.1.call-update) | async-done | bytes 1048592 | tf_op jit(solution)/shard_map/all_gather | solution.py:46
  226.6 5.7 fusion.38
  232.4 6.0 fusion.46
  238.4 48.1 %all-gather.28.cloned.1.call-done = bf16[32,448,64]{1,2,0:T(8,128)(2,1)} async-done(((bf16[1,448,64]{1,2,0:T(8,128)(2,1)}), bf16[32,448,64]{1,2,0:T(8,128)(2,1)}) %all-gather.28.cloned.1.call-update) | async-done | bytes 1835024 | tf_op jit(solution)/shard_map/all_gather | solution.py:54
  292.6 6.0 select_dynamic-update-slice_fusion.2
  305.7 48.8 %all-gather.20.cloned.1.call-done = bf16[64,8192]{1,0:T(8,128)(2,1)} async-done(((bf16[64,256]{1,0:T(8,128)(2,1)}), bf16[64,8192]{1,0:T(8,128)(2,1)}) %all-gather.20.cloned.1.call-update) | async-done | bytes 1048592 | tf_op jit(solution)/shard_map/all_gather | solution.py:46
  356.1 5.7 fusion.34
  361.8 6.0 fusion.47
  368.3 47.7 %all-gather.30.cloned.1.call-done = bf16[32,448,64]{1,2,0:T(8,128)(2,1)} async-done(((bf16[1,448,64]{1,2,0:T(8,128)(2,1)}), bf16[32,448,64]{1,2,0:T(8,128)(2,1)}) %all-gather.30.cloned.1.call-update) | async-done | bytes 1835024 | tf_op jit(solution)/shard_map/all_gather | solution.py:54
  422.1 6.0 select_dynamic-update-slice_fusion.1
  435.2 48.8 %all-gather.22.cloned.1.call-done = bf16[64,8192]{1,0:T(8,128)(2,1)} async-done(((bf16[64,256]{1,0:T(8,128)(2,1)}), bf16[64,8192]{1,0:T(8,128)(2,1)}) %all-gather.22.cloned.1.call-update) | async-done | bytes 1048592 | tf_op jit(solution)/shard_map/all_gather | solution.py:46
  485.6 5.7 fusion.30
  491.3 6.0 fusion.48
  497.4 48.1 %all-gather.32.cloned.1.call-done = bf16[32,448,64]{1,2,0:T(8,128)(2,1)} async-done(((bf16[1,448,64]{1,2,0:T(8,128)(2,1)}), bf16[32,448,64]{1,2,0:T(8,128)(2,1)}) %all-gather.32.cloned.1.call-update) | async-done | bytes 1835024 | tf_op jit(solution)/shard_map/all_gather | solution.py:54
  551.6 6.0 select_dynamic-update-slice_fusion
  564.8 48.7 %all-gather.24.cloned.1.call-done = bf16[64,8192]{1,0:T(8,128)(2,1)} async-done(((bf16[64,256]{1,0:T(8,128)(2,1)}), bf16[64,8192]{1,0:T(8,128)(2,1)}) %all-gather.24.cloned.1.call-update) | async-done | bytes 1048592 | tf_op jit(solution)/shard_map/all_gather | solution.py:46
  615.1 5.7 fusion.26
  620.8 6.0 fusion.49
  627.4 47.5 %all-gather.34.cloned.1.call-done = bf16[32,448,64]{1,2,0:T(8,128)(2,1)} async-done(((bf16[1,448,64]{1,2,0:T(8,128)(2,1)}), bf16[32,448,64]{1,2,0:T(8,128)(2,1)}) %all-gather.34.cloned.1.call-update) | async-done | bytes 1835024 | tf_op jit(solution)/shard_map/all_gather | solution.py:54
  681.1 6.6 fusion.52
  (86 shorter events, 73.3 us)
Async XLA Ops:
  6.5 88.8 %all-gather.16.cloned.1.call-start = ((), (), s32[]{:S(2)}) async-start(), calls=%async_computation | async-start | bytes 1081344 | tf_op jit(solution)/shard_map/all_gather | solution.py:46
  7.9 149.1 %all-gather.26.cloned.1.call-start = ((), (), s32[]{:S(2)}) async-start(), calls=%async_computation.5 | async-start | bytes 2162688 | tf_op jit(solution)/shard_map/all_gather | solution.py:54
  75.4 21.6 %copy-start.6 = (f32[1,8192]{1,0:T(1,128)S(1)}, f32[1,8192]{1,0:T(1,128)}, u32[]{:S(2)}) copy-start(f32[1,8192]{1,0:T(1,128)} %param.8) | copy-start | bytes 98308
  96.9 5.8 copy-start
  96.9 5.8 copy-start.1
  102.8 3.2 copy-start.13
  105.7 119.4 %all-gather.18.cloned.1.call-start = ((), (), s32[]{:S(2)}) async-start(), calls=%async_computation.1 | async-start | bytes 1081344 | tf_op jit(solution)/shard_map/all_gather | solution.py:46
  159.8 3.4 copy-start.12
  163.1 12.4 %copy-start.7 = (bf16[128,256]{1,0:T(8,128)(2,1)S(1)}, bf16[128,256]{1,0:T(8,128)(2,1)}, u32[]{:S(2)}) copy-start(bf16[128,256]{1,0:T(8,128)(2,1)} %param.7) | copy-start | bytes 196612
  169.2 6.4 collective-permute-start
  176.2 110.3 %all-gather.28.cloned.1.call-start = ((), (), s32[]{:S(2)}) async-start(), calls=%async_computation.6 | async-start | bytes 2162688 | tf_op jit(solution)/shard_map/all_gather | solution.py:54
  226.6 5.7 copy-start.3
  238.3 116.2 %all-gather.20.cloned.1.call-start = ((), (), s32[]{:S(2)}) async-start(), calls=%async_computation.2 | async-start | bytes 1081344 | tf_op jit(solution)/shard_map/all_gather | solution.py:46
  289.3 3.4 copy-start.10
  298.6 6.4 collective-permute-start.1
  305.7 110.3 %all-gather.30.cloned.1.call-start = ((), (), s32[]{:S(2)}) async-start(), calls=%async_computation.7 | async-start | bytes 2162688 | tf_op jit(solution)/shard_map/all_gather | solution.py:54
  356.1 5.7 copy-start.4
  367.8 116.2 %all-gather.22.cloned.1.call-start = ((), (), s32[]{:S(2)}) async-start(), calls=%async_computation.3 | async-start | bytes 1081344 | tf_op jit(solution)/shard_map/all_gather | solution.py:46
  418.8 3.4 copy-start.11
  428.1 6.4 collective-permute-start.2
  435.1 110.3 %all-gather.32.cloned.1.call-start = ((), (), s32[]{:S(2)}) async-start(), calls=%async_computation.8 | async-start | bytes 2162688 | tf_op jit(solution)/shard_map/all_gather | solution.py:54
  485.6 5.7 copy-start.5
  497.3 116.2 %all-gather.24.cloned.1.call-start = ((), (), s32[]{:S(2)}) async-start(), calls=%async_computation.4 | async-start | bytes 1081344 | tf_op jit(solution)/shard_map/all_gather | solution.py:46
  548.2 3.4 copy-start.9
  557.6 6.4 collective-permute-start.3
  564.6 110.3 %all-gather.34.cloned.1.call-start = ((), (), s32[]{:S(2)}) async-start(), calls=%async_computation.9 | async-start | bytes 2162688 | tf_op jit(solution)/shard_map/all_gather | solution.py:54
  615.0 5.7 copy-start.2
  677.7 3.4 copy-start.8
Sparse Core Ops, SparseCore 0:
  9.8 50.4 all-gather.15
  105.8 51.1 all-gather.25
  176.3 48.7 all-gather.17
  238.5 48.0 all-gather.27
  305.8 48.7 all-gather.19
  367.9 48.0 all-gather.29
  435.3 48.7 all-gather.21
  497.4 48.0 all-gather.31
  564.7 48.7 all-gather.23
  626.9 48.0 all-gather.33
where the time goes:
time: 708 us; the launch traced here: 695 us
  waiting for transfers between devices  396 us (56%)
  local copies, waits for them, and re-layouts  139 us (20%)
  matrix products  111 us (16%)
  starting transfers between devices  22.9 us (3%)
  between operations  14 us (2%)
  other arithmetic  11.5 us (2%)
    all_gather x5, waiting for transfers between devices, local(): lax.all_gather(section_hidden, 'tensor', axis=1, tiled=True)  197 us
    all_gather x5, waiting for transfers between devices, local(): whole = lax.all_gather(incoming, 'tensor', axis=1, tiled=True)  195 us
    reshape x3, local copies, waits for them, and re-layouts, densify(): jnp.transpose(dense, (1, 2, 0, 3)).reshape(row_blocks * BS, tile_count * BS)  58.6 us
    transpose x3, local copies, waits for them, and re-layouts, densify(): jnp.transpose(dense, (1, 2, 0, 3)).reshape(row_blocks * BS, tile_count * BS)  48.6 us
    dot_general x5, matrix products, local(): jnp.dot(lax.all_gather(section_hidden, 'tensor', axis=1, tiled=True), dow...  30.6 us
    dot_general x5, matrix products, local(): jnp.dot(section_normed, gate_dense, preferred_element_type=jnp.float32)  28.7 us
    dot_general x5, matrix products, local(): jnp.dot(section_normed, up_dense, preferred_element_type=jnp.float32)  26.7 us
    dot_general x3, matrix products, densify(): jnp.einsum('crm,cmq->crq', picks, blocks, preferred_element_type=jnp.bflo...  24.9 us
  transfers between devices with their start and end apart: 14, of which 13 were waited for; matrix products, arithmetic and copies ran while one was open for 19% of the time, Pallas kernels for 0%

commit v1 on v0

v1 whole, which is shorter than its diff:
```python
import functools

import jax
import jax.numpy as jnp
from jax import lax
from jax.experimental import pallas as pl
from jax.experimental.pallas import tpu as pltpu
from jax.sharding import PartitionSpec as P

D = 8192
FFW = 14336
BS = 64
CHIPS = 16
ROWS = 64
GU_ROWS = D // 2
GU_COLS = 14 * 128
DN_ROWS = 32 * 256
DN_COLS = 4 * 128
MIB = 1 << 20


def pack_target(kept, per_device, stride, rows):
    device = kept // per_device
    block = (device % 2) * CHIPS + device // 2
    return pl.multiple_of(
        jnp.where(kept >= 0, block * stride + (kept % per_device) * 32, rows - 32), 32
    )


def clear(target):
    rows, cols = target.shape

    def one(at, _):
        target[pl.ds(pl.multiple_of(at * 32, 32), 32), :] = jnp.zeros((32, cols), target.dtype)
        return 0

    lax.fori_loop(0, rows // 32, one, 0)


def wide_pack_kernel(index_ref, gate_hbm, up_hbm, target, buf, spread, sems):
    tiles, slots = index_ref.shape
    copies = []
    for which, source in enumerate((gate_hbm, up_hbm)):
        for tile in range(tiles):
            at = which * tiles + tile
            copies.append(pltpu.make_async_copy(source.at[tile], buf.at[at], sems.at[at]))
    for copy in copies:
        copy.start()
    clear(target)

    def place(chunk, count, first, half, tile, column):
        for part in range(32):
            spread[half, part * 16 : part * 16 + count, :] = chunk[:, part * 128 : (part + 1) * 128]
        for row in range(count):
            at = pack_target(index_ref[tile, first + row], 4, 128, target.shape[0])
            piece = spread[half, pl.ds(row, 32, stride=16), :]
            target[pl.ds(at, 32), pl.ds(column, 128)] = piece.astype(target.dtype)

    def one(at, _):
        pltpu.make_async_copy(gate_hbm.at[0], buf.at[at], sems.at[at]).wait()
        which = (at >= tiles).astype(jnp.int32)
        tile = at - which * tiles
        last = tiles - 1
        column = pl.multiple_of(jnp.where(tile == last, 2 * last + which, which * last + tile) * 128, 128)

        def pair(step, _):
            for half in range(2):
                first = pl.multiple_of(step * 32 + half * 16, 16)
                chunk = buf[at, pl.ds(first, 16), :].astype(jnp.float32)
                place(chunk, 16, first, half, tile, column)
            return 0

        lax.fori_loop(0, slots // 32, pair, 0)
        done = slots // 32 * 32
        half = 0
        while done < slots:
            count = min(16, slots - done)
            chunk = buf[at, done : done + count, :].astype(jnp.float32)
            place(chunk, count, done, half, tile, column)
            done += count
            half = 1 - half
        return 0

    lax.fori_loop(0, 2 * tiles, one, 0)


def down_pack_kernel(index_ref, source, target, buf, spread, sems):
    tiles, slots = index_ref.shape
    parts = 7
    size = slots // parts
    copies = [
        pltpu.make_async_copy(
            source.at[pl.ds(part * size, size)], buf.at[pl.ds(part * size, size)], sems.at[part]
        )
        for part in range(parts)
    ]
    for copy in copies:
        copy.start()
    clear(target)
    def one(part, _):
        pltpu.make_async_copy(
            source.at[pl.ds(0, size)], buf.at[pl.ds(part * size, size)], sems.at[part]
        ).wait()

        def step(at, _):
            for half in range(2):
                slot = part * size + at * 6 + half * 3
                for inner in range(3):
                    chunk = buf[slot + inner].astype(jnp.float32)
                    for lane in range(32):
                        spread[half, lane * 16 + inner * 4 : lane * 16 + inner * 4 + 4, :] = chunk[
                            :, lane * 128 : (lane + 1) * 128
                        ]
                for inner in range(3):
                    for tile in range(tiles):
                        goal = pack_target(index_ref[tile, slot + inner], 7, 256, target.shape[0])
                        piece = spread[half, pl.ds(inner * 4 + tile, 32, stride=16), :]
                        target[pl.ds(goal, 32), tile * 128 : (tile + 1) * 128] = piece.astype(target.dtype)
            return 0

        lax.fori_loop(0, size // 6, step, 0)
        return 0

    lax.fori_loop(0, parts, one, 0)


def pack(kernel, index, sources, buf, copies, shape, name):
    sources = [pltpu.with_memory_space_constraint(source, pltpu.HBM) for source in sources]
    return pl.pallas_call(
        kernel,
        out_shape=pltpu.VMEM(shape, jnp.bfloat16),
        in_specs=[pl.BlockSpec(memory_space=pltpu.SMEM)]
        + [pl.BlockSpec(memory_space=pltpu.HBM)] * len(sources),
        out_specs=pl.BlockSpec(memory_space=pltpu.VMEM),
        scratch_shapes=[
            pltpu.VMEM(buf, jnp.bfloat16),
            pltpu.VMEM((2, 32 * 16, 128), jnp.float32),
            pltpu.SemaphoreType.DMA((copies,)),
        ],
        compiler_params=pltpu.CompilerParams(vmem_limit_bytes=12 * MIB),
        cost_estimate=pl.CostEstimate(flops=0, bytes_accessed=40 * MIB, transcendentals=0),
        name=name,
    )(index, *sources)


def densify_wide(index, gate_blocks, up_blocks):
    tiles, slots = index.shape
    buf = (2 * tiles, slots, BS * BS)
    shape = (GU_ROWS + 32, GU_COLS)
    return pack(wide_pack_kernel, index, (gate_blocks, up_blocks), buf, 2 * tiles, shape, "pack_wide")


def densify_down(index, blocks):
    tiles, slots = index.shape
    shape = (DN_ROWS + 32, DN_COLS)
    blocks = jnp.transpose(blocks, (1, 0, 2))
    return pack(down_pack_kernel, index, (blocks,), (slots, tiles, BS * BS), 7, shape, "pack_down")


def densify(in_index, gate_blocks, up_blocks, out_index, down_blocks):
    return densify_wide(in_index, gate_blocks, up_blocks), densify_down(out_index, down_blocks)


def fold(even, odd, at):
    low = lax.broadcasted_iota(jnp.int32, (ROWS, 128), 1) < 64
    e0, e1 = even[:, at : at + 128], even[:, at + 128 : at + 256]
    o0, o1 = odd[:, at : at + 128], odd[:, at + 128 : at + 256]
    return jnp.where(low, e0, o1) + pltpu.roll(jnp.where(low, e1, o0), 64, 1)


def wide_kernel(core_ref, mine_ref, other_ref, gain_ref, weight_ref, order_ref, out_ref, normed):
    core = core_ref[0]
    total = jnp.zeros((2 * ROWS, 128), jnp.float32)
    for ref in (mine_ref, other_ref):
        for chip in range(CHIPS):
            value = ref[chip].astype(jnp.float32)
            total += value * value
    stat = jnp.sum(total[:ROWS] + total[ROWS:], axis=1, keepdims=True) / D
    scale = lax.rsqrt(stat + 1e-05)
    scale = jnp.concatenate([scale, scale], axis=0)
    starts = (core, 1 - core)
    for which, ref in enumerate((mine_ref, other_ref)):
        gains = gain_ref[pl.ds(pl.multiple_of(starts[which] * 32, 32), 32), :]
        for chip in range(CHIPS):
            gain = jnp.concatenate(
                [
                    jnp.broadcast_to(gains[2 * chip : 2 * chip + 1], (ROWS, 128)),
                    jnp.broadcast_to(gains[2 * chip + 1 : 2 * chip + 2], (ROWS, 128)),
                ],
                axis=0,
            )
            value = ref[chip].astype(jnp.float32) * scale * gain
            normed[which, :, chip * 128 : (chip + 1) * 128] = value.astype(jnp.bfloat16)

    def product(tile):
        acc = None
        for which in range(2):
            rows = pl.ds(pl.multiple_of(starts[which] * (GU_ROWS // 2), GU_ROWS // 2), GU_ROWS // 2)
            part = jnp.dot(
                normed[which],
                weight_ref[rows, tile * 256 : (tile + 1) * 256],
                preferred_element_type=jnp.float32,
            )
            acc = part if acc is None else acc + part
        return fold(acc[:ROWS], acc[ROWS:], 0)

    pieces = []
    for pair in range(3):
        gate = product(pair)
        up = product(pair + 3)
        pieces.append((gate / (1.0 + jnp.exp(-gate)) * up).astype(jnp.bfloat16))
    both = product(6)
    last = both / (1.0 + jnp.exp(-both)) * pltpu.roll(both, 64, 1)
    low = lax.broadcasted_iota(jnp.int32, (ROWS, 128), 1) < 64
    pieces.append(jnp.where(low, last, 0.0).astype(jnp.bfloat16))
    hidden = jnp.dot(
        jnp.concatenate(pieces, axis=1), order_ref[...], preferred_element_type=jnp.float32
    ).astype(jnp.bfloat16)
    hidden = jnp.concatenate([hidden[:, :256], hidden[:, 256:]], axis=0)
    for chip in range(CHIPS):
        out_ref[chip] = hidden


def down_kernel(core_ref, mine_ref, other_ref, weight_ref, taken_ref, order_ref, back_ref, out_ref, next_ref):
    core = core_ref[0]
    acc = None
    for ref, start in ((mine_ref, core), (other_ref, 1 - core)):
        rows = pl.ds(pl.multiple_of(start * (DN_ROWS // 2), DN_ROWS // 2), DN_ROWS // 2)
        left = jnp.concatenate([ref[chip] for chip in range(CHIPS)], axis=1)
        part = jnp.dot(left, weight_ref[rows, :], preferred_element_type=jnp.float32)
        acc = part if acc is None else acc + part
    even, odd = acc[:ROWS], acc[ROWS:]
    mixed = jnp.concatenate([fold(even, odd, 0), fold(even, odd, 256)], axis=1)
    taken = jnp.concatenate([taken_ref[:ROWS], taken_ref[ROWS:]], axis=1)
    taken = jnp.dot(taken, back_ref[...], preferred_element_type=jnp.float32)
    produced = (taken + mixed).astype(jnp.bfloat16)
    out_ref[...] = produced
    ordered = jnp.dot(produced, order_ref[...], preferred_element_type=jnp.float32).astype(jnp.bfloat16)
    next_ref[...] = jnp.concatenate([ordered[:, :128], ordered[:, 128:]], axis=0)


def call_wide(core, mine, other, gain, weight, order):
    vmem = pl.BlockSpec(memory_space=pltpu.VMEM)
    return pl.pallas_call(
        wide_kernel,
        out_shape=jax.ShapeDtypeStruct((CHIPS, 2 * ROWS, 256), jnp.bfloat16),
        in_specs=[pl.BlockSpec(memory_space=pltpu.SMEM)] + [vmem] * 5,
        out_specs=vmem,
        scratch_shapes=[pltpu.VMEM((2, 2 * ROWS, GU_ROWS // 2), jnp.bfloat16)],
        compiler_params=pltpu.CompilerParams(vmem_limit_bytes=24 * MIB),
        cost_estimate=pl.CostEstimate(flops=2 * 128 * GU_ROWS * GU_COLS, bytes_accessed=2 * MIB, transcendentals=0),
        name="wide",
    )(core, mine, other, gain, pltpu.with_memory_space_constraint(weight, pltpu.VMEM), order)


def call_down(core, mine, other, weight, taken, order, back):
    vmem = pl.BlockSpec(memory_space=pltpu.VMEM)
    return pl.pallas_call(
        down_kernel,
        out_shape=(
            jax.ShapeDtypeStruct((ROWS, 256), jnp.bfloat16),
            jax.ShapeDtypeStruct((2 * ROWS, 128), jnp.bfloat16),
        ),
        in_specs=[pl.BlockSpec(memory_space=pltpu.SMEM)] + [vmem] * 6,
        out_specs=(vmem, vmem),
        compiler_params=pltpu.CompilerParams(vmem_limit_bytes=24 * MIB),
        cost_estimate=pl.CostEstimate(flops=2 * 128 * DN_ROWS * DN_COLS, bytes_accessed=2 * MIB, transcendentals=0),
        name="down",
    )(core, mine, other, pltpu.with_memory_space_constraint(weight, pltpu.VMEM), taken, order, back)


def orders():
    source = jnp.arange(256)
    goal = (source % 2) * 128 + source // 64 * 32 + source % 64 // 2
    x_order = (goal[:, None] == jnp.arange(256)[None, :]).astype(jnp.bfloat16)
    source = jnp.arange(512)
    goal = (source % 2) * 256 + source // 64 * 32 + source % 64 // 2
    h_order = (goal[:, None] == jnp.arange(512)[None, :]).astype(jnp.bfloat16)
    return x_order, h_order


def gathered(value):
    same_core = [[2 * chip + core for chip in range(CHIPS)] for core in range(2)]
    mine = lax.all_to_all(value, "tensor", 0, 0, axis_index_groups=same_core)
    swap = [(i, i ^ 1) for i in range(2 * CHIPS)]
    return mine, lax.ppermute(mine, "tensor", swap)


def local(x_in, norm_gain, in_index, gate_blocks, up_blocks, out_index, down_blocks):
    segment_count = lax.axis_size("segment")
    segment_at = lax.axis_index("segment")
    core = (lax.axis_index("tensor") % 2).astype(jnp.int32)[None]
    tokens = x_in.shape[0]
    group_count = tokens // ROWS
    tick_count = group_count + segment_count - 1
    x_order, h_order = orders()
    x_back = x_order.T
    gain = jnp.dot(
        norm_gain[0].reshape(2 * CHIPS, 256), x_order.astype(jnp.float32), precision=lax.Precision.HIGHEST
    )
    gain = gain.reshape(CHIPS, 2, 2, 128).transpose(1, 0, 2, 3).reshape(4 * CHIPS, 128)
    x_ordered = jnp.dot(x_in, x_order, preferred_element_type=jnp.float32).astype(jnp.bfloat16)
    firsts = []
    for group in range(group_count):
        part = x_ordered[group * ROWS : (group + 1) * ROWS]
        firsts.append(jnp.concatenate([part[:, :128], part[:, 128:]], axis=0))
    here = [jnp.broadcast_to(segment_at == segment, (8, 128)).astype(jnp.bfloat16) for segment in range(segment_count)]
    in_index, out_index = in_index[0], out_index[0]
    in_index, out_index, core, x_order, x_back, h_order, gain, firsts, here = lax.optimization_barrier(
        (in_index, out_index, core, x_order, x_back, h_order, gain, firsts, here)
    )
    wide = densify_wide(in_index, gate_blocks[0], up_blocks[0])
    down = densify_down(out_index, down_blocks[0])
    firsts, wide, down = lax.optimization_barrier((firsts, wide, down))

    def is_here(segment, shape):
        return jnp.tile(here[segment], (shape[0] // 8, shape[1] // 128)) > 0

    carried = None
    made = []
    hops = [(i, i + 1) for i in range(segment_count - 1)]
    for tick in range(tick_count):
        taken = firsts[min(tick, group_count - 1)]
        if carried is not None:
            taken = jnp.where(is_here(0, taken.shape), taken, carried)
        mine, other = gathered(jnp.broadcast_to(taken[None], (CHIPS, 2 * ROWS, 128)))
        hidden = call_wide(core, mine, other, gain, wide, h_order)
        mine, other = gathered(hidden)
        produced, ordered = call_down(core, mine, other, down, taken, x_order, x_back)
        made.append(produced)
        if tick + 1 < tick_count:
            carried = lax.ppermute(ordered, "segment", hops)
    groups = []
    for group in range(group_count):
        chosen = made[group]
        for segment in range(1, segment_count):
            chosen = jnp.where(is_here(segment, chosen.shape), made[group + segment], chosen)
        groups.append(chosen)
    return jnp.concatenate(groups, axis=0)[None]


def solution(mesh):
    placed = (
        P("replica", "tensor"),
        P("segment", None),
        P("segment", "tensor", None),
        P("segment", "tensor", None, None),
        P("segment", "tensor", None, None),
        P("segment", "tensor", None),
        P("segment", "tensor", None, None),
    )
    return jax.shard_map(
        local,
        mesh=mesh,
        in_specs=placed,
        out_specs=P("segment", "replica", "tensor"),
        check_vma=False,
    )
```

time: 708 us -> 288 us (0.41); the launches traced: 695 us -> 287 us
  waiting for transfers between devices: 396 us -> 23.1 us
  blocking collectives: 0 us -> 160 us
  local copies, waits for them, and re-layouts: 139 us -> 2.43 us
  matrix products: 111 us -> 0.52 us
  Pallas kernels: 0 us -> 49.4 us
  starting transfers between devices: 22.9 us -> 49.6 us
  between operations: 14 us -> 0.36 us
  other arithmetic: 11.5 us -> 2.46 us
    all_gather x10 -> x0, waiting for transfers between devices: 392 us -> none  [the longest x5 197 us: local(): lax.all_gather(section_hidden, 'tensor', axis=1, tiled=True)]
    all_to_all x0 -> x10, blocking collectives: none -> 160 us  [gathered(): mine = lax.all_to_all(value, 'tensor', 0, 0, axis_index_groups=same_core)]
    dot_general x18 -> x2, matrix products: 111 us -> 0.52 us  [the longest x1 0.27 us: local(): jnp.dot(norm_gain[0].reshape(2 * CHIPS, 256), x_order.astype(jnp.float32)...]
    reshape x3 -> x2, local copies, waits for them, and re-layouts: 58.6 us -> 0.03 us  [local(): gain.reshape(CHIPS, 2, 2, 128).transpose(1, 0, 2, 3).reshape(4 * CHIPS, 128)]
    pallas_call x0 -> x12, Pallas kernels: none -> 49.4 us  [the longest x2 26.9 us: pack(): pl.pallas_call(kernel, out_shape=pltpu.VMEM(shape, jnp.bfloat16), in_spec...]
    transpose x3 -> x0, local copies, waits for them, and re-layouts: 48.6 us -> none  [densify(): jnp.transpose(dense, (1, 2, 0, 3)).reshape(row_blocks * BS, tile_count * BS)]
    ppermute x4 -> x14, starting transfers between devices: 21.5 us -> 49.6 us  [the longest x10 26.2 us: gathered(): return (mine, lax.ppermute(mine, 'tensor', swap))]
    ppermute x4 -> x14, waiting for transfers between devices: 4.01 us -> 23.1 us  [the longest x10 19.1 us: gathered(): return (mine, lax.ppermute(mine, 'tensor', swap))]
  transfers between devices with their start and end apart: 14 -> 14, of which waited for: 13 -> 14; matrix products, arithmetic and copies ran while one was open for 19% -> 0% of each run, Pallas kernels for 0% -> 0%
where the time goes in v1:
time: 288 us; the launch traced here: 287 us
  blocking collectives  160 us (56%)
  starting transfers between devices  49.6 us (17%)
  Pallas kernels  49.4 us (17%)
  waiting for transfers between devices  23.1 us (8%)
    all_to_all x10, blocking collectives, gathered(): mine = lax.all_to_all(value, 'tensor', 0, 0, axis_index_groups=same_core)  160 us
    pallas_call x2, Pallas kernels, pack(): pl.pallas_call(kernel, out_shape=pltpu.VMEM(shape, jnp.bfloat16), in_spec...  26.9 us
    ppermute x10, starting transfers between devices, gathered(): return (mine, lax.ppermute(mine, 'tensor', swap))  26.2 us
    ppermute x4, starting transfers between devices, local(): carried = lax.ppermute(ordered, 'segment', hops)  23.4 us
    ppermute x10, waiting for transfers between devices, gathered(): return (mine, lax.ppermute(mine, 'tensor', swap))  19.1 us
    pallas_call x5, Pallas kernels, call_wide(): pl.pallas_call(wide_kernel, out_shape=jax.ShapeDtypeStruct((CHIPS, 2 * RO...  14.6 us
    pallas_call x5, Pallas kernels, call_down(): pl.pallas_call(down_kernel, out_shape=(jax.ShapeDtypeStruct((ROWS, 256),...  7.81 us
  transfers between devices with their start and end apart: 14, of which 14 were waited for; matrix products, arithmetic and copies ran while one was open for 0% of the time, Pallas kernels for 0%

profile of v1, /device:TPU:65, one launch (start us, length us, event | category | flops | bytes accessed | tf_op | source)
XLA Modules:
  0.0 287.5 jit_solution(15862343016016267020)
XLA Ops:
  4.4 9.6 %pack_down.1.weight_ref = bf16[8224,512]{1,0:T(8,128)(2,1)S(1)} custom-call(s32[4,126]{1,0:T(4,128)S(1)} %bitcast.49, bf16[126,4,4096]{2,1,0:T(4,128)(2,1)} %bitcast.50), custom_call_target="tpu_custom_call" | custom-call | bytes 41943040 | tf_op jit(solution)/shard_map/pack_down/pallas_call | solution.py:129
  14.0 17.3 %pack_wide.1.weight_ref = bf16[4128,1792]{1,0:T(8,128)(2,1)S(1)} custom-call(s32[7,72]{1,0:T(8,128)S(1)} %bitcast.48, bf16[7,72,4096]{2,1,0:T(8,128)(2,1)} %bitcast.51, bf16[7,72,4096]{2,1,0:T(8,128)(2,1)} %bitcast.52), custom_call_target="tpu_custom_call" | custom-call | bytes 41943040 | tf_op jit(solution)/shard_map/pack_wide/pallas_call | solution.py:129
  31.4 16.9 %all_to_all.50.mine_ref = bf16[16,128,128]{2,1,0:T(8,128)(2,1)S(1)} all-to-all(bf16[16,128,128]{2,1,0:T(8,128)(2,1)S(1)} %broadcast_in_dim.27), channel_id=1, replica_groups={{0,2,4,6,8,10,12,14,16,18,20,22,24,26,28,30},{1,3,5,7,9,11,13,15,17,19,..., dimensions={0} | all-to-all | bytes 1048576 | tf_op jit(solution)/shard_map/all_to_all | solution.py:284
  48.4 2.1 collective-permute-start
  52.0 2.9 %wide.5 = bf16[16,128,256]{2,1,0:T(8,128)(2,1)S(1)} custom-call(s32[1]{0:T(128)} %bitcast.1.core_ref, bf16[16,128,128]{2,1,0:T(8,128)(2,1)S(1)} %all_to_all.50.mine_ref, bf16[16,128,128]{2,1,0:T(8,128)(2,1)S(1)} %collective-permute-done.other_ref, f32[64,128]{1,0:T(8,128)S(1)} %bitcast.43, bf16[4128,1792]{1,0:T(8,128)(2,1)S(1)} %pack_wide.1.weight_ref, ...), custom_call_target="tpu_custom_call" | custom-call | flops 1879048192 | bytes 2097152 | tf_op jit(solution)/shard_map/wide/pallas_call | solution.py:244
  54.9 19.0 %all_to_all.51.mine_ref = bf16[16,128,256]{2,1,0:T(8,128)(2,1)S(1)} all-to-all(bf16[16,128,256]{2,1,0:T(8,128)(2,1)S(1)} %wide.5), channel_id=1, replica_groups={{0,2,4,6,8,10,12,14,16,18,20,22,24,26,28,30},{1,3,5,7,9,11,13,15,17,19,..., dimensions={0} | all-to-all | bytes 2097152 | tf_op jit(solution)/shard_map/all_to_all | solution.py:284
  76.0 2.3 collective-permute-done.1.other_ref
  79.7 6.1 %collective-permute-start.2 = (bf16[128,128]{1,0:T(8,128)(2,1)S(1)}, bf16[128,128]{1,0:T(8,128)(2,1)S(1)}, u32[]{:S(2)}, u32[]{:S(2)}) collective-permute-start(bf16[128,128]{1,0:T(8,128)(2,1)S(1)} %get-tuple-element.46), channel_id=1, source_target_pairs={{0,32},{32,64},{64,96},{1,33},{33,65},{65,97},{2,34},{34,66},{66,9... | collective-permute-start | bytes 98312 | tf_op jit(solution)/shard_map/ppermute | solution.py:332
  87.0 12.0 %all_to_all.52.mine_ref = bf16[16,128,128]{2,1,0:T(8,128)(2,1)S(1)} all-to-all(bf16[16,128,128]{2,1,0:T(8,128)(2,1)S(1)} %broadcast_in_dim.28), channel_id=1, replica_groups={{0,2,4,6,8,10,12,14,16,18,20,22,24,26,28,30},{1,3,5,7,9,11,13,15,17,19,..., dimensions={0} | all-to-all | bytes 1048576 | tf_op jit(solution)/shard_map/all_to_all | solution.py:284
  98.9 3.5 %collective-permute-start.3 = (bf16[16,128,128]{2,1,0:T(8,128)(2,1)S(1)}, bf16[16,128,128]{2,1,0:T(8,128)(2,1)S(1)}, u32[]{:S(2)}, u32[]{:S(2)}) collective-permute-start(bf16[16,128,128]{2,1,0:T(8,128)(2,1)S(1)} %all_to_all.52.mine_ref), channel_id=1, source_target_pairs={{0,1},{1,0},{2,3},{3,2},{4,5},{5,4},{6,7},{7,6},{8,9},{9,8},{10,11... | collective-permute-start | bytes 1572872 | tf_op jit(solution)/shard_map/ppermute | solution.py:286
  103.9 2.9 %wide.6 = bf16[16,128,256]{2,1,0:T(8,128)(2,1)S(1)} custom-call(s32[1]{0:T(128)} %bitcast.1.core_ref, bf16[16,128,128]{2,1,0:T(8,128)(2,1)S(1)} %all_to_all.52.mine_ref, bf16[16,128,128]{2,1,0:T(8,128)(2,1)S(1)} %collective-permute-done.3.other_ref, f32[64,128]{1,0:T(8,128)S(1)} %bitcast.44, bf16[4128,1792]{1,0:T(8,128)(2,1)S(1)} %pack_wide.1.weight_ref, ...), custom_call_target="tpu_custom_call" | custom-call | flops 1879048192 | bytes 2097152 | tf_op jit(solution)/shard_map/wide/pallas_call | solution.py:244
  106.8 19.0 %all_to_all.53.mine_ref = bf16[16,128,256]{2,1,0:T(8,128)(2,1)S(1)} all-to-all(bf16[16,128,256]{2,1,0:T(8,128)(2,1)S(1)} %wide.6), channel_id=1, replica_groups={{0,2,4,6,8,10,12,14,16,18,20,22,24,26,28,30},{1,3,5,7,9,11,13,15,17,19,..., dimensions={0} | all-to-all | bytes 2097152 | tf_op jit(solution)/shard_map/all_to_all | solution.py:284
  125.8 2.1 collective-permute-start.4
  127.9 2.3 collective-permute-done.4.other_ref
  131.6 5.8 %collective-permute-start.5 = (bf16[128,128]{1,0:T(8,128)(2,1)S(1)}, bf16[128,128]{1,0:T(8,128)(2,1)S(1)}, u32[]{:S(2)}, u32[]{:S(2)}) collective-permute-start(bf16[128,128]{1,0:T(8,128)(2,1)S(1)} %get-tuple-element.47), channel_id=1, source_target_pairs={{0,32},{32,64},{64,96},{1,33},{33,65},{65,97},{2,34},{34,66},{66,9... | collective-permute-start | bytes 98312 | tf_op jit(solution)/shard_map/ppermute | solution.py:332
  138.5 12.0 %all_to_all.54.mine_ref = bf16[16,128,128]{2,1,0:T(8,128)(2,1)S(1)} all-to-all(bf16[16,128,128]{2,1,0:T(8,128)(2,1)S(1)} %broadcast_in_dim.29), channel_id=1, replica_groups={{0,2,4,6,8,10,12,14,16,18,20,22,24,26,28,30},{1,3,5,7,9,11,13,15,17,19,..., dimensions={0} | all-to-all | bytes 1048576 | tf_op jit(solution)/shard_map/all_to_all | solution.py:284
  150.4 3.5 %collective-permute-start.6 = (bf16[16,128,128]{2,1,0:T(8,128)(2,1)S(1)}, bf16[16,128,128]{2,1,0:T(8,128)(2,1)S(1)}, u32[]{:S(2)}, u32[]{:S(2)}) collective-permute-start(bf16[16,128,128]{2,1,0:T(8,128)(2,1)S(1)} %all_to_all.54.mine_ref), channel_id=1, source_target_pairs={{0,1},{1,0},{2,3},{3,2},{4,5},{5,4},{6,7},{7,6},{8,9},{9,8},{10,11... | collective-permute-start | bytes 1572872 | tf_op jit(solution)/shard_map/ppermute | solution.py:286
  155.4 2.9 %wide.7 = bf16[16,128,256]{2,1,0:T(8,128)(2,1)S(1)} custom-call(s32[1]{0:T(128)} %bitcast.1.core_ref, bf16[16,128,128]{2,1,0:T(8,128)(2,1)S(1)} %all_to_all.54.mine_ref, bf16[16,128,128]{2,1,0:T(8,128)(2,1)S(1)} %collective-permute-done.6.other_ref, f32[64,128]{1,0:T(8,128)S(1)} %bitcast.45, bf16[4128,1792]{1,0:T(8,128)(2,1)S(1)} %pack_wide.1.weight_ref, ...), custom_call_target="tpu_custom_call" | custom-call | flops 1879048192 | bytes 2097152 | tf_op jit(solution)/shard_map/wide/pallas_call | solution.py:244
  158.4 19.0 %all_to_all.55.mine_ref = bf16[16,128,256]{2,1,0:T(8,128)(2,1)S(1)} all-to-all(bf16[16,128,256]{2,1,0:T(8,128)(2,1)S(1)} %wide.7), channel_id=1, replica_groups={{0,2,4,6,8,10,12,14,16,18,20,22,24,26,28,30},{1,3,5,7,9,11,13,15,17,19,..., dimensions={0} | all-to-all | bytes 2097152 | tf_op jit(solution)/shard_map/all_to_all | solution.py:284
  179.4 2.3 collective-permute-done.7.other_ref
  183.1 5.8 %collective-permute-start.8 = (bf16[128,128]{1,0:T(8,128)(2,1)S(1)}, bf16[128,128]{1,0:T(8,128)(2,1)S(1)}, u32[]{:S(2)}, u32[]{:S(2)}) collective-permute-start(bf16[128,128]{1,0:T(8,128)(2,1)S(1)} %get-tuple-element.48), channel_id=1, source_target_pairs={{0,32},{32,64},{64,96},{1,33},{33,65},{65,97},{2,34},{34,66},{66,9... | collective-permute-start | bytes 98312 | tf_op jit(solution)/shard_map/ppermute | solution.py:332
  190.0 12.0 %all_to_all.56.mine_ref = bf16[16,128,128]{2,1,0:T(8,128)(2,1)S(1)} all-to-all(bf16[16,128,128]{2,1,0:T(8,128)(2,1)S(1)} %broadcast_in_dim.60), channel_id=1, replica_groups={{0,2,4,6,8,10,12,14,16,18,20,22,24,26,28,30},{1,3,5,7,9,11,13,15,17,19,..., dimensions={0} | all-to-all | bytes 1048576 | tf_op jit(solution)/shard_map/all_to_all | solution.py:284
  202.0 3.4 %collective-permute-start.9 = (bf16[16,128,128]{2,1,0:T(8,128)(2,1)S(1)}, bf16[16,128,128]{2,1,0:T(8,128)(2,1)S(1)}, u32[]{:S(2)}, u32[]{:S(2)}) collective-permute-start(bf16[16,128,128]{2,1,0:T(8,128)(2,1)S(1)} %all_to_all.56.mine_ref), channel_id=1, source_target_pairs={{0,1},{1,0},{2,3},{3,2},{4,5},{5,4},{6,7},{7,6},{8,9},{9,8},{10,11... | collective-permute-start | bytes 1572872 | tf_op jit(solution)/shard_map/ppermute | solution.py:286
  207.0 2.9 %wide.8 = bf16[16,128,256]{2,1,0:T(8,128)(2,1)S(1)} custom-call(s32[1]{0:T(128)} %bitcast.1.core_ref, bf16[16,128,128]{2,1,0:T(8,128)(2,1)S(1)} %all_to_all.56.mine_ref, bf16[16,128,128]{2,1,0:T(8,128)(2,1)S(1)} %collective-permute-done.9.other_ref, f32[64,128]{1,0:T(8,128)S(1)} %bitcast.46, bf16[4128,1792]{1,0:T(8,128)(2,1)S(1)} %pack_wide.1.weight_ref, ...), custom_call_target="tpu_custom_call" | custom-call | flops 1879048192 | bytes 2097152 | tf_op jit(solution)/shard_map/wide/pallas_call | solution.py:244
  209.9 19.0 %all_to_all.57.mine_ref = bf16[16,128,256]{2,1,0:T(8,128)(2,1)S(1)} all-to-all(bf16[16,128,256]{2,1,0:T(8,128)(2,1)S(1)} %wide.8), channel_id=1, replica_groups={{0,2,4,6,8,10,12,14,16,18,20,22,24,26,28,30},{1,3,5,7,9,11,13,15,17,19,..., dimensions={0} | all-to-all | bytes 2097152 | tf_op jit(solution)/shard_map/all_to_all | solution.py:284
  230.9 2.3 collective-permute-done.10.other_ref
  234.7 5.8 %collective-permute-start.11 = (bf16[128,128]{1,0:T(8,128)(2,1)S(1)}, bf16[128,128]{1,0:T(8,128)(2,1)S(1)}, u32[]{:S(2)}, u32[]{:S(2)}) collective-permute-start(bf16[128,128]{1,0:T(8,128)(2,1)S(1)} %get-tuple-element.55), channel_id=1, source_target_pairs={{0,32},{32,64},{64,96},{1,33},{33,65},{65,97},{2,34},{34,66},{66,9... | collective-permute-start | bytes 98312 | tf_op jit(solution)/shard_map/ppermute | solution.py:332
  241.5 12.0 %all_to_all.58.mine_ref = bf16[16,128,128]{2,1,0:T(8,128)(2,1)S(1)} all-to-all(bf16[16,128,128]{2,1,0:T(8,128)(2,1)S(1)} %broadcast_in_dim.61), channel_id=1, replica_groups={{0,2,4,6,8,10,12,14,16,18,20,22,24,26,28,30},{1,3,5,7,9,11,13,15,17,19,..., dimensions={0} | all-to-all | bytes 1048576 | tf_op jit(solution)/shard_map/all_to_all | solution.py:284
  253.5 3.4 %collective-permute-start.12 = (bf16[16,128,128]{2,1,0:T(8,128)(2,1)S(1)}, bf16[16,128,128]{2,1,0:T(8,128)(2,1)S(1)}, u32[]{:S(2)}, u32[]{:S(2)}) collective-permute-start(bf16[16,128,128]{2,1,0:T(8,128)(2,1)S(1)} %all_to_all.58.mine_ref), channel_id=1, source_target_pairs={{0,1},{1,0},{2,3},{3,2},{4,5},{5,4},{6,7},{7,6},{8,9},{9,8},{10,11... | collective-permute-start | bytes 1572872 | tf_op jit(solution)/shard_map/ppermute | solution.py:286
  258.5 2.9 %wide.9 = bf16[16,128,256]{2,1,0:T(8,128)(2,1)S(1)} custom-call(s32[1]{0:T(128)} %bitcast.1.core_ref, bf16[16,128,128]{2,1,0:T(8,128)(2,1)S(1)} %all_to_all.58.mine_ref, bf16[16,128,128]{2,1,0:T(8,128)(2,1)S(1)} %collective-permute-done.12.other_ref, f32[64,128]{1,0:T(8,128)S(1)} %bitcast.47, bf16[4128,1792]{1,0:T(8,128)(2,1)S(1)} %pack_wide.1.weight_ref, ...), custom_call_target="tpu_custom_call" | custom-call | flops 1879048192 | bytes 2097152 | tf_op jit(solution)/shard_map/wide/pallas_call | solution.py:244
  261.4 19.0 %all_to_all.59.mine_ref = bf16[16,128,256]{2,1,0:T(8,128)(2,1)S(1)} all-to-all(bf16[16,128,256]{2,1,0:T(8,128)(2,1)S(1)} %wide.9), channel_id=1, replica_groups={{0,2,4,6,8,10,12,14,16,18,20,22,24,26,28,30},{1,3,5,7,9,11,13,15,17,19,..., dimensions={0} | all-to-all | bytes 2097152 | tf_op jit(solution)/shard_map/all_to_all | solution.py:284
  282.5 2.3 collective-permute-done.13.other_ref
  (55 shorter events, 33.2 us)
Async XLA Ops:
  0.0 3.2 %copy-start = (bf16[128,256]{1,0:T(8,128)(2,1)S(1)}, bf16[128,256]{1,0:T(8,128)(2,1)}, u32[]{:S(2)}) copy-start(bf16[128,256]{1,0:T(8,128)(2,1)} %param.7) | copy-start | bytes 196612
  3.7 0.7 copy-start.1
  48.4 3.6 %collective-permute-start = (bf16[16,128,128]{2,1,0:T(8,128)(2,1)S(1)}, bf16[16,128,128]{2,1,0:T(8,128)(2,1)S(1)}, u32[]{:S(2)}, u32[]{:S(2)}) collective-permute-start(bf16[16,128,128]{2,1,0:T(8,128)(2,1)S(1)} %all_to_all.50.mine_ref), channel_id=1, source_target_pairs={{0,1},{1,0},{2,3},{3,2},{4,5},{5,4},{6,7},{7,6},{8,9},{9,8},{10,11... | collective-permute-start | bytes 1572872 | tf_op jit(solution)/shard_map/ppermute | solution.py:286
  73.9 4.4 %collective-permute-start.1 = (bf16[16,128,256]{2,1,0:T(8,128)(2,1)S(1)}, bf16[16,128,256]{2,1,0:T(8,128)(2,1)S(1)}, u32[]{:S(2)}, u32[]{:S(2)}) collective-permute-start(bf16[16,128,256]{2,1,0:T(8,128)(2,1)S(1)} %all_to_all.51.mine_ref), channel_id=1, source_target_pairs={{0,1},{1,0},{2,3},{3,2},{4,5},{5,4},{6,7},{7,6},{8,9},{9,8},{10,11... | collective-permute-start | bytes 3145736 | tf_op jit(solution)/shard_map/ppermute | solution.py:286
  79.7 7.1 %collective-permute-start.2 = (bf16[128,128]{1,0:T(8,128)(2,1)S(1)}, bf16[128,128]{1,0:T(8,128)(2,1)S(1)}, u32[]{:S(2)}, u32[]{:S(2)}) collective-permute-start(bf16[128,128]{1,0:T(8,128)(2,1)S(1)} %get-tuple-element.46), channel_id=1, source_target_pairs={{0,32},{32,64},{64,96},{1,33},{33,65},{65,97},{2,34},{34,66},{66,9... | collective-permute-start | bytes 98312 | tf_op jit(solution)/shard_map/ppermute | solution.py:332
  98.9 5.0 %collective-permute-start.3 = (bf16[16,128,128]{2,1,0:T(8,128)(2,1)S(1)}, bf16[16,128,128]{2,1,0:T(8,128)(2,1)S(1)}, u32[]{:S(2)}, u32[]{:S(2)}) collective-permute-start(bf16[16,128,128]{2,1,0:T(8,128)(2,1)S(1)} %all_to_all.52.mine_ref), channel_id=1, source_target_pairs={{0,1},{1,0},{2,3},{3,2},{4,5},{5,4},{6,7},{7,6},{8,9},{9,8},{10,11... | collective-permute-start | bytes 1572872 | tf_op jit(solution)/shard_map/ppermute | solution.py:286
  125.8 4.4 %collective-permute-start.4 = (bf16[16,128,256]{2,1,0:T(8,128)(2,1)S(1)}, bf16[16,128,256]{2,1,0:T(8,128)(2,1)S(1)}, u32[]{:S(2)}, u32[]{:S(2)}) collective-permute-start(bf16[16,128,256]{2,1,0:T(8,128)(2,1)S(1)} %all_to_all.53.mine_ref), channel_id=1, source_target_pairs={{0,1},{1,0},{2,3},{3,2},{4,5},{5,4},{6,7},{7,6},{8,9},{9,8},{10,11... | collective-permute-start | bytes 3145736 | tf_op jit(solution)/shard_map/ppermute | solution.py:286
  131.6 6.8 %collective-permute-start.5 = (bf16[128,128]{1,0:T(8,128)(2,1)S(1)}, bf16[128,128]{1,0:T(8,128)(2,1)S(1)}, u32[]{:S(2)}, u32[]{:S(2)}) collective-permute-start(bf16[128,128]{1,0:T(8,128)(2,1)S(1)} %get-tuple-element.47), channel_id=1, source_target_pairs={{0,32},{32,64},{64,96},{1,33},{33,65},{65,97},{2,34},{34,66},{66,9... | collective-permute-start | bytes 98312 | tf_op jit(solution)/shard_map/ppermute | solution.py:332
  150.4 5.0 %collective-permute-start.6 = (bf16[16,128,128]{2,1,0:T(8,128)(2,1)S(1)}, bf16[16,128,128]{2,1,0:T(8,128)(2,1)S(1)}, u32[]{:S(2)}, u32[]{:S(2)}) collective-permute-start(bf16[16,128,128]{2,1,0:T(8,128)(2,1)S(1)} %all_to_all.54.mine_ref), channel_id=1, source_target_pairs={{0,1},{1,0},{2,3},{3,2},{4,5},{5,4},{6,7},{7,6},{8,9},{9,8},{10,11... | collective-permute-start | bytes 1572872 | tf_op jit(solution)/shard_map/ppermute | solution.py:286
  177.3 4.4 %collective-permute-start.7 = (bf16[16,128,256]{2,1,0:T(8,128)(2,1)S(1)}, bf16[16,128,256]{2,1,0:T(8,128)(2,1)S(1)}, u32[]{:S(2)}, u32[]{:S(2)}) collective-permute-start(bf16[16,128,256]{2,1,0:T(8,128)(2,1)S(1)} %all_to_all.55.mine_ref), channel_id=1, source_target_pairs={{0,1},{1,0},{2,3},{3,2},{4,5},{5,4},{6,7},{7,6},{8,9},{9,8},{10,11... | collective-permute-start | bytes 3145736 | tf_op jit(solution)/shard_map/ppermute | solution.py:286
  183.1 6.8 %collective-permute-start.8 = (bf16[128,128]{1,0:T(8,128)(2,1)S(1)}, bf16[128,128]{1,0:T(8,128)(2,1)S(1)}, u32[]{:S(2)}, u32[]{:S(2)}) collective-permute-start(bf16[128,128]{1,0:T(8,128)(2,1)S(1)} %get-tuple-element.48), channel_id=1, source_target_pairs={{0,32},{32,64},{64,96},{1,33},{33,65},{65,97},{2,34},{34,66},{66,9... | collective-permute-start | bytes 98312 | tf_op jit(solution)/shard_map/ppermute | solution.py:332
  202.0 5.0 %collective-permute-start.9 = (bf16[16,128,128]{2,1,0:T(8,128)(2,1)S(1)}, bf16[16,128,128]{2,1,0:T(8,128)(2,1)S(1)}, u32[]{:S(2)}, u32[]{:S(2)}) collective-permute-start(bf16[16,128,128]{2,1,0:T(8,128)(2,1)S(1)} %all_to_all.56.mine_ref), channel_id=1, source_target_pairs={{0,1},{1,0},{2,3},{3,2},{4,5},{5,4},{6,7},{7,6},{8,9},{9,8},{10,11... | collective-permute-start | bytes 1572872 | tf_op jit(solution)/shard_map/ppermute | solution.py:286
  228.9 4.4 %collective-permute-start.10 = (bf16[16,128,256]{2,1,0:T(8,128)(2,1)S(1)}, bf16[16,128,256]{2,1,0:T(8,128)(2,1)S(1)}, u32[]{:S(2)}, u32[]{:S(2)}) collective-permute-start(bf16[16,128,256]{2,1,0:T(8,128)(2,1)S(1)} %all_to_all.57.mine_ref), channel_id=1, source_target_pairs={{0,1},{1,0},{2,3},{3,2},{4,5},{5,4},{6,7},{7,6},{8,9},{9,8},{10,11... | collective-permute-start | bytes 3145736 | tf_op jit(solution)/shard_map/ppermute | solution.py:286
  234.7 6.8 %collective-permute-start.11 = (bf16[128,128]{1,0:T(8,128)(2,1)S(1)}, bf16[128,128]{1,0:T(8,128)(2,1)S(1)}, u32[]{:S(2)}, u32[]{:S(2)}) collective-permute-start(bf16[128,128]{1,0:T(8,128)(2,1)S(1)} %get-tuple-element.55), channel_id=1, source_target_pairs={{0,32},{32,64},{64,96},{1,33},{33,65},{65,97},{2,34},{34,66},{66,9... | collective-permute-start | bytes 98312 | tf_op jit(solution)/shard_map/ppermute | solution.py:332
  253.5 5.0 %collective-permute-start.12 = (bf16[16,128,128]{2,1,0:T(8,128)(2,1)S(1)}, bf16[16,128,128]{2,1,0:T(8,128)(2,1)S(1)}, u32[]{:S(2)}, u32[]{:S(2)}) collective-permute-start(bf16[16,128,128]{2,1,0:T(8,128)(2,1)S(1)} %all_to_all.58.mine_ref), channel_id=1, source_target_pairs={{0,1},{1,0},{2,3},{3,2},{4,5},{5,4},{6,7},{7,6},{8,9},{9,8},{10,11... | collective-permute-start | bytes 1572872 | tf_op jit(solution)/shard_map/ppermute | solution.py:286
  280.4 4.4 %collective-permute-start.13 = (bf16[16,128,256]{2,1,0:T(8,128)(2,1)S(1)}, bf16[16,128,256]{2,1,0:T(8,128)(2,1)S(1)}, u32[]{:S(2)}, u32[]{:S(2)}) collective-permute-start(bf16[16,128,256]{2,1,0:T(8,128)(2,1)S(1)} %all_to_all.59.mine_ref), channel_id=1, source_target_pairs={{0,1},{1,0},{2,3},{3,2},{4,5},{5,4},{6,7},{7,6},{8,9},{9,8},{10,11... | collective-permute-start | bytes 3145736 | tf_op jit(solution)/shard_map/ppermute | solution.py:286

commit v2 on v1

--- a/solution.py
+++ b/solution.py
@@ -19,12 +19,10 @@
 MIB = 1 << 20
 
 
-def pack_target(kept, per_device, stride, rows):
-    device = kept // per_device
+def targets(index, per_device, stride, rows):
+    device = index // per_device
     block = (device % 2) * CHIPS + device // 2
-    return pl.multiple_of(
-        jnp.where(kept >= 0, block * stride + (kept % per_device) * 32, rows - 32), 32
-    )
+    return jnp.where(index >= 0, block * stride + (index % per_device) * 32, rows - 32)
 
 
 def clear(target):
@@ -37,24 +35,24 @@
     lax.fori_loop(0, rows // 32, one, 0)
 
 
-def wide_pack_kernel(index_ref, gate_hbm, up_hbm, target, buf, spread, sems):
-    tiles, slots = index_ref.shape
-    copies = []
+def wide_pack_kernel(goal_ref, gate_hbm, up_hbm, target, buf, spread, sems):
+    tiles, slots = goal_ref.shape
     for which, source in enumerate((gate_hbm, up_hbm)):
         for tile in range(tiles):
             at = which * tiles + tile
-            copies.append(pltpu.make_async_copy(source.at[tile], buf.at[at], sems.at[at]))
-    for copy in copies:
-        copy.start()
+            pltpu.make_async_copy(source.at[tile], buf.at[at], sems.at[at]).start()
     clear(target)
 
     def place(chunk, count, first, half, tile, column):
-        for part in range(32):
-            spread[half, part * 16 : part * 16 + count, :] = chunk[:, part * 128 : (part + 1) * 128]
+        for group in range(0, count, 8):
+            for part in range(32):
+                spread[half, group * 32 + part * 8 : group * 32 + part * 8 + 8, :] = chunk[
+                    group : group + 8, part * 128 : (part + 1) * 128
+                ]
         for row in range(count):
-            at = pack_target(index_ref[tile, first + row], 4, 128, target.shape[0])
-            piece = spread[half, pl.ds(row, 32, stride=16), :]
-            target[pl.ds(at, 32), pl.ds(column, 128)] = piece.astype(target.dtype)
+            goal = pl.multiple_of(goal_ref[tile, first + row], 32)
+            piece = spread[half, pl.ds(row // 8 * 256 + row % 8, 32, stride=8), :]
+            target[pl.ds(goal, 32), pl.ds(column, 128)] = piece.astype(target.dtype)
 
     def one(at, _):
         pltpu.make_async_copy(gate_hbm.at[0], buf.at[at], sems.at[at]).wait()
@@ -84,37 +82,34 @@
     lax.fori_loop(0, 2 * tiles, one, 0)
 
 
-def down_pack_kernel(index_ref, source, target, buf, spread, sems):
-    tiles, slots = index_ref.shape
+def down_pack_kernel(goal_ref, source, target, buf, spread, sems):
+    tiles, slots = goal_ref.shape
     parts = 7
     size = slots // parts
-    copies = [
+    for part in range(parts):
         pltpu.make_async_copy(
             source.at[pl.ds(part * size, size)], buf.at[pl.ds(part * size, size)], sems.at[part]
-        )
-        for part in range(parts)
-    ]
-    for copy in copies:
-        copy.start()
+        ).start()
     clear(target)
+
     def one(part, _):
         pltpu.make_async_copy(
             source.at[pl.ds(0, size)], buf.at[pl.ds(part * size, size)], sems.at[part]
         ).wait()
 
         def step(at, _):
-            for half in range(2):
-                slot = part * size + at * 6 + half * 3
-                for inner in range(3):
+            for half in range(3):
+                slot = part * size + at * 6 + half * 2
+                for inner in range(2):
                     chunk = buf[slot + inner].astype(jnp.float32)
                     for lane in range(32):
-                        spread[half, lane * 16 + inner * 4 : lane * 16 + inner * 4 + 4, :] = chunk[
+                        spread[half, lane * 8 + inner * 4 : lane * 8 + inner * 4 + 4, :] = chunk[
                             :, lane * 128 : (lane + 1) * 128
                         ]
-                for inner in range(3):
+                for inner in range(2):
                     for tile in range(tiles):
-                        goal = pack_target(index_ref[tile, slot + inner], 7, 256, target.shape[0])
-                        piece = spread[half, pl.ds(inner * 4 + tile, 32, stride=16), :]
+                        goal = pl.multiple_of(goal_ref[tile, slot + inner], 32)
+                        piece = spread[half, pl.ds(inner * 4 + tile, 32, stride=8), :]
                         target[pl.ds(goal, 32), tile * 128 : (tile + 1) * 128] = piece.astype(target.dtype)
             return 0
 
@@ -124,7 +119,7 @@
     lax.fori_loop(0, parts, one, 0)
 
 
-def pack(kernel, index, sources, buf, copies, shape, name):
+def pack(kernel, goals, sources, buf, spread, copies, shape, name):
     sources = [pltpu.with_memory_space_constraint(source, pltpu.HBM) for source in sources]
     return pl.pallas_call(
         kernel,
@@ -134,31 +129,43 @@
         out_specs=pl.BlockSpec(memory_space=pltpu.VMEM),
         scratch_shapes=[
             pltpu.VMEM(buf, jnp.bfloat16),
-            pltpu.VMEM((2, 32 * 16, 128), jnp.float32),
+            pltpu.VMEM(spread + (128,), jnp.float32),
             pltpu.SemaphoreType.DMA((copies,)),
         ],
         compiler_params=pltpu.CompilerParams(vmem_limit_bytes=12 * MIB),
         cost_estimate=pl.CostEstimate(flops=0, bytes_accessed=40 * MIB, transcendentals=0),
         name=name,
-    )(index, *sources)
-
-
-def densify_wide(index, gate_blocks, up_blocks):
-    tiles, slots = index.shape
+    )(goals, *sources)
+
+
+def densify_wide(goals, gate_blocks, up_blocks):
+    tiles, slots = goals.shape
     buf = (2 * tiles, slots, BS * BS)
     shape = (GU_ROWS + 32, GU_COLS)
-    return pack(wide_pack_kernel, index, (gate_blocks, up_blocks), buf, 2 * tiles, shape, "pack_wide")
-
-
-def densify_down(index, blocks):
-    tiles, slots = index.shape
+    sources = (gate_blocks, up_blocks)
+    return pack(wide_pack_kernel, goals, sources, buf, (2, 512), 2 * tiles, shape, "pack_wide")
+
+
+def densify_down(goals, blocks):
+    tiles, slots = goals.shape
     shape = (DN_ROWS + 32, DN_COLS)
     blocks = jnp.transpose(blocks, (1, 0, 2))
-    return pack(down_pack_kernel, index, (blocks,), (slots, tiles, BS * BS), 7, shape, "pack_down")
+    return pack(down_pack_kernel, goals, (blocks,), (slots, tiles, BS * BS), (3, 256), 7, shape, "pack_down")
+
+
+def in_goals(index):
+    return targets(index, 4, 128, GU_ROWS + 32)
+
+
+def out_goals(index):
+    return targets(index, 7, 256, DN_ROWS + 32)
 
 
 def densify(in_index, gate_blocks, up_blocks, out_index, down_blocks):
-    return densify_wide(in_index, gate_blocks, up_blocks), densify_down(out_index, down_blocks)
+    return (
+        densify_wide(in_goals(in_index), gate_blocks, up_blocks),
+        densify_down(out_goals(out_index), down_blocks),
+    )
 
 
 def fold(even, odd, at):
@@ -279,11 +286,13 @@
     return x_order, h_order
 
 
-def gathered(value):
+def exchanged(value):
     same_core = [[2 * chip + core for chip in range(CHIPS)] for core in range(2)]
-    mine = lax.all_to_all(value, "tensor", 0, 0, axis_index_groups=same_core)
-    swap = [(i, i ^ 1) for i in range(2 * CHIPS)]
-    return mine, lax.ppermute(mine, "tensor", swap)
+    return lax.all_to_all(value, "tensor", 0, 0, axis_index_groups=same_core)
+
+
+def swapped(value):
+    return lax.ppermute(value, "tensor", [(i, i ^ 1) for i in range(2 * CHIPS)])
 
 
 def local(x_in, norm_gain, in_index, gate_blocks, up_blocks, out_index, down_blocks):
@@ -296,7 +305,7 @@
     x_order, h_order = orders()
     x_back = x_order.T
     gain = jnp.dot(
-        norm_gain[0].reshape(2 * CHIPS, 256), x_order.astype(jnp.float32), precision=lax.Precision.HIGHEST
+        norm_gain.reshape(2 * CHIPS, 256), x_order.astype(jnp.float32), precision=lax.Precision.HIGHEST
     )
     gain = gain.reshape(CHIPS, 2, 2, 128).transpose(1, 0, 2, 3).reshape(4 * CHIPS, 128)
     x_ordered = jnp.dot(x_in, x_order, preferred_element_type=jnp.float32).astype(jnp.bfloat16)
@@ -305,13 +314,10 @@
         part = x_ordered[group * ROWS : (group + 1) * ROWS]
         firsts.append(jnp.concatenate([part[:, :128], part[:, 128:]], axis=0))
     here = [jnp.broadcast_to(segment_at == segment, (8, 128)).astype(jnp.bfloat16) for segment in range(segment_count)]
-    in_index, out_index = in_index[0], out_index[0]
-    in_index, out_index, core, x_order, x_back, h_order, gain, firsts, here = lax.optimization_barrier(
-        (in_index, out_index, core, x_order, x_back, h_order, gain, firsts, here)
-    )
-    wide = densify_wide(in_index, gate_blocks[0], up_blocks[0])
-    down = densify_down(out_index, down_blocks[0])
-    firsts, wide, down = lax.optimization_barrier((firsts, wide, down))
+    to_wide, to_down = in_goals(in_index[0]), out_goals(out_index[0])
+    to_wide, to_down, core, x_order, x_back, h_order, gain, firsts, here = lax.optimization_barrier(
+        (to_wide, to_down, core, x_order, x_back, h_order, gain, firsts, here)
+    )
 
     def is_here(segment, shape):
         return jnp.tile(here[segment], (shape[0] // 8, shape[1] // 128)) > 0
@@ -323,9 +329,17 @@
         taken = firsts[min(tick, group_count - 1)]
         if carried is not None:
             taken = jnp.where(is_here(0, taken.shape), taken, carried)
-        mine, other = gathered(jnp.broadcast_to(taken[None], (CHIPS, 2 * ROWS, 128)))
+        mine = exchanged(jnp.broadcast_to(taken[None], (CHIPS, 2 * ROWS, 128)))
+        if tick == 0:
+            mine, to_wide = lax.optimization_barrier((mine, to_wide))
+            wide = densify_wide(to_wide, gate_blocks[0], up_blocks[0])
+        other = swapped(mine)
         hidden = call_wide(core, mine, other, gain, wide, h_order)
-        mine, other = gathered(hidden)
+        mine = exchanged(hidden)
+        if tick == 0:
+            mine, to_down = lax.optimization_barrier((mine, to_down))
+            down = densify_down(to_down, down_blocks[0])
+        other = swapped(mine)
         produced, ordered = call_down(core, mine, other, down, taken, x_order, x_back)
         made.append(produced)
         if tick + 1 < tick_count:

time: 288 us -> 269 us (0.934)
  Pallas kernels: 49.4 us -> 34.3 us
  waiting for transfers between devices: 23.1 us -> 19.3 us
    pallas_call x2, Pallas kernels: 26.9 us -> 11.8 us  [pack(): pl.pallas_call(kernel, out_shape=pltpu.VMEM(shape, jnp.bfloat16), in_spec...]
    ppermute x10, waiting for transfers between devices: 19.1 us -> 15.3 us  [swapped(): return lax.ppermute(value, 'tensor', [(i, i ^ 1) for i in range(2 * CHIPS)])]
  transfers between devices with their start and end apart: 14 -> 14, of which waited for: 14 -> 12; matrix products, arithmetic and copies ran while one was open for 0% -> 0% of each run, Pallas kernels for 0% -> 4%
where the time goes in v2:
time: 269 us
  blocking collectives  161 us (60%)
  starting transfers between devices  48.6 us (18%)
  Pallas kernels  34.3 us (13%)
  waiting for transfers between devices  19.3 us (7%)
  other arithmetic  3.88 us (1%)
    all_to_all x10, blocking collectives, exchanged(): return lax.all_to_all(value, 'tensor', 0, 0, axis_index_groups=same_core)  161 us
    ppermute x10, starting transfers between devices, swapped(): return lax.ppermute(value, 'tensor', [(i, i ^ 1) for i in range(2 * CHIPS)])  25.2 us
    ppermute x4, starting transfers between devices, local(): carried = lax.ppermute(ordered, 'segment', hops)  23.4 us
    ppermute x10, waiting for transfers between devices, swapped(): return lax.ppermute(value, 'tensor', [(i, i ^ 1) for i in range(2 * CHIPS)])  15.3 us
    pallas_call x5, Pallas kernels, call_wide(): pl.pallas_call(wide_kernel, out_shape=jax.ShapeDtypeStruct((CHIPS, 2 * RO...  14.6 us
    pallas_call x2, Pallas kernels, pack(): pl.pallas_call(kernel, out_shape=pltpu.VMEM(shape, jnp.bfloat16), in_spec...  11.8 us
    pallas_call x5, Pallas kernels, call_down(): pl.pallas_call(down_kernel, out_shape=(jax.ShapeDtypeStruct((ROWS, 256),...  7.81 us
  transfers between devices with their start and end apart: 14, of which 12 were waited for; matrix products, arithmetic and copies ran while one was open for 0% of the time, Pallas kernels for 4%

profile of v2, /device:TPU:65, one launch (start us, length us, event | category | flops | bytes accessed | tf_op | source)
XLA Modules:
  0.0 268.7 jit_solution(10438939328851013476)
XLA Ops:
  4.5 16.9 %all_to_all.50.mine_ref = bf16[16,128,128]{2,1,0:T(8,128)(2,1)S(1)} all-to-all(bf16[16,128,128]{2,1,0:T(8,128)(2,1)S(1)} %broadcast_in_dim.67), channel_id=1, replica_groups={{0,2,4,6,8,10,12,14,16,18,20,22,24,26,28,30},{1,3,5,7,9,11,13,15,17,19,..., dimensions={0} | all-to-all | bytes 1048576 | tf_op jit(solution)/shard_map/all_to_all | solution.py:291
  21.5 2.1 collective-permute-start
  23.5 6.9 %pack_wide.1.weight_ref = bf16[4128,1792]{1,0:T(8,128)(2,1)S(1)} custom-call(s32[7,72]{1,0:T(8,128)S(1)} %fusion.18.goal_ref, bf16[7,72,4096]{2,1,0:T(8,128)(2,1)} %bitcast.88, bf16[7,72,4096]{2,1,0:T(8,128)(2,1)} %bitcast.89), custom_call_target="tpu_custom_call" | custom-call | bytes 41943040 | tf_op jit(solution)/shard_map/pack_wide/pallas_call | solution.py:124
  30.5 2.9 %wide.5 = bf16[16,128,256]{2,1,0:T(8,128)(2,1)S(1)} custom-call(s32[1]{0:T(128)} %bitcast.4.core_ref, bf16[16,128,128]{2,1,0:T(8,128)(2,1)S(1)} %all_to_all.50.mine_ref, bf16[16,128,128]{2,1,0:T(8,128)(2,1)S(1)} %collective-permute-done.other_ref, f32[64,128]{1,0:T(8,128)S(1)} %bitcast.82, bf16[4128,1792]{1,0:T(8,128)(2,1)S(1)} %pack_wide.1.weight_ref, ...), custom_call_target="tpu_custom_call" | custom-call | flops 1879048192 | bytes 2097152 | tf_op jit(solution)/shard_map/wide/pallas_call | solution.py:251
  33.4 18.8 %all_to_all.51.mine_ref = bf16[16,128,256]{2,1,0:T(8,128)(2,1)S(1)} all-to-all(bf16[16,128,256]{2,1,0:T(8,128)(2,1)S(1)} %wide.5), channel_id=1, replica_groups={{0,2,4,6,8,10,12,14,16,18,20,22,24,26,28,30},{1,3,5,7,9,11,13,15,17,19,..., dimensions={0} | all-to-all | bytes 2097152 | tf_op jit(solution)/shard_map/all_to_all | solution.py:291
  52.2 2.3 collective-permute-start.1
  54.5 4.9 %pack_down.1.weight_ref = bf16[8224,512]{1,0:T(8,128)(2,1)S(1)} custom-call(s32[4,126]{1,0:T(4,128)S(1)} %fusion.31.goal_ref, bf16[126,4,4096]{2,1,0:T(4,128)(2,1)} %bitcast.87), custom_call_target="tpu_custom_call" | custom-call | bytes 41943040 | tf_op jit(solution)/shard_map/pack_down/pallas_call | solution.py:124
  60.9 6.1 %collective-permute-start.2 = (bf16[128,128]{1,0:T(8,128)(2,1)S(1)}, bf16[128,128]{1,0:T(8,128)(2,1)S(1)}, u32[]{:S(2)}, u32[]{:S(2)}) collective-permute-start(bf16[128,128]{1,0:T(8,128)(2,1)S(1)} %get-tuple-element.46), channel_id=1, source_target_pairs={{0,32},{32,64},{64,96},{1,33},{33,65},{65,97},{2,34},{34,66},{66,9... | collective-permute-start | bytes 98312 | tf_op jit(solution)/shard_map/ppermute | solution.py:346
  68.1 13.3 %all_to_all.52.mine_ref = bf16[16,128,128]{2,1,0:T(8,128)(2,1)S(1)} all-to-all(bf16[16,128,128]{2,1,0:T(8,128)(2,1)S(1)} %broadcast_in_dim.68), channel_id=1, replica_groups={{0,2,4,6,8,10,12,14,16,18,20,22,24,26,28,30},{1,3,5,7,9,11,13,15,17,19,..., dimensions={0} | all-to-all | bytes 1048576 | tf_op jit(solution)/shard_map/all_to_all | solution.py:291
  81.4 2.2 collective-permute-start.3
  85.1 2.9 %wide.6 = bf16[16,128,256]{2,1,0:T(8,128)(2,1)S(1)} custom-call(s32[1]{0:T(128)} %bitcast.4.core_ref, bf16[16,128,128]{2,1,0:T(8,128)(2,1)S(1)} %all_to_all.52.mine_ref, bf16[16,128,128]{2,1,0:T(8,128)(2,1)S(1)} %collective-permute-done.3.other_ref, f32[64,128]{1,0:T(8,128)S(1)} %bitcast.83, bf16[4128,1792]{1,0:T(8,128)(2,1)S(1)} %pack_wide.1.weight_ref, ...), custom_call_target="tpu_custom_call" | custom-call | flops 1879048192 | bytes 2097152 | tf_op jit(solution)/shard_map/wide/pallas_call | solution.py:251
  88.0 19.0 %all_to_all.53.mine_ref = bf16[16,128,256]{2,1,0:T(8,128)(2,1)S(1)} all-to-all(bf16[16,128,256]{2,1,0:T(8,128)(2,1)S(1)} %wide.6), channel_id=1, replica_groups={{0,2,4,6,8,10,12,14,16,18,20,22,24,26,28,30},{1,3,5,7,9,11,13,15,17,19,..., dimensions={0} | all-to-all | bytes 2097152 | tf_op jit(solution)/shard_map/all_to_all | solution.py:291
  107.0 2.1 collective-permute-start.4
  109.1 2.3 collective-permute-done.4.other_ref
  112.9 5.8 %collective-permute-start.5 = (bf16[128,128]{1,0:T(8,128)(2,1)S(1)}, bf16[128,128]{1,0:T(8,128)(2,1)S(1)}, u32[]{:S(2)}, u32[]{:S(2)}) collective-permute-start(bf16[128,128]{1,0:T(8,128)(2,1)S(1)} %get-tuple-element.47), channel_id=1, source_target_pairs={{0,32},{32,64},{64,96},{1,33},{33,65},{65,97},{2,34},{34,66},{66,9... | collective-permute-start | bytes 98312 | tf_op jit(solution)/shard_map/ppermute | solution.py:346
  119.7 12.0 %all_to_all.54.mine_ref = bf16[16,128,128]{2,1,0:T(8,128)(2,1)S(1)} all-to-all(bf16[16,128,128]{2,1,0:T(8,128)(2,1)S(1)} %broadcast_in_dim.69), channel_id=1, replica_groups={{0,2,4,6,8,10,12,14,16,18,20,22,24,26,28,30},{1,3,5,7,9,11,13,15,17,19,..., dimensions={0} | all-to-all | bytes 1048576 | tf_op jit(solution)/shard_map/all_to_all | solution.py:291
  131.7 3.5 %collective-permute-start.6 = (bf16[16,128,128]{2,1,0:T(8,128)(2,1)S(1)}, bf16[16,128,128]{2,1,0:T(8,128)(2,1)S(1)}, u32[]{:S(2)}, u32[]{:S(2)}) collective-permute-start(bf16[16,128,128]{2,1,0:T(8,128)(2,1)S(1)} %all_to_all.54.mine_ref), channel_id=1, source_target_pairs={{0,1},{1,0},{2,3},{3,2},{4,5},{5,4},{6,7},{7,6},{8,9},{9,8},{10,11... | collective-permute-start | bytes 1572872 | tf_op jit(solution)/shard_map/ppermute | solution.py:295
  136.7 2.9 %wide.7 = bf16[16,128,256]{2,1,0:T(8,128)(2,1)S(1)} custom-call(s32[1]{0:T(128)} %bitcast.4.core_ref, bf16[16,128,128]{2,1,0:T(8,128)(2,1)S(1)} %all_to_all.54.mine_ref, bf16[16,128,128]{2,1,0:T(8,128)(2,1)S(1)} %collective-permute-done.6.other_ref, f32[64,128]{1,0:T(8,128)S(1)} %bitcast.84, bf16[4128,1792]{1,0:T(8,128)(2,1)S(1)} %pack_wide.1.weight_ref, ...), custom_call_target="tpu_custom_call" | custom-call | flops 1879048192 | bytes 2097152 | tf_op jit(solution)/shard_map/wide/pallas_call | solution.py:251
  139.6 19.0 %all_to_all.55.mine_ref = bf16[16,128,256]{2,1,0:T(8,128)(2,1)S(1)} all-to-all(bf16[16,128,256]{2,1,0:T(8,128)(2,1)S(1)} %wide.7), channel_id=1, replica_groups={{0,2,4,6,8,10,12,14,16,18,20,22,24,26,28,30},{1,3,5,7,9,11,13,15,17,19,..., dimensions={0} | all-to-all | bytes 2097152 | tf_op jit(solution)/shard_map/all_to_all | solution.py:291
  160.7 2.3 collective-permute-done.7.other_ref
  164.4 5.8 %collective-permute-start.8 = (bf16[128,128]{1,0:T(8,128)(2,1)S(1)}, bf16[128,128]{1,0:T(8,128)(2,1)S(1)}, u32[]{:S(2)}, u32[]{:S(2)}) collective-permute-start(bf16[128,128]{1,0:T(8,128)(2,1)S(1)} %get-tuple-element.48), channel_id=1, source_target_pairs={{0,32},{32,64},{64,96},{1,33},{33,65},{65,97},{2,34},{34,66},{66,9... | collective-permute-start | bytes 98312 | tf_op jit(solution)/shard_map/ppermute | solution.py:346
  171.3 12.0 %all_to_all.56.mine_ref = bf16[16,128,128]{2,1,0:T(8,128)(2,1)S(1)} all-to-all(bf16[16,128,128]{2,1,0:T(8,128)(2,1)S(1)} %broadcast_in_dim.70), channel_id=1, replica_groups={{0,2,4,6,8,10,12,14,16,18,20,22,24,26,28,30},{1,3,5,7,9,11,13,15,17,19,..., dimensions={0} | all-to-all | bytes 1048576 | tf_op jit(solution)/shard_map/all_to_all | solution.py:291
  183.2 3.4 %collective-permute-start.9 = (bf16[16,128,128]{2,1,0:T(8,128)(2,1)S(1)}, bf16[16,128,128]{2,1,0:T(8,128)(2,1)S(1)}, u32[]{:S(2)}, u32[]{:S(2)}) collective-permute-start(bf16[16,128,128]{2,1,0:T(8,128)(2,1)S(1)} %all_to_all.56.mine_ref), channel_id=1, source_target_pairs={{0,1},{1,0},{2,3},{3,2},{4,5},{5,4},{6,7},{7,6},{8,9},{9,8},{10,11... | collective-permute-start | bytes 1572872 | tf_op jit(solution)/shard_map/ppermute | solution.py:295
  188.2 2.9 %wide.8 = bf16[16,128,256]{2,1,0:T(8,128)(2,1)S(1)} custom-call(s32[1]{0:T(128)} %bitcast.4.core_ref, bf16[16,128,128]{2,1,0:T(8,128)(2,1)S(1)} %all_to_all.56.mine_ref, bf16[16,128,128]{2,1,0:T(8,128)(2,1)S(1)} %collective-permute-done.9.other_ref, f32[64,128]{1,0:T(8,128)S(1)} %bitcast.85, bf16[4128,1792]{1,0:T(8,128)(2,1)S(1)} %pack_wide.1.weight_ref, ...), custom_call_target="tpu_custom_call" | custom-call | flops 1879048192 | bytes 2097152 | tf_op jit(solution)/shard_map/wide/pallas_call | solution.py:251
  191.2 19.0 %all_to_all.57.mine_ref = bf16[16,128,256]{2,1,0:T(8,128)(2,1)S(1)} all-to-all(bf16[16,128,256]{2,1,0:T(8,128)(2,1)S(1)} %wide.8), channel_id=1, replica_groups={{0,2,4,6,8,10,12,14,16,18,20,22,24,26,28,30},{1,3,5,7,9,11,13,15,17,19,..., dimensions={0} | all-to-all | bytes 2097152 | tf_op jit(solution)/shard_map/all_to_all | solution.py:291
  212.2 2.3 collective-permute-done.10.other_ref
  215.9 5.8 %collective-permute-start.11 = (bf16[128,128]{1,0:T(8,128)(2,1)S(1)}, bf16[128,128]{1,0:T(8,128)(2,1)S(1)}, u32[]{:S(2)}, u32[]{:S(2)}) collective-permute-start(bf16[128,128]{1,0:T(8,128)(2,1)S(1)} %get-tuple-element.55), channel_id=1, source_target_pairs={{0,32},{32,64},{64,96},{1,33},{33,65},{65,97},{2,34},{34,66},{66,9... | collective-permute-start | bytes 98312 | tf_op jit(solution)/shard_map/ppermute | solution.py:346
  222.8 12.0 %all_to_all.58.mine_ref = bf16[16,128,128]{2,1,0:T(8,128)(2,1)S(1)} all-to-all(bf16[16,128,128]{2,1,0:T(8,128)(2,1)S(1)} %broadcast_in_dim.71), channel_id=1, replica_groups={{0,2,4,6,8,10,12,14,16,18,20,22,24,26,28,30},{1,3,5,7,9,11,13,15,17,19,..., dimensions={0} | all-to-all | bytes 1048576 | tf_op jit(solution)/shard_map/all_to_all | solution.py:291
  234.8 3.4 %collective-permute-start.12 = (bf16[16,128,128]{2,1,0:T(8,128)(2,1)S(1)}, bf16[16,128,128]{2,1,0:T(8,128)(2,1)S(1)}, u32[]{:S(2)}, u32[]{:S(2)}) collective-permute-start(bf16[16,128,128]{2,1,0:T(8,128)(2,1)S(1)} %all_to_all.58.mine_ref), channel_id=1, source_target_pairs={{0,1},{1,0},{2,3},{3,2},{4,5},{5,4},{6,7},{7,6},{8,9},{9,8},{10,11... | collective-permute-start | bytes 1572872 | tf_op jit(solution)/shard_map/ppermute | solution.py:295
  239.8 2.9 %wide.9 = bf16[16,128,256]{2,1,0:T(8,128)(2,1)S(1)} custom-call(s32[1]{0:T(128)} %bitcast.4.core_ref, bf16[16,128,128]{2,1,0:T(8,128)(2,1)S(1)} %all_to_all.58.mine_ref, bf16[16,128,128]{2,1,0:T(8,128)(2,1)S(1)} %collective-permute-done.12.other_ref, f32[64,128]{1,0:T(8,128)S(1)} %bitcast.86, bf16[4128,1792]{1,0:T(8,128)(2,1)S(1)} %pack_wide.1.weight_ref, ...), custom_call_target="tpu_custom_call" | custom-call | flops 1879048192 | bytes 2097152 | tf_op jit(solution)/shard_map/wide/pallas_call | solution.py:251
  242.7 19.0 %all_to_all.59.mine_ref = bf16[16,128,256]{2,1,0:T(8,128)(2,1)S(1)} all-to-all(bf16[16,128,256]{2,1,0:T(8,128)(2,1)S(1)} %wide.9), channel_id=1, replica_groups={{0,2,4,6,8,10,12,14,16,18,20,22,24,26,28,30},{1,3,5,7,9,11,13,15,17,19,..., dimensions={0} | all-to-all | bytes 2097152 | tf_op jit(solution)/shard_map/all_to_all | solution.py:291
  263.8 2.3 collective-permute-done.13.other_ref
  (54 shorter events, 29.6 us)
Async XLA Ops:
  0.0 3.9 %copy-start = (bf16[128,256]{1,0:T(8,128)(2,1)S(1)}, bf16[128,256]{1,0:T(8,128)(2,1)}, u32[]{:S(2)}) copy-start(bf16[128,256]{1,0:T(8,128)(2,1)} %param.7) | copy-start | bytes 196612
  21.5 9.0 %collective-permute-start = (bf16[16,128,128]{2,1,0:T(8,128)(2,1)S(1)}, bf16[16,128,128]{2,1,0:T(8,128)(2,1)S(1)}, u32[]{:S(2)}, u32[]{:S(2)}) collective-permute-start(bf16[16,128,128]{2,1,0:T(8,128)(2,1)S(1)} %all_to_all.50.mine_ref), channel_id=1, source_target_pairs={{0,1},{1,0},{2,3},{3,2},{4,5},{5,4},{6,7},{7,6},{8,9},{9,8},{10,11... | collective-permute-start | bytes 1572872 | tf_op jit(solution)/shard_map/ppermute | solution.py:295
  52.2 7.3 %collective-permute-start.1 = (bf16[16,128,256]{2,1,0:T(8,128)(2,1)S(1)}, bf16[16,128,256]{2,1,0:T(8,128)(2,1)S(1)}, u32[]{:S(2)}, u32[]{:S(2)}) collective-permute-start(bf16[16,128,256]{2,1,0:T(8,128)(2,1)S(1)} %all_to_all.51.mine_ref), channel_id=1, source_target_pairs={{0,1},{1,0},{2,3},{3,2},{4,5},{5,4},{6,7},{7,6},{8,9},{9,8},{10,11... | collective-permute-start | bytes 3145736 | tf_op jit(solution)/shard_map/ppermute | solution.py:295
  60.9 7.1 %collective-permute-start.2 = (bf16[128,128]{1,0:T(8,128)(2,1)S(1)}, bf16[128,128]{1,0:T(8,128)(2,1)S(1)}, u32[]{:S(2)}, u32[]{:S(2)}) collective-permute-start(bf16[128,128]{1,0:T(8,128)(2,1)S(1)} %get-tuple-element.46), channel_id=1, source_target_pairs={{0,32},{32,64},{64,96},{1,33},{33,65},{65,97},{2,34},{34,66},{66,9... | collective-permute-start | bytes 98312 | tf_op jit(solution)/shard_map/ppermute | solution.py:346
  81.4 3.7 %collective-permute-start.3 = (bf16[16,128,128]{2,1,0:T(8,128)(2,1)S(1)}, bf16[16,128,128]{2,1,0:T(8,128)(2,1)S(1)}, u32[]{:S(2)}, u32[]{:S(2)}) collective-permute-start(bf16[16,128,128]{2,1,0:T(8,128)(2,1)S(1)} %all_to_all.52.mine_ref), channel_id=1, source_target_pairs={{0,1},{1,0},{2,3},{3,2},{4,5},{5,4},{6,7},{7,6},{8,9},{9,8},{10,11... | collective-permute-start | bytes 1572872 | tf_op jit(solution)/shard_map/ppermute | solution.py:295
  107.0 4.4 %collective-permute-start.4 = (bf16[16,128,256]{2,1,0:T(8,128)(2,1)S(1)}, bf16[16,128,256]{2,1,0:T(8,128)(2,1)S(1)}, u32[]{:S(2)}, u32[]{:S(2)}) collective-permute-start(bf16[16,128,256]{2,1,0:T(8,128)(2,1)S(1)} %all_to_all.53.mine_ref), channel_id=1, source_target_pairs={{0,1},{1,0},{2,3},{3,2},{4,5},{5,4},{6,7},{7,6},{8,9},{9,8},{10,11... | collective-permute-start | bytes 3145736 | tf_op jit(solution)/shard_map/ppermute | solution.py:295
  112.9 6.8 %collective-permute-start.5 = (bf16[128,128]{1,0:T(8,128)(2,1)S(1)}, bf16[128,128]{1,0:T(8,128)(2,1)S(1)}, u32[]{:S(2)}, u32[]{:S(2)}) collective-permute-start(bf16[128,128]{1,0:T(8,128)(2,1)S(1)} %get-tuple-element.47), channel_id=1, source_target_pairs={{0,32},{32,64},{64,96},{1,33},{33,65},{65,97},{2,34},{34,66},{66,9... | collective-permute-start | bytes 98312 | tf_op jit(solution)/shard_map/ppermute | solution.py:346
  131.7 5.0 %collective-permute-start.6 = (bf16[16,128,128]{2,1,0:T(8,128)(2,1)S(1)}, bf16[16,128,128]{2,1,0:T(8,128)(2,1)S(1)}, u32[]{:S(2)}, u32[]{:S(2)}) collective-permute-start(bf16[16,128,128]{2,1,0:T(8,128)(2,1)S(1)} %all_to_all.54.mine_ref), channel_id=1, source_target_pairs={{0,1},{1,0},{2,3},{3,2},{4,5},{5,4},{6,7},{7,6},{8,9},{9,8},{10,11... | collective-permute-start | bytes 1572872 | tf_op jit(solution)/shard_map/ppermute | solution.py:295
  158.6 4.4 %collective-permute-start.7 = (bf16[16,128,256]{2,1,0:T(8,128)(2,1)S(1)}, bf16[16,128,256]{2,1,0:T(8,128)(2,1)S(1)}, u32[]{:S(2)}, u32[]{:S(2)}) collective-permute-start(bf16[16,128,256]{2,1,0:T(8,128)(2,1)S(1)} %all_to_all.55.mine_ref), channel_id=1, source_target_pairs={{0,1},{1,0},{2,3},{3,2},{4,5},{5,4},{6,7},{7,6},{8,9},{9,8},{10,11... | collective-permute-start | bytes 3145736 | tf_op jit(solution)/shard_map/ppermute | solution.py:295
  164.4 6.8 %collective-permute-start.8 = (bf16[128,128]{1,0:T(8,128)(2,1)S(1)}, bf16[128,128]{1,0:T(8,128)(2,1)S(1)}, u32[]{:S(2)}, u32[]{:S(2)}) collective-permute-start(bf16[128,128]{1,0:T(8,128)(2,1)S(1)} %get-tuple-element.48), channel_id=1, source_target_pairs={{0,32},{32,64},{64,96},{1,33},{33,65},{65,97},{2,34},{34,66},{66,9... | collective-permute-start | bytes 98312 | tf_op jit(solution)/shard_map/ppermute | solution.py:346
  183.2 5.0 %collective-permute-start.9 = (bf16[16,128,128]{2,1,0:T(8,128)(2,1)S(1)}, bf16[16,128,128]{2,1,0:T(8,128)(2,1)S(1)}, u32[]{:S(2)}, u32[]{:S(2)}) collective-permute-start(bf16[16,128,128]{2,1,0:T(8,128)(2,1)S(1)} %all_to_all.56.mine_ref), channel_id=1, source_target_pairs={{0,1},{1,0},{2,3},{3,2},{4,5},{5,4},{6,7},{7,6},{8,9},{9,8},{10,11... | collective-permute-start | bytes 1572872 | tf_op jit(solution)/shard_map/ppermute | solution.py:295
  210.1 4.4 %collective-permute-start.10 = (bf16[16,128,256]{2,1,0:T(8,128)(2,1)S(1)}, bf16[16,128,256]{2,1,0:T(8,128)(2,1)S(1)}, u32[]{:S(2)}, u32[]{:S(2)}) collective-permute-start(bf16[16,128,256]{2,1,0:T(8,128)(2,1)S(1)} %all_to_all.57.mine_ref), channel_id=1, source_target_pairs={{0,1},{1,0},{2,3},{3,2},{4,5},{5,4},{6,7},{7,6},{8,9},{9,8},{10,11... | collective-permute-start | bytes 3145736 | tf_op jit(solution)/shard_map/ppermute | solution.py:295
  215.9 6.8 %collective-permute-start.11 = (bf16[128,128]{1,0:T(8,128)(2,1)S(1)}, bf16[128,128]{1,0:T(8,128)(2,1)S(1)}, u32[]{:S(2)}, u32[]{:S(2)}) collective-permute-start(bf16[128,128]{1,0:T(8,128)(2,1)S(1)} %get-tuple-element.55), channel_id=1, source_target_pairs={{0,32},{32,64},{64,96},{1,33},{33,65},{65,97},{2,34},{34,66},{66,9... | collective-permute-start | bytes 98312 | tf_op jit(solution)/shard_map/ppermute | solution.py:346
  234.8 5.0 %collective-permute-start.12 = (bf16[16,128,128]{2,1,0:T(8,128)(2,1)S(1)}, bf16[16,128,128]{2,1,0:T(8,128)(2,1)S(1)}, u32[]{:S(2)}, u32[]{:S(2)}) collective-permute-start(bf16[16,128,128]{2,1,0:T(8,128)(2,1)S(1)} %all_to_all.58.mine_ref), channel_id=1, source_target_pairs={{0,1},{1,0},{2,3},{3,2},{4,5},{5,4},{6,7},{7,6},{8,9},{9,8},{10,11... | collective-permute-start | bytes 1572872 | tf_op jit(solution)/shard_map/ppermute | solution.py:295
  261.7 4.4 %collective-permute-start.13 = (bf16[16,128,256]{2,1,0:T(8,128)(2,1)S(1)}, bf16[16,128,256]{2,1,0:T(8,128)(2,1)S(1)}, u32[]{:S(2)}, u32[]{:S(2)}) collective-permute-start(bf16[16,128,256]{2,1,0:T(8,128)(2,1)S(1)} %all_to_all.59.mine_ref), channel_id=1, source_target_pairs={{0,1},{1,0},{2,3},{3,2},{4,5},{5,4},{6,7},{7,6},{8,9},{9,8},{10,11... | collective-permute-start | bytes 3145736 | tf_op jit(solution)/shard_map/ppermute | solution.py:295

commit v3 on v2

v3 whole, which is shorter than its diff:
```python
import functools

import jax
import jax.numpy as jnp
from jax import lax
from jax.experimental import pallas as pl
from jax.experimental.pallas import tpu as pltpu
from jax.sharding import PartitionSpec as P

D = 8192
FFW = 14336
BS = 64
CHIPS = 16
ROWS = 64
GU_ROWS = D // 2
GU_COLS = 14 * 128
DN_ROWS = 32 * 256
DN_COLS = 4 * 128
MIB = 1 << 20


def clear(target):
    rows, cols = target.shape

    def one(at, _):
        target[pl.ds(pl.multiple_of(at * 32, 32), 32), :] = jnp.zeros((32, cols), target.dtype)
        return 0

    lax.fori_loop(0, rows // 32, one, 0)


def wide_pack_kernel(goal_ref, gate_hbm, up_hbm, target, buf, spread, sems):
    tiles, slots = goal_ref.shape
    for which, source in enumerate((gate_hbm, up_hbm)):
        for tile in range(tiles):
            at = which * tiles + tile
            pltpu.make_async_copy(source.at[tile], buf.at[at], sems.at[at]).start()
    clear(target)

    def place(chunk, count, first, half, tile, column):
        for group in range(0, count, 8):
            for part in range(32):
                spread[half, group * 32 + part * 8 : group * 32 + part * 8 + 8, :] = chunk[
                    group : group + 8, part * 128 : (part + 1) * 128
                ]
        for row in range(count):
            goal = pl.multiple_of(goal_ref[tile, first + row], 32)
            piece = spread[half, pl.ds(row // 8 * 256 + row % 8, 32, stride=8), :]
            target[pl.ds(goal, 32), pl.ds(column, 128)] = piece.astype(target.dtype)

    def one(at, _):
        pltpu.make_async_copy(gate_hbm.at[0], buf.at[at], sems.at[at]).wait()
        which = (at >= tiles).astype(jnp.int32)
        tile = at - which * tiles
        last = tiles - 1
        column = pl.multiple_of(jnp.where(tile == last, 2 * last + which, which * last + tile) * 128, 128)

        def pair(step, _):
            for half in range(2):
                first = pl.multiple_of(step * 32 + half * 16, 16)
                chunk = buf[at, pl.ds(first, 16), :].astype(jnp.float32)
                place(chunk, 16, first, half, tile, column)
            return 0

        lax.fori_loop(0, slots // 32, pair, 0)
        done = slots // 32 * 32
        half = 0
        while done < slots:
            count = min(16, slots - done)
            chunk = buf[at, done : done + count, :].astype(jnp.float32)
            place(chunk, count, done, half, tile, column)
            done += count
            half = 1 - half
        return 0

    lax.fori_loop(0, 2 * tiles, one, 0)


def down_pack_kernel(goal_ref, source, near, far, buf, spread, sems):
    tiles, slots = goal_ref.shape[0] // 2, goal_ref.shape[1]
    parts = 7
    size = slots // parts
    for part in range(parts):
        pltpu.make_async_copy(
            source.at[pl.ds(part * size, size)], buf.at[pl.ds(part * size, size)], sems.at[part]
        ).start()
    clear(near)
    clear(far)

    def one(part, _):
        pltpu.make_async_copy(
            source.at[pl.ds(0, size)], buf.at[pl.ds(part * size, size)], sems.at[part]
        ).wait()

        def step(at, _):
            for half in range(3):
                slot = part * size + at * 6 + half * 2
                for inner in range(2):
                    chunk = buf[slot + inner].astype(jnp.float32)
                    for lane in range(32):
                        spread[half, lane * 8 + inner * 4 : lane * 8 + inner * 4 + 4, :] = chunk[
                            :, lane * 128 : (lane + 1) * 128
                        ]
                for inner in range(2):
                    for tile in range(tiles):
                        piece = spread[half, pl.ds(inner * 4 + tile, 32, stride=8), :].astype(near.dtype)
                        for which, target in enumerate((near, far)):
                            goal = pl.multiple_of(goal_ref[which * tiles + tile, slot + inner], 32)
                            target[pl.ds(goal, 32), tile * 128 : (tile + 1) * 128] = piece
            return 0

        lax.fori_loop(0, size // 6, step, 0)
        return 0

    lax.fori_loop(0, parts, one, 0)


def pack(kernel, goals, sources, buf, spread, copies, shape, results, name):
    sources = [pltpu.with_memory_space_constraint(source, pltpu.HBM) for source in sources]
    return pl.pallas_call(
        kernel,
        out_shape=[pltpu.VMEM(shape, jnp.bfloat16)] * results,
        in_specs=[pl.BlockSpec(memory_space=pltpu.SMEM)]
        + [pl.BlockSpec(memory_space=pltpu.HBM)] * len(sources),
        out_specs=[pl.BlockSpec(memory_space=pltpu.VMEM)] * results,
        scratch_shapes=[
            pltpu.VMEM(buf, jnp.bfloat16),
            pltpu.VMEM(spread + (128,), jnp.float32),
            pltpu.SemaphoreType.DMA((copies,)),
        ],
        compiler_params=pltpu.CompilerParams(vmem_limit_bytes=12 * MIB),
        cost_estimate=pl.CostEstimate(flops=0, bytes_accessed=40 * MIB, transcendentals=0),
        name=name,
    )(goals, *sources)


def densify_wide(goals, gate_blocks, up_blocks):
    tiles, slots = goals.shape
    buf = (2 * tiles, slots, BS * BS)
    shape = (GU_ROWS + 32, GU_COLS)
    sources = (gate_blocks, up_blocks)
    return pack(wide_pack_kernel, goals, sources, buf, (2, 512), 2 * tiles, shape, 1, "pack_wide")[0]


def densify_down(goals, blocks):
    tiles, slots = blocks.shape[:2]
    shape = (DN_ROWS // 2 + 32, DN_COLS)
    blocks = jnp.transpose(blocks, (1, 0, 2))
    buf = (slots, tiles, BS * BS)
    return pack(down_pack_kernel, goals, (blocks,), buf, (3, 256), 7, shape, 2, "pack_down")


def in_goals(index):
    device = index // 4
    row = ((device % 2) * CHIPS + device // 2) * 128 + (index % 4) * 32
    return jnp.where(index >= 0, row, GU_ROWS)


def out_goals(index, core):
    device = index // 7
    row = device // 2 * 256 + (index % 7) * 32
    near = (device % 2) == core
    trash = DN_ROWS // 2
    return jnp.concatenate(
        [
            jnp.where((index >= 0) & near, row, trash),
            jnp.where((index >= 0) & jnp.logical_not(near), row, trash),
        ],
        axis=0,
    )


def fold(even, odd, at):
    low = lax.broadcasted_iota(jnp.int32, (ROWS, 128), 1) < 64
    e0, e1 = even[:, at : at + 128], even[:, at + 128 : at + 256]
    o0, o1 = odd[:, at : at + 128], odd[:, at + 128 : at + 256]
    return jnp.where(low, e0, o1) + pltpu.roll(jnp.where(low, e1, o0), 64, 1)


def near_kernel(core_ref, part_ref, gain_ref, weight_ref, acc_ref, square_ref, scaled):
    core = core_ref[0]
    total = jnp.zeros((2 * ROWS, 128), jnp.float32)
    gains = gain_ref[pl.ds(pl.multiple_of(core * 32, 32), 32), :]
    for chip in range(CHIPS):
        value = part_ref[chip].astype(jnp.float32)
        total += value * value
        scaled[:, chip * 128 : (chip + 1) * 128] = (value * both_rows(gains, chip)).astype(jnp.bfloat16)
    square_ref[...] = total
    rows = pl.ds(pl.multiple_of(core * (GU_ROWS // 2), GU_ROWS // 2), GU_ROWS // 2)
    for tile in range(7):
        acc_ref[:, tile * 256 : (tile + 1) * 256] = jnp.dot(
            scaled[...], weight_ref[rows, tile * 256 : (tile + 1) * 256], preferred_element_type=jnp.float32
        )


def both_rows(gains, chip):
    return jnp.concatenate(
        [jnp.broadcast_to(gains[2 * chip + p : 2 * chip + p + 1], (ROWS, 128)) for p in range(2)], axis=0
    )


def far_kernel(core_ref, part_ref, gain_ref, weight_ref, order_ref, acc_ref, square_ref, out_ref, scaled):
    core = 1 - core_ref[0]
    total = square_ref[...]
    gains = gain_ref[pl.ds(pl.multiple_of(core * 32, 32), 32), :]
    for chip in range(CHIPS):
        value = part_ref[chip].astype(jnp.float32)
        total += value * value
        scaled[:, chip * 128 : (chip + 1) * 128] = (value * both_rows(gains, chip)).astype(jnp.bfloat16)
    stat = jnp.sum(total[:ROWS] + total[ROWS:], axis=1, keepdims=True) / D
    scale = lax.rsqrt(stat + 1e-05)
    rows = pl.ds(pl.multiple_of(core * (GU_ROWS // 2), GU_ROWS // 2), GU_ROWS // 2)

    def product(tile):
        acc = acc_ref[:, tile * 256 : (tile + 1) * 256] + jnp.dot(
            scaled[...], weight_ref[rows, tile * 256 : (tile + 1) * 256], preferred_element_type=jnp.float32
        )
        return fold(acc[:ROWS], acc[ROWS:], 0) * scale

    pieces = []
    for pair in range(3):
        gate = product(pair)
        up = product(pair + 3)
        pieces.append((gate / (1.0 + jnp.exp(-gate)) * up).astype(jnp.bfloat16))
    both = product(6)
    last = both / (1.0 + jnp.exp(-both)) * pltpu.roll(both, 64, 1)
    low = lax.broadcasted_iota(jnp.int32, (ROWS, 128), 1) < 64
    pieces.append(jnp.where(low, last, 0.0).astype(jnp.bfloat16))
    hidden = jnp.dot(
        jnp.concatenate(pieces, axis=1), order_ref[...], preferred_element_type=jnp.float32
    ).astype(jnp.bfloat16)
    hidden = jnp.concatenate([hidden[:, :256], hidden[:, 256:]], axis=0)
    for chip in range(CHIPS):
        out_ref[chip] = hidden


def mixed_of(part_ref, weight_ref):
    left = jnp.concatenate([part_ref[chip] for chip in range(CHIPS)], axis=1)
    acc = jnp.dot(left, weight_ref[: DN_ROWS // 2, :], preferred_element_type=jnp.float32)
    even, odd = acc[:ROWS], acc[ROWS:]
    return jnp.concatenate([fold(even, odd, 0), fold(even, odd, 256)], axis=1)


def send_kernel(part_ref, weight_ref, out_ref):
    out_ref[...] = mixed_of(part_ref, weight_ref)


def keep_kernel(part_ref, weight_ref, got_ref, taken_ref, order_ref, back_ref, out_ref, next_ref):
    taken = jnp.concatenate([taken_ref[:ROWS], taken_ref[ROWS:]], axis=1)
    taken = jnp.dot(taken, back_ref[...], preferred_element_type=jnp.float32)
    produced = (taken + (mixed_of(part_ref, weight_ref) + got_ref[...])).astype(jnp.bfloat16)
    out_ref[...] = produced
    ordered = jnp.dot(produced, order_ref[...], preferred_element_type=jnp.float32).astype(jnp.bfloat16)
    next_ref[...] = jnp.concatenate([ordered[:, :128], ordered[:, 128:]], axis=0)


def prepare_kernel(x_ref, norm_ref, order_ref, *refs):
    firsts, gain_ref, rows_ref = refs[:-2], refs[-2], refs[-1]
    for device in range(2 * CHIPS):
        rows_ref[device : device + 1, :] = norm_ref[:, device * 256 : (device + 1) * 256]
    left = rows_ref[...]
    gain = jnp.zeros(left.shape, jnp.float32)
    for _ in range(3):
        piece = left.astype(jnp.bfloat16)
        left = left - piece.astype(jnp.float32)
        gain = gain + jnp.dot(piece, order_ref[...], preferred_element_type=jnp.float32)
    for device in range(2 * CHIPS):
        at = 2 * (device % 2 * CHIPS + device // 2)
        for p in range(2):
            gain_ref[at + p : at + p + 1, :] = gain[device : device + 1, p * 128 : (p + 1) * 128]
    ordered = jnp.dot(x_ref[...], order_ref[...], preferred_element_type=jnp.float32).astype(jnp.bfloat16)
    for group, ref in enumerate(firsts):
        part = ordered[group * ROWS : (group + 1) * ROWS]
        ref[...] = jnp.concatenate([part[:, :128], part[:, 128:]], axis=0)


def pick_kernel(place_ref, *refs):
    made, out_ref = refs[:-1], refs[-1]
    groups = out_ref.shape[0] // ROWS
    for segment in range(len(made) - groups + 1):

        @pl.when(place_ref[0] == segment)
        def _():
            for group in range(groups):
                out_ref[group * ROWS : (group + 1) * ROWS, :] = made[group + segment][...]


VMEM = pl.BlockSpec(memory_space=pltpu.VMEM)
SMEM = pl.BlockSpec(memory_space=pltpu.SMEM)


def resident(weight):
    return pltpu.with_memory_space_constraint(weight, pltpu.VMEM)


def cost(products):
    return pl.CostEstimate(flops=2 * 128 * products, bytes_accessed=2 * MIB, transcendentals=0)


def prepare(x_in, norm_gain, x_order):
    groups = x_in.shape[0] // ROWS
    return pl.pallas_call(
        prepare_kernel,
        out_shape=[jax.ShapeDtypeStruct((2 * ROWS, 128), jnp.bfloat16)] * groups
        + [jax.ShapeDtypeStruct((4 * CHIPS, 128), jnp.float32)],
        in_specs=[VMEM] * 3,
        out_specs=[VMEM] * (groups + 1),
        scratch_shapes=[pltpu.VMEM((2 * CHIPS, 256), jnp.float32)],
        compiler_params=pltpu.CompilerParams(vmem_limit_bytes=8 * MIB),
        name="prepare",
    )(x_in, norm_gain, x_order)


def call_near(core, part, gain, weight):
    return pl.pallas_call(
        near_kernel,
        out_shape=(
            jax.ShapeDtypeStruct((2 * ROWS, GU_COLS), jnp.float32),
            jax.ShapeDtypeStruct((2 * ROWS, 128), jnp.float32),
        ),
        in_specs=[SMEM, VMEM, VMEM, VMEM],
        out_specs=(VMEM, VMEM),
        scratch_shapes=[pltpu.VMEM((2 * ROWS, GU_ROWS // 2), jnp.bfloat16)],
        compiler_params=pltpu.CompilerParams(vmem_limit_bytes=16 * MIB),
        cost_estimate=cost(GU_ROWS * GU_COLS // 2),
        name="near",
    )(core, part, gain, resident(weight))


def call_far(core, part, gain, weight, order, acc, square):
    return pl.pallas_call(
        far_kernel,
        out_shape=jax.ShapeDtypeStruct((CHIPS, 2 * ROWS, 256), jnp.bfloat16),
        in_specs=[SMEM] + [VMEM] * 6,
        out_specs=VMEM,
        scratch_shapes=[pltpu.VMEM((2 * ROWS, GU_ROWS // 2), jnp.bfloat16)],
        compiler_params=pltpu.CompilerParams(vmem_limit_bytes=16 * MIB),
        cost_estimate=cost(GU_ROWS * GU_COLS // 2),
        name="far",
    )(core, part, gain, resident(weight), order, acc, square)


def call_send(part, weight):
    return pl.pallas_call(
        send_kernel,
        out_shape=jax.ShapeDtypeStruct((ROWS, 256), jnp.float32),
        in_specs=[VMEM] * 2,
        out_specs=VMEM,
        compiler_params=pltpu.CompilerParams(vmem_limit_bytes=16 * MIB),
        cost_estimate=cost(DN_ROWS * DN_COLS // 2),
        name="send",
    )(part, resident(weight))


def call_keep(part, weight, got, taken, order, back):
    return pl.pallas_call(
        keep_kernel,
        out_shape=(
            jax.ShapeDtypeStruct((ROWS, 256), jnp.bfloat16),
            jax.ShapeDtypeStruct((2 * ROWS, 128), jnp.bfloat16),
        ),
        in_specs=[VMEM] * 6,
        out_specs=(VMEM, VMEM),
        compiler_params=pltpu.CompilerParams(vmem_limit_bytes=16 * MIB),
        cost_estimate=cost(DN_ROWS * DN_COLS // 2),
        name="keep",
    )(part, resident(weight), got, taken, order, back)


def call_pick(place, made, groups):
    return pl.pallas_call(
        pick_kernel,
        out_shape=jax.ShapeDtypeStruct((groups * ROWS, 256), jnp.bfloat16),
        in_specs=[SMEM] + [VMEM] * len(made),
        out_specs=VMEM,
        compiler_params=pltpu.CompilerParams(vmem_limit_bytes=4 * MIB),
        name="pick",
    )(place, *made)


def orders():
    source = jnp.arange(256)
    goal = (source % 2) * 128 + source // 64 * 32 + source % 64 // 2
    x_order = (goal[:, None] == jnp.arange(256)[None, :]).astype(jnp.bfloat16)
    source = jnp.arange(512)
    goal = (source % 2) * 256 + source // 64 * 32 + source % 64 // 2
    h_order = (goal[:, None] == jnp.arange(512)[None, :]).astype(jnp.bfloat16)
    return x_order, h_order


def exchanged(value):
    same_core = [[2 * chip + core for chip in range(CHIPS)] for core in range(2)]
    return lax.all_to_all(value, "tensor", 0, 0, axis_index_groups=same_core)


def swapped(value):
    return lax.ppermute(value, "tensor", [(i, i ^ 1) for i in range(2 * CHIPS)])


def local(x_in, norm_gain, in_index, gate_blocks, up_blocks, out_index, down_blocks):
    segment_count = lax.axis_size("segment")
    segment_at = lax.axis_index("segment")
    core = (lax.axis_index("tensor") % 2).astype(jnp.int32)[None]
    tokens = x_in.shape[0]
    group_count = tokens // ROWS
    tick_count = group_count + segment_count - 1
    x_order, h_order = orders()
    x_back = x_order.T
    *firsts, gain = prepare(x_in, norm_gain, x_order)
    is_first = jnp.broadcast_to(segment_at == 0, (8, 128)).astype(jnp.bfloat16)
    place = segment_at.astype(jnp.int32)[None]
    to_wide, to_down = in_goals(in_index[0]), out_goals(out_index[0], core[0])
    to_wide, to_down, core, place, x_order, x_back, h_order, gain, firsts, is_first = lax.optimization_barrier(
        (to_wide, to_down, core, place, x_order, x_back, h_order, gain, firsts, is_first)
    )
    carried = None
    made = []
    hops = [(i, i + 1) for i in range(segment_count - 1)]
    for tick in range(tick_count):
        taken = firsts[min(tick, group_count - 1)]
        if carried is not None:
            taken = jnp.where(jnp.tile(is_first, (2 * ROWS // 8, 1)) > 0, taken, carried)
        mine = exchanged(jnp.broadcast_to(taken[None], (CHIPS, 2 * ROWS, 128)))
        if tick == 0:
            mine, to_wide, to_down = lax.optimization_barrier((mine, to_wide, to_down))
            wide = densify_wide(to_wide, gate_blocks[0], up_blocks[0])
            down, lent = densify_down(to_down, down_blocks[0])
            borrowed = swapped(lent)
        other = swapped(mine)
        acc, square = call_near(core, mine, gain, wide)
        hidden = call_far(core, other, gain, wide, h_order, acc, square)
        mine = exchanged(hidden)
        got = swapped(call_send(mine, borrowed))
        produced, ordered = call_keep(mine, down, got, taken, x_order, x_back)
        made.append(produced)
        if tick + 1 < tick_count:
            carried = lax.ppermute(ordered, "segment", hops)
    return call_pick(place, made, group_count)[None]


def solution(mesh):
    placed = (
        P("replica", "tensor"),
        P("segment", None),
        P("segment", "tensor", None),
        P("segment", "tensor", None, None),
        P("segment", "tensor", None, None),
        P("segment", "tensor", None),
        P("segment", "tensor", None, None),
    )
    return jax.shard_map(
        local,
        mesh=mesh,
        in_specs=placed,
        out_specs=P("segment", "replica", "tensor"),
        check_vma=False,
    )
```

time: 269 us -> 262 us (0.974)
  waiting for transfers between devices: 19.3 us -> 9.7 us
  Pallas kernels: 34.3 us -> 37.1 us
    ppermute x10 -> x11, waiting for transfers between devices: 15.3 us -> 5.7 us  [swapped(): return lax.ppermute(value, 'tensor', [(i, i ^ 1) for i in range(2 * CHIPS)])]
    pallas_call x12 -> x24, Pallas kernels: 34.3 us -> 37.1 us  [the longest x2 12.4 us: pack(): pl.pallas_call(kernel, out_shape=[pltpu.VMEM(shape, jnp.bfloat16)] * resu...]
    ppermute x10 -> x11, starting transfers between devices: 25.2 us -> 26.8 us  [swapped(): return lax.ppermute(value, 'tensor', [(i, i ^ 1) for i in range(2 * CHIPS)])]
  transfers between devices with their start and end apart: 14 -> 15, of which waited for: 12 -> 13; matrix products, arithmetic and copies ran while one was open for 0% -> 0% of each run, Pallas kernels for 4% -> 6%
where the time goes in v3:
time: 262 us; the launch traced here: 261 us
  blocking collectives  160 us (61%)
  starting transfers between devices  50.2 us (19%)
  Pallas kernels  37.1 us (14%)
  waiting for transfers between devices  9.7 us (4%)
    all_to_all x10, blocking collectives, exchanged(): return lax.all_to_all(value, 'tensor', 0, 0, axis_index_groups=same_core)  160 us
    ppermute x11, starting transfers between devices, swapped(): return lax.ppermute(value, 'tensor', [(i, i ^ 1) for i in range(2 * CHIPS)])  26.8 us
    ppermute x4, starting transfers between devices, local(): carried = lax.ppermute(ordered, 'segment', hops)  23.4 us
    pallas_call x2, Pallas kernels, pack(): pl.pallas_call(kernel, out_shape=[pltpu.VMEM(shape, jnp.bfloat16)] * resu...  12.4 us
    pallas_call x5, Pallas kernels, call_far(): pl.pallas_call(far_kernel, out_shape=jax.ShapeDtypeStruct((CHIPS, 2 * ROW...  8.71 us
    pallas_call x5, Pallas kernels, call_near(): pl.pallas_call(near_kernel, out_shape=(jax.ShapeDtypeStruct((2 * ROWS, GU...  6.17 us
    ppermute x11, waiting for transfers between devices, swapped(): return lax.ppermute(value, 'tensor', [(i, i ^ 1) for i in range(2 * CHIPS)])  5.7 us
  transfers between devices with their start and end apart: 15, of which 13 were waited for; matrix products, arithmetic and copies ran while one was open for 0% of the time, Pallas kernels for 6%

profile of v3, /device:TPU:65, one launch (start us, length us, event | category | flops | bytes accessed | tf_op | source)
XLA Modules:
  0.0 260.9 jit_solution(10428657921006163399)
XLA Ops:
  3.7 16.9 %all_to_all.50.part_ref = bf16[16,128,128]{2,1,0:T(8,128)(2,1)S(1)} all-to-all(bf16[16,128,128]{2,1,0:T(8,128)(2,1)S(1)} %broadcast_in_dim.60), channel_id=1, replica_groups={{0,2,4,6,8,10,12,14,16,18,20,22,24,26,28,30},{1,3,5,7,9,11,13,15,17,19,..., dimensions={0} | all-to-all | bytes 1048576 | tf_op jit(solution)/shard_map/all_to_all | solution.py:393
  20.6 5.5 %pack_down.1 = (bf16[4128,512]{1,0:T(8,128)(2,1)S(1)}, bf16[4128,512]{1,0:T(8,128)(2,1)S(1)}) custom-call(s32[8,126]{1,0:T(8,128)S(1)} %pad_add_fusion.goal_ref, bf16[126,4,4096]{2,1,0:T(4,128)(2,1)} %bitcast.77), custom_call_target="tpu_custom_call" | custom-call | bytes 41943040 | tf_op jit(solution)/shard_map/pack_down/pallas_call | solution.py:120
  26.1 2.2 collective-permute-start.1
  28.4 6.9 %pack_wide.1.weight_ref = bf16[4128,1792]{1,0:T(8,128)(2,1)S(1)} custom-call(s32[7,72]{1,0:T(8,128)S(1)} %fusion.15.goal_ref, bf16[7,72,4096]{2,1,0:T(8,128)(2,1)} %bitcast.78, bf16[7,72,4096]{2,1,0:T(8,128)(2,1)} %bitcast.79), custom_call_target="tpu_custom_call" | custom-call | bytes 41943040 | tf_op jit(solution)/shard_map/pack_wide/pallas_call | solution.py:120
  36.6 1.8 far.5
  38.3 19.0 %all_to_all.51.part_ref = bf16[16,128,256]{2,1,0:T(8,128)(2,1)S(1)} all-to-all(bf16[16,128,256]{2,1,0:T(8,128)(2,1)S(1)} %far.5), channel_id=1, replica_groups={{0,2,4,6,8,10,12,14,16,18,20,22,24,26,28,30},{1,3,5,7,9,11,13,15,17,19,..., dimensions={0} | all-to-all | bytes 2097152 | tf_op jit(solution)/shard_map/all_to_all | solution.py:393
  58.1 2.2 collective-permute-start.2
  62.1 6.1 %collective-permute-start.3 = (bf16[128,128]{1,0:T(8,128)(2,1)S(1)}, bf16[128,128]{1,0:T(8,128)(2,1)S(1)}, u32[]{:S(2)}, u32[]{:S(2)}) collective-permute-start(bf16[128,128]{1,0:T(8,128)(2,1)S(1)} %get-tuple-element.65), channel_id=1, source_target_pairs={{0,32},{32,64},{64,96},{1,33},{33,65},{65,97},{2,34},{34,66},{66,9... | collective-permute-start | bytes 98312 | tf_op jit(solution)/shard_map/ppermute | solution.py:437
  69.3 12.0 %all_to_all.52.part_ref = bf16[16,128,128]{2,1,0:T(8,128)(2,1)S(1)} all-to-all(bf16[16,128,128]{2,1,0:T(8,128)(2,1)S(1)} %broadcast_in_dim.61), channel_id=1, replica_groups={{0,2,4,6,8,10,12,14,16,18,20,22,24,26,28,30},{1,3,5,7,9,11,13,15,17,19,..., dimensions={0} | all-to-all | bytes 1048576 | tf_op jit(solution)/shard_map/all_to_all | solution.py:393
  81.3 3.4 %collective-permute-start.4 = (bf16[16,128,128]{2,1,0:T(8,128)(2,1)S(1)}, bf16[16,128,128]{2,1,0:T(8,128)(2,1)S(1)}, u32[]{:S(2)}, u32[]{:S(2)}) collective-permute-start(bf16[16,128,128]{2,1,0:T(8,128)(2,1)S(1)} %all_to_all.52.part_ref), channel_id=1, source_target_pairs={{0,1},{1,0},{2,3},{3,2},{4,5},{5,4},{6,7},{7,6},{8,9},{9,8},{10,11... | collective-permute-start | bytes 1572872 | tf_op jit(solution)/shard_map/ppermute | solution.py:397
  86.3 1.7 far.6
  88.0 19.0 %all_to_all.53.part_ref = bf16[16,128,256]{2,1,0:T(8,128)(2,1)S(1)} all-to-all(bf16[16,128,256]{2,1,0:T(8,128)(2,1)S(1)} %far.6), channel_id=1, replica_groups={{0,2,4,6,8,10,12,14,16,18,20,22,24,26,28,30},{1,3,5,7,9,11,13,15,17,19,..., dimensions={0} | all-to-all | bytes 2097152 | tf_op jit(solution)/shard_map/all_to_all | solution.py:393
  107.8 2.1 collective-permute-start.5
  111.7 5.8 %collective-permute-start.6 = (bf16[128,128]{1,0:T(8,128)(2,1)S(1)}, bf16[128,128]{1,0:T(8,128)(2,1)S(1)}, u32[]{:S(2)}, u32[]{:S(2)}) collective-permute-start(bf16[128,128]{1,0:T(8,128)(2,1)S(1)} %get-tuple-element.69), channel_id=1, source_target_pairs={{0,32},{32,64},{64,96},{1,33},{33,65},{65,97},{2,34},{34,66},{66,9... | collective-permute-start | bytes 98312 | tf_op jit(solution)/shard_map/ppermute | solution.py:437
  118.6 12.0 %all_to_all.54.part_ref = bf16[16,128,128]{2,1,0:T(8,128)(2,1)S(1)} all-to-all(bf16[16,128,128]{2,1,0:T(8,128)(2,1)S(1)} %broadcast_in_dim.62), channel_id=1, replica_groups={{0,2,4,6,8,10,12,14,16,18,20,22,24,26,28,30},{1,3,5,7,9,11,13,15,17,19,..., dimensions={0} | all-to-all | bytes 1048576 | tf_op jit(solution)/shard_map/all_to_all | solution.py:393
  130.6 3.4 %collective-permute-start.7 = (bf16[16,128,128]{2,1,0:T(8,128)(2,1)S(1)}, bf16[16,128,128]{2,1,0:T(8,128)(2,1)S(1)}, u32[]{:S(2)}, u32[]{:S(2)}) collective-permute-start(bf16[16,128,128]{2,1,0:T(8,128)(2,1)S(1)} %all_to_all.54.part_ref), channel_id=1, source_target_pairs={{0,1},{1,0},{2,3},{3,2},{4,5},{5,4},{6,7},{7,6},{8,9},{9,8},{10,11... | collective-permute-start | bytes 1572872 | tf_op jit(solution)/shard_map/ppermute | solution.py:397
  135.6 1.7 far.7
  137.3 19.0 %all_to_all.55.part_ref = bf16[16,128,256]{2,1,0:T(8,128)(2,1)S(1)} all-to-all(bf16[16,128,256]{2,1,0:T(8,128)(2,1)S(1)} %far.7), channel_id=1, replica_groups={{0,2,4,6,8,10,12,14,16,18,20,22,24,26,28,30},{1,3,5,7,9,11,13,15,17,19,..., dimensions={0} | all-to-all | bytes 2097152 | tf_op jit(solution)/shard_map/all_to_all | solution.py:393
  157.1 2.2 collective-permute-start.8
  161.0 5.8 %collective-permute-start.9 = (bf16[128,128]{1,0:T(8,128)(2,1)S(1)}, bf16[128,128]{1,0:T(8,128)(2,1)S(1)}, u32[]{:S(2)}, u32[]{:S(2)}) collective-permute-start(bf16[128,128]{1,0:T(8,128)(2,1)S(1)} %get-tuple-element.73), channel_id=1, source_target_pairs={{0,32},{32,64},{64,96},{1,33},{33,65},{65,97},{2,34},{34,66},{66,9... | collective-permute-start | bytes 98312 | tf_op jit(solution)/shard_map/ppermute | solution.py:437
  167.9 12.0 %all_to_all.56.part_ref = bf16[16,128,128]{2,1,0:T(8,128)(2,1)S(1)} all-to-all(bf16[16,128,128]{2,1,0:T(8,128)(2,1)S(1)} %broadcast_in_dim.63), channel_id=1, replica_groups={{0,2,4,6,8,10,12,14,16,18,20,22,24,26,28,30},{1,3,5,7,9,11,13,15,17,19,..., dimensions={0} | all-to-all | bytes 1048576 | tf_op jit(solution)/shard_map/all_to_all | solution.py:393
  179.9 3.4 %collective-permute-start.10 = (bf16[16,128,128]{2,1,0:T(8,128)(2,1)S(1)}, bf16[16,128,128]{2,1,0:T(8,128)(2,1)S(1)}, u32[]{:S(2)}, u32[]{:S(2)}) collective-permute-start(bf16[16,128,128]{2,1,0:T(8,128)(2,1)S(1)} %all_to_all.56.part_ref), channel_id=1, source_target_pairs={{0,1},{1,0},{2,3},{3,2},{4,5},{5,4},{6,7},{7,6},{8,9},{9,8},{10,11... | collective-permute-start | bytes 1572872 | tf_op jit(solution)/shard_map/ppermute | solution.py:397
  184.9 1.7 far.8
  186.6 19.0 %all_to_all.57.part_ref = bf16[16,128,256]{2,1,0:T(8,128)(2,1)S(1)} all-to-all(bf16[16,128,256]{2,1,0:T(8,128)(2,1)S(1)} %far.8), channel_id=1, replica_groups={{0,2,4,6,8,10,12,14,16,18,20,22,24,26,28,30},{1,3,5,7,9,11,13,15,17,19,..., dimensions={0} | all-to-all | bytes 2097152 | tf_op jit(solution)/shard_map/all_to_all | solution.py:393
  206.4 2.2 collective-permute-start.11
  210.3 5.8 %collective-permute-start.12 = (bf16[128,128]{1,0:T(8,128)(2,1)S(1)}, bf16[128,128]{1,0:T(8,128)(2,1)S(1)}, u32[]{:S(2)}, u32[]{:S(2)}) collective-permute-start(bf16[128,128]{1,0:T(8,128)(2,1)S(1)} %get-tuple-element.77), channel_id=1, source_target_pairs={{0,32},{32,64},{64,96},{1,33},{33,65},{65,97},{2,34},{34,66},{66,9... | collective-permute-start | bytes 98312 | tf_op jit(solution)/shard_map/ppermute | solution.py:437
  217.2 12.0 %all_to_all.58.part_ref = bf16[16,128,128]{2,1,0:T(8,128)(2,1)S(1)} all-to-all(bf16[16,128,128]{2,1,0:T(8,128)(2,1)S(1)} %broadcast_in_dim.64), channel_id=1, replica_groups={{0,2,4,6,8,10,12,14,16,18,20,22,24,26,28,30},{1,3,5,7,9,11,13,15,17,19,..., dimensions={0} | all-to-all | bytes 1048576 | tf_op jit(solution)/shard_map/all_to_all | solution.py:393
  229.2 3.4 %collective-permute-start.13 = (bf16[16,128,128]{2,1,0:T(8,128)(2,1)S(1)}, bf16[16,128,128]{2,1,0:T(8,128)(2,1)S(1)}, u32[]{:S(2)}, u32[]{:S(2)}) collective-permute-start(bf16[16,128,128]{2,1,0:T(8,128)(2,1)S(1)} %all_to_all.58.part_ref), channel_id=1, source_target_pairs={{0,1},{1,0},{2,3},{3,2},{4,5},{5,4},{6,7},{7,6},{8,9},{9,8},{10,11... | collective-permute-start | bytes 1572872 | tf_op jit(solution)/shard_map/ppermute | solution.py:397
  234.2 1.7 far.9
  235.9 19.0 %all_to_all.59.part_ref = bf16[16,128,256]{2,1,0:T(8,128)(2,1)S(1)} all-to-all(bf16[16,128,256]{2,1,0:T(8,128)(2,1)S(1)} %far.9), channel_id=1, replica_groups={{0,2,4,6,8,10,12,14,16,18,20,22,24,26,28,30},{1,3,5,7,9,11,13,15,17,19,..., dimensions={0} | all-to-all | bytes 2097152 | tf_op jit(solution)/shard_map/all_to_all | solution.py:393
  255.7 2.1 collective-permute-start.14
  258.7 1.5 keep.9
  (55 shorter events, 28.1 us)
Async XLA Ops:
  1.8 0.8 copy-start
  2.6 0.8 copy-start.1
  26.1 31.2 %collective-permute-start.1 = (bf16[4128,512]{1,0:T(8,128)(2,1)S(1)}, bf16[4128,512]{1,0:T(8,128)(2,1)S(1)}, u32[]{:S(2)}, u32[]{:S(2)}) collective-permute-start(bf16[4128,512]{1,0:T(8,128)(2,1)S(1)} %get-tuple-element.59), channel_id=1, source_target_pairs={{0,1},{1,0},{2,3},{3,2},{4,5},{5,4},{6,7},{7,6},{8,9},{9,8},{10,11... | collective-permute-start | bytes 12681224 | tf_op jit(solution)/shard_map/ppermute | solution.py:397
  28.3 8.2 %collective-permute-start = (bf16[16,128,128]{2,1,0:T(8,128)(2,1)S(1)}, bf16[16,128,128]{2,1,0:T(8,128)(2,1)S(1)}, u32[]{:S(2)}, u32[]{:S(2)}) collective-permute-start(bf16[16,128,128]{2,1,0:T(8,128)(2,1)S(1)} %all_to_all.50.part_ref), channel_id=1, source_target_pairs={{0,1},{1,0},{2,3},{3,2},{4,5},{5,4},{6,7},{7,6},{8,9},{9,8},{10,11... | collective-permute-start | bytes 1572872 | tf_op jit(solution)/shard_map/ppermute | solution.py:397
  58.1 3.1 %collective-permute-start.2 = (f32[64,256]{1,0:T(8,128)S(1)}, f32[64,256]{1,0:T(8,128)S(1)}, u32[]{:S(2)}, u32[]{:S(2)}) collective-permute-start(f32[64,256]{1,0:T(8,128)S(1)} %send.5), channel_id=1, source_target_pairs={{0,1},{1,0},{2,3},{3,2},{4,5},{5,4},{6,7},{7,6},{8,9},{9,8},{10,11... | collective-permute-start | bytes 196616 | tf_op jit(solution)/shard_map/ppermute | solution.py:397
  62.1 7.1 %collective-permute-start.3 = (bf16[128,128]{1,0:T(8,128)(2,1)S(1)}, bf16[128,128]{1,0:T(8,128)(2,1)S(1)}, u32[]{:S(2)}, u32[]{:S(2)}) collective-permute-start(bf16[128,128]{1,0:T(8,128)(2,1)S(1)} %get-tuple-element.65), channel_id=1, source_target_pairs={{0,32},{32,64},{64,96},{1,33},{33,65},{65,97},{2,34},{34,66},{66,9... | collective-permute-start | bytes 98312 | tf_op jit(solution)/shard_map/ppermute | solution.py:437
  81.3 5.0 %collective-permute-start.4 = (bf16[16,128,128]{2,1,0:T(8,128)(2,1)S(1)}, bf16[16,128,128]{2,1,0:T(8,128)(2,1)S(1)}, u32[]{:S(2)}, u32[]{:S(2)}) collective-permute-start(bf16[16,128,128]{2,1,0:T(8,128)(2,1)S(1)} %all_to_all.52.part_ref), channel_id=1, source_target_pairs={{0,1},{1,0},{2,3},{3,2},{4,5},{5,4},{6,7},{7,6},{8,9},{9,8},{10,11... | collective-permute-start | bytes 1572872 | tf_op jit(solution)/shard_map/ppermute | solution.py:397
  107.8 3.0 %collective-permute-start.5 = (f32[64,256]{1,0:T(8,128)S(1)}, f32[64,256]{1,0:T(8,128)S(1)}, u32[]{:S(2)}, u32[]{:S(2)}) collective-permute-start(f32[64,256]{1,0:T(8,128)S(1)} %send.6), channel_id=1, source_target_pairs={{0,1},{1,0},{2,3},{3,2},{4,5},{5,4},{6,7},{7,6},{8,9},{9,8},{10,11... | collective-permute-start | bytes 196616 | tf_op jit(solution)/shard_map/ppermute | solution.py:397
  111.7 6.8 %collective-permute-start.6 = (bf16[128,128]{1,0:T(8,128)(2,1)S(1)}, bf16[128,128]{1,0:T(8,128)(2,1)S(1)}, u32[]{:S(2)}, u32[]{:S(2)}) collective-permute-start(bf16[128,128]{1,0:T(8,128)(2,1)S(1)} %get-tuple-element.69), channel_id=1, source_target_pairs={{0,32},{32,64},{64,96},{1,33},{33,65},{65,97},{2,34},{34,66},{66,9... | collective-permute-start | bytes 98312 | tf_op jit(solution)/shard_map/ppermute | solution.py:437
  130.6 5.0 %collective-permute-start.7 = (bf16[16,128,128]{2,1,0:T(8,128)(2,1)S(1)}, bf16[16,128,128]{2,1,0:T(8,128)(2,1)S(1)}, u32[]{:S(2)}, u32[]{:S(2)}) collective-permute-start(bf16[16,128,128]{2,1,0:T(8,128)(2,1)S(1)} %all_to_all.54.part_ref), channel_id=1, source_target_pairs={{0,1},{1,0},{2,3},{3,2},{4,5},{5,4},{6,7},{7,6},{8,9},{9,8},{10,11... | collective-permute-start | bytes 1572872 | tf_op jit(solution)/shard_map/ppermute | solution.py:397
  157.1 3.1 %collective-permute-start.8 = (f32[64,256]{1,0:T(8,128)S(1)}, f32[64,256]{1,0:T(8,128)S(1)}, u32[]{:S(2)}, u32[]{:S(2)}) collective-permute-start(f32[64,256]{1,0:T(8,128)S(1)} %send.7), channel_id=1, source_target_pairs={{0,1},{1,0},{2,3},{3,2},{4,5},{5,4},{6,7},{7,6},{8,9},{9,8},{10,11... | collective-permute-start | bytes 196616 | tf_op jit(solution)/shard_map/ppermute | solution.py:397
  161.0 6.8 %collective-permute-start.9 = (bf16[128,128]{1,0:T(8,128)(2,1)S(1)}, bf16[128,128]{1,0:T(8,128)(2,1)S(1)}, u32[]{:S(2)}, u32[]{:S(2)}) collective-permute-start(bf16[128,128]{1,0:T(8,128)(2,1)S(1)} %get-tuple-element.73), channel_id=1, source_target_pairs={{0,32},{32,64},{64,96},{1,33},{33,65},{65,97},{2,34},{34,66},{66,9... | collective-permute-start | bytes 98312 | tf_op jit(solution)/shard_map/ppermute | solution.py:437
  179.9 5.0 %collective-permute-start.10 = (bf16[16,128,128]{2,1,0:T(8,128)(2,1)S(1)}, bf16[16,128,128]{2,1,0:T(8,128)(2,1)S(1)}, u32[]{:S(2)}, u32[]{:S(2)}) collective-permute-start(bf16[16,128,128]{2,1,0:T(8,128)(2,1)S(1)} %all_to_all.56.part_ref), channel_id=1, source_target_pairs={{0,1},{1,0},{2,3},{3,2},{4,5},{5,4},{6,7},{7,6},{8,9},{9,8},{10,11... | collective-permute-start | bytes 1572872 | tf_op jit(solution)/shard_map/ppermute | solution.py:397
  206.4 3.1 %collective-permute-start.11 = (f32[64,256]{1,0:T(8,128)S(1)}, f32[64,256]{1,0:T(8,128)S(1)}, u32[]{:S(2)}, u32[]{:S(2)}) collective-permute-start(f32[64,256]{1,0:T(8,128)S(1)} %send.8), channel_id=1, source_target_pairs={{0,1},{1,0},{2,3},{3,2},{4,5},{5,4},{6,7},{7,6},{8,9},{9,8},{10,11... | collective-permute-start | bytes 196616 | tf_op jit(solution)/shard_map/ppermute | solution.py:397
  210.3 6.8 %collective-permute-start.12 = (bf16[128,128]{1,0:T(8,128)(2,1)S(1)}, bf16[128,128]{1,0:T(8,128)(2,1)S(1)}, u32[]{:S(2)}, u32[]{:S(2)}) collective-permute-start(bf16[128,128]{1,0:T(8,128)(2,1)S(1)} %get-tuple-element.77), channel_id=1, source_target_pairs={{0,32},{32,64},{64,96},{1,33},{33,65},{65,97},{2,34},{34,66},{66,9... | collective-permute-start | bytes 98312 | tf_op jit(solution)/shard_map/ppermute | solution.py:437
  229.2 5.0 %collective-permute-start.13 = (bf16[16,128,128]{2,1,0:T(8,128)(2,1)S(1)}, bf16[16,128,128]{2,1,0:T(8,128)(2,1)S(1)}, u32[]{:S(2)}, u32[]{:S(2)}) collective-permute-start(bf16[16,128,128]{2,1,0:T(8,128)(2,1)S(1)} %all_to_all.58.part_ref), channel_id=1, source_target_pairs={{0,1},{1,0},{2,3},{3,2},{4,5},{5,4},{6,7},{7,6},{8,9},{9,8},{10,11... | collective-permute-start | bytes 1572872 | tf_op jit(solution)/shard_map/ppermute | solution.py:397
  255.7 3.0 %collective-permute-start.14 = (f32[64,256]{1,0:T(8,128)S(1)}, f32[64,256]{1,0:T(8,128)S(1)}, u32[]{:S(2)}, u32[]{:S(2)}) collective-permute-start(f32[64,256]{1,0:T(8,128)S(1)} %send.9), channel_id=1, source_target_pairs={{0,1},{1,0},{2,3},{3,2},{4,5},{5,4},{6,7},{7,6},{8,9},{9,8},{10,11... | collective-permute-start | bytes 196616 | tf_op jit(solution)/shard_map/ppermute | solution.py:397

commit v4 on v3

--- a/solution.py
+++ b/solution.py
@@ -151,15 +151,14 @@
 
 
 def in_goals(index):
-    device = index // 4
-    row = ((device % 2) * CHIPS + device // 2) * 128 + (index % 4) * 32
+    row = (((index >> 2) & 1) * CHIPS + (index >> 3)) * 128 + (index & 3) * 32
     return jnp.where(index >= 0, row, GU_ROWS)
 
 
 def out_goals(index, core):
-    device = index // 7
-    row = device // 2 * 256 + (index % 7) * 32
-    near = (device % 2) == core
+    device = lax.div(index, jnp.int32(7))
+    row = (device >> 1) * 256 + (index - device * 7) * 32
+    near = (device & 1) == core
     trash = DN_ROWS // 2
     return jnp.concatenate(
         [
@@ -254,8 +253,7 @@
     next_ref[...] = jnp.concatenate([ordered[:, :128], ordered[:, 128:]], axis=0)
 
 
-def prepare_kernel(x_ref, norm_ref, order_ref, *refs):
-    firsts, gain_ref, rows_ref = refs[:-2], refs[-2], refs[-1]
+def gain_kernel(norm_ref, order_ref, gain_ref, rows_ref):
     for device in range(2 * CHIPS):
         rows_ref[device : device + 1, :] = norm_ref[:, device * 256 : (device + 1) * 256]
     left = rows_ref[...]
@@ -268,12 +266,26 @@
         at = 2 * (device % 2 * CHIPS + device // 2)
         for p in range(2):
             gain_ref[at + p : at + p + 1, :] = gain[device : device + 1, p * 128 : (p + 1) * 128]
+
+
+def prepare_kernel(x_ref, order_ref, *firsts):
     ordered = jnp.dot(x_ref[...], order_ref[...], preferred_element_type=jnp.float32).astype(jnp.bfloat16)
     for group, ref in enumerate(firsts):
         part = ordered[group * ROWS : (group + 1) * ROWS]
         ref[...] = jnp.concatenate([part[:, :128], part[:, 128:]], axis=0)
 
 
+def line_kernel(at_ref, *refs):
+    for shift, ref in enumerate(refs[:4]):
+        refs[-1][(at_ref[0] - shift) & 3] = ref[...]
+
+
+def plane_kernel(at_ref, *refs):
+    for shift, ref in enumerate(refs[:4]):
+        for line in range(4):
+            refs[-1][line * 4 + ((at_ref[0] - shift) & 3)] = ref[line]
+
+
 def pick_kernel(place_ref, *refs):
     made, out_ref = refs[:-1], refs[-1]
     groups = out_ref.shape[0] // ROWS
@@ -297,18 +309,51 @@
     return pl.CostEstimate(flops=2 * 128 * products, bytes_accessed=2 * MIB, transcendentals=0)
 
 
-def prepare(x_in, norm_gain, x_order):
+def prepare(x_in, x_order):
     groups = x_in.shape[0] // ROWS
     return pl.pallas_call(
         prepare_kernel,
-        out_shape=[jax.ShapeDtypeStruct((2 * ROWS, 128), jnp.bfloat16)] * groups
-        + [jax.ShapeDtypeStruct((4 * CHIPS, 128), jnp.float32)],
-        in_specs=[VMEM] * 3,
-        out_specs=[VMEM] * (groups + 1),
+        out_shape=[jax.ShapeDtypeStruct((2 * ROWS, 128), jnp.bfloat16)] * groups,
+        in_specs=[VMEM] * 2,
+        out_specs=[VMEM] * groups,
+        compiler_params=pltpu.CompilerParams(vmem_limit_bytes=4 * MIB),
+        name="prepare",
+    )(x_in, x_order)
+
+
+def gains_of(norm_gain, x_order):
+    return pl.pallas_call(
+        gain_kernel,
+        out_shape=jax.ShapeDtypeStruct((4 * CHIPS, 128), jnp.float32),
+        in_specs=[VMEM] * 2,
+        out_specs=VMEM,
         scratch_shapes=[pltpu.VMEM((2 * CHIPS, 256), jnp.float32)],
+        compiler_params=pltpu.CompilerParams(vmem_limit_bytes=4 * MIB),
+        name="gains",
+    )(norm_gain, x_order)
+
+
+def placed_by(kernel, at, parts, count):
+    return pl.pallas_call(
+        kernel,
+        out_shape=jax.ShapeDtypeStruct((count,) + parts[0].shape[-2:], parts[0].dtype),
+        in_specs=[SMEM] + [VMEM] * len(parts),
+        out_specs=VMEM,
         compiler_params=pltpu.CompilerParams(vmem_limit_bytes=8 * MIB),
-        name="prepare",
-    )(x_in, norm_gain, x_order)
+        name="placed",
+    )(at, *parts)
+
+
+def shifted_all(value, along_x):
+    parts = [value]
+    for shift in range(1, 4):
+        pairs = []
+        for x in range(4):
+            for y in range(4):
+                goal = ((x + shift) % 4 * 4 + y) if along_x else (x * 4 + (y + shift) % 4)
+                pairs += [(2 * (x * 4 + y) + core, 2 * goal + core) for core in range(2)]
+        parts.append(lax.ppermute(value, "tensor", pairs))
+    return parts
 
 
 def call_near(core, part, gain, weight):
@@ -400,19 +445,21 @@
 def local(x_in, norm_gain, in_index, gate_blocks, up_blocks, out_index, down_blocks):
     segment_count = lax.axis_size("segment")
     segment_at = lax.axis_index("segment")
-    core = (lax.axis_index("tensor") % 2).astype(jnp.int32)[None]
+    tensor_at = lax.axis_index("tensor").astype(jnp.int32)
+    core = (tensor_at & 1)[None]
     tokens = x_in.shape[0]
     group_count = tokens // ROWS
     tick_count = group_count + segment_count - 1
     x_order, h_order = orders()
     x_back = x_order.T
-    *firsts, gain = prepare(x_in, norm_gain, x_order)
+    firsts = prepare(x_in, x_order)
     is_first = jnp.broadcast_to(segment_at == 0, (8, 128)).astype(jnp.bfloat16)
     place = segment_at.astype(jnp.int32)[None]
-    to_wide, to_down = in_goals(in_index[0]), out_goals(out_index[0], core[0])
-    to_wide, to_down, core, place, x_order, x_back, h_order, gain, firsts, is_first = lax.optimization_barrier(
-        (to_wide, to_down, core, place, x_order, x_back, h_order, gain, firsts, is_first)
+    x_at, y_at = (tensor_at >> 3)[None], ((tensor_at >> 1) & 3)[None]
+    core, place, x_at, y_at, x_order, x_back, h_order, firsts, is_first = lax.optimization_barrier(
+        (core, place, x_at, y_at, x_order, x_back, h_order, firsts, is_first)
     )
+
     carried = None
     made = []
     hops = [(i, i + 1) for i in range(segment_count - 1)]
@@ -420,15 +467,24 @@
         taken = firsts[min(tick, group_count - 1)]
         if carried is not None:
             taken = jnp.where(jnp.tile(is_first, (2 * ROWS // 8, 1)) > 0, taken, carried)
-        mine = exchanged(jnp.broadcast_to(taken[None], (CHIPS, 2 * ROWS, 128)))
         if tick == 0:
-            mine, to_wide, to_down = lax.optimization_barrier((mine, to_wide, to_down))
-            wide = densify_wide(to_wide, gate_blocks[0], up_blocks[0])
-            down, lent = densify_down(to_down, down_blocks[0])
-            borrowed = swapped(lent)
+            parts = shifted_all(taken, True)
+            out_now, norm_gain, core = lax.optimization_barrier((out_index[0], norm_gain, core))
+            gain = gains_of(norm_gain, x_order)
+            down, lent = densify_down(out_goals(out_now, core[0]), down_blocks[0])
+            line = placed_by(line_kernel, x_at, parts + [resident(down)], 4)
+            in_now, line = lax.optimization_barrier((in_index[0], line))
+            parts = shifted_all(line, False)
+            wide = densify_wide(in_goals(in_now), gate_blocks[0], up_blocks[0])
+            mine = placed_by(plane_kernel, y_at, parts + [resident(wide)], CHIPS)
+        else:
+            mine = exchanged(jnp.broadcast_to(taken[None], (CHIPS, 2 * ROWS, 128)))
         other = swapped(mine)
         acc, square = call_near(core, mine, gain, wide)
         hidden = call_far(core, other, gain, wide, h_order, acc, square)
+        if tick == 0:
+            hidden, lent = lax.optimization_barrier((hidden, lent))
+            borrowed = swapped(lent)
         mine = exchanged(hidden)
         got = swapped(call_send(mine, borrowed))
         produced, ordered = call_keep(mine, down, got, taken, x_order, x_back)

time: 262 us -> 255 us (0.973)
  blocking collectives: 160 us -> 144 us
  starting transfers between devices: 50.2 us -> 58 us
    all_to_all x10 -> x9, blocking collectives: 160 us -> 144 us  [exchanged(): return lax.all_to_all(value, 'tensor', 0, 0, axis_index_groups=same_core)]
    ppermute x0 -> x6, starting transfers between devices: none -> 7.53 us  [shifted_all(): parts.append(lax.ppermute(value, 'tensor', pairs))]
  transfers between devices with their start and end apart: 15 -> 21, of which waited for: 13 -> 15; matrix products, arithmetic and copies ran while one was open for 0% -> 1% of each run, Pallas kernels for 6% -> 7%
where the time goes in v4:
time: 255 us; the launch traced here: 254 us
  blocking collectives  144 us (56%)
  starting transfers between devices  58 us (23%)
  Pallas kernels  37.4 us (15%)
  waiting for transfers between devices  10.6 us (4%)
    all_to_all x9, blocking collectives, exchanged(): return lax.all_to_all(value, 'tensor', 0, 0, axis_index_groups=same_core)  144 us
    ppermute x11, starting transfers between devices, swapped(): return lax.ppermute(value, 'tensor', [(i, i ^ 1) for i in range(2 * CHIPS)])  27 us
    ppermute x4, starting transfers between devices, local(): carried = lax.ppermute(ordered, 'segment', hops)  23.4 us
    pallas_call x2, Pallas kernels, pack(): pl.pallas_call(kernel, out_shape=[pltpu.VMEM(shape, jnp.bfloat16)] * resu...  12.4 us
    pallas_call x5, Pallas kernels, call_far(): pl.pallas_call(far_kernel, out_shape=jax.ShapeDtypeStruct((CHIPS, 2 * ROW...  8.76 us
    ppermute x6, starting transfers between devices, shifted_all(): parts.append(lax.ppermute(value, 'tensor', pairs))  7.53 us
    pallas_call x5, Pallas kernels, call_near(): pl.pallas_call(near_kernel, out_shape=(jax.ShapeDtypeStruct((2 * ROWS, GU...  6.21 us
    ppermute x11, waiting for transfers between devices, swapped(): return lax.ppermute(value, 'tensor', [(i, i ^ 1) for i in range(2 * CHIPS)])  5.78 us
  transfers between devices with their start and end apart: 21, of which 15 were waited for; matrix products, arithmetic and copies ran while one was open for 1% of the time, Pallas kernels for 7%

profile of v4, /device:TPU:65, one launch (start us, length us, event | category | flops | bytes accessed | tf_op | source)
XLA Modules:
  0.0 254.4 jit_solution(4564248085083106659)
XLA Ops:
  1.3 2.6 %collective-permute-start.2 = (bf16[128,128]{1,0:T(8,128)(2,1)S(1)}, bf16[128,128]{1,0:T(8,128)(2,1)S(1)}, u32[]{:S(2)}, u32[]{:S(2)}) collective-permute-start(bf16[128,128]{1,0:T(8,128)(2,1)S(1)} %get-tuple-element.52.refs_0_.taken_ref), channel_id=1, source_target_pairs={{0,24},{1,25},{2,26},{3,27},{4,28},{5,29},{6,30},{7,31},{8,0},{9,1... | collective-permute-start | bytes 98312 | tf_op jit(solution)/shard_map/ppermute | solution.py:355
  7.1 5.5 %pack_down.1 = (bf16[4128,512]{1,0:T(8,128)(2,1)S(1)}, bf16[4128,512]{1,0:T(8,128)(2,1)S(1)}) custom-call(s32[8,126]{1,0:T(8,128)S(1)} %pad_add_fusion.goal_ref, bf16[126,4,4096]{2,1,0:T(4,128)(2,1)} %bitcast.20), custom_call_target="tpu_custom_call" | custom-call | bytes 41943040 | tf_op jit(solution)/shard_map/pack_down/pallas_call | solution.py:120
  12.7 2.8 %collective-permute-start.5 = (bf16[4,128,128]{2,1,0:T(8,128)(2,1)S(1)}, bf16[4,128,128]{2,1,0:T(8,128)(2,1)S(1)}, u32[]{:S(2)}, u32[]{:S(2)}) collective-permute-start(bf16[4,128,128]{2,1,0:T(8,128)(2,1)S(1)} %placed.2.refs_0_), channel_id=1, source_target_pairs={{0,6},{1,7},{2,0},{3,1},{4,2},{5,3},{6,4},{7,5},{8,14},{9,15},{10,... | collective-permute-start | bytes 393224 | tf_op jit(solution)/shard_map/ppermute | solution.py:355
  16.5 6.9 %pack_wide.1.refs_4_.weight_ref = bf16[4128,1792]{1,0:T(8,128)(2,1)S(1)} custom-call(s32[7,72]{1,0:T(8,128)S(1)} %add_select_fusion.goal_ref, bf16[7,72,4096]{2,1,0:T(8,128)(2,1)} %bitcast.21, bf16[7,72,4096]{2,1,0:T(8,128)(2,1)} %bitcast.22), custom_call_target="tpu_custom_call" | custom-call | bytes 41943040 | tf_op jit(solution)/shard_map/pack_wide/pallas_call | solution.py:120
  24.3 1.6 collective-permute-start.6
  27.5 1.7 far.5
  29.8 20.7 %all_to_all.45.part_ref = bf16[16,128,256]{2,1,0:T(8,128)(2,1)S(1)} all-to-all(bf16[16,128,256]{2,1,0:T(8,128)(2,1)S(1)} %far.5), channel_id=1, replica_groups={{0,2,4,6,8,10,12,14,16,18,20,22,24,26,28,30},{1,3,5,7,9,11,13,15,17,19,..., dimensions={0} | all-to-all | bytes 2097152 | tf_op jit(solution)/shard_map/all_to_all | solution.py:438
  51.3 2.4 collective-permute-start.8
  55.5 6.1 %collective-permute-start.9 = (bf16[128,128]{1,0:T(8,128)(2,1)S(1)}, bf16[128,128]{1,0:T(8,128)(2,1)S(1)}, u32[]{:S(2)}, u32[]{:S(2)}) collective-permute-start(bf16[128,128]{1,0:T(8,128)(2,1)S(1)} %get-tuple-element.69), channel_id=1, source_target_pairs={{0,32},{32,64},{64,96},{1,33},{33,65},{65,97},{2,34},{34,66},{66,9... | collective-permute-start | bytes 98312 | tf_op jit(solution)/shard_map/ppermute | solution.py:493
  62.8 12.0 %all_to_all.46.part_ref = bf16[16,128,128]{2,1,0:T(8,128)(2,1)S(1)} all-to-all(bf16[16,128,128]{2,1,0:T(8,128)(2,1)S(1)} %broadcast_in_dim.62), channel_id=1, replica_groups={{0,2,4,6,8,10,12,14,16,18,20,22,24,26,28,30},{1,3,5,7,9,11,13,15,17,19,..., dimensions={0} | all-to-all | bytes 1048576 | tf_op jit(solution)/shard_map/all_to_all | solution.py:438
  74.7 3.4 %collective-permute-start.10 = (bf16[16,128,128]{2,1,0:T(8,128)(2,1)S(1)}, bf16[16,128,128]{2,1,0:T(8,128)(2,1)S(1)}, u32[]{:S(2)}, u32[]{:S(2)}) collective-permute-start(bf16[16,128,128]{2,1,0:T(8,128)(2,1)S(1)} %all_to_all.46.part_ref), channel_id=1, source_target_pairs={{0,1},{1,0},{2,3},{3,2},{4,5},{5,4},{6,7},{7,6},{8,9},{9,8},{10,11... | collective-permute-start | bytes 1572872 | tf_op jit(solution)/shard_map/ppermute | solution.py:442
  79.7 1.8 far.6
  81.5 18.9 %all_to_all.47.part_ref = bf16[16,128,256]{2,1,0:T(8,128)(2,1)S(1)} all-to-all(bf16[16,128,256]{2,1,0:T(8,128)(2,1)S(1)} %far.6), channel_id=1, replica_groups={{0,2,4,6,8,10,12,14,16,18,20,22,24,26,28,30},{1,3,5,7,9,11,13,15,17,19,..., dimensions={0} | all-to-all | bytes 2097152 | tf_op jit(solution)/shard_map/all_to_all | solution.py:438
  101.2 2.2 collective-permute-start.11
  105.2 5.8 %collective-permute-start.12 = (bf16[128,128]{1,0:T(8,128)(2,1)S(1)}, bf16[128,128]{1,0:T(8,128)(2,1)S(1)}, u32[]{:S(2)}, u32[]{:S(2)}) collective-permute-start(bf16[128,128]{1,0:T(8,128)(2,1)S(1)} %get-tuple-element.73), channel_id=1, source_target_pairs={{0,32},{32,64},{64,96},{1,33},{33,65},{65,97},{2,34},{34,66},{66,9... | collective-permute-start | bytes 98312 | tf_op jit(solution)/shard_map/ppermute | solution.py:493
  112.1 12.0 %all_to_all.48.part_ref = bf16[16,128,128]{2,1,0:T(8,128)(2,1)S(1)} all-to-all(bf16[16,128,128]{2,1,0:T(8,128)(2,1)S(1)} %broadcast_in_dim.63), channel_id=1, replica_groups={{0,2,4,6,8,10,12,14,16,18,20,22,24,26,28,30},{1,3,5,7,9,11,13,15,17,19,..., dimensions={0} | all-to-all | bytes 1048576 | tf_op jit(solution)/shard_map/all_to_all | solution.py:438
  124.0 3.4 %collective-permute-start.13 = (bf16[16,128,128]{2,1,0:T(8,128)(2,1)S(1)}, bf16[16,128,128]{2,1,0:T(8,128)(2,1)S(1)}, u32[]{:S(2)}, u32[]{:S(2)}) collective-permute-start(bf16[16,128,128]{2,1,0:T(8,128)(2,1)S(1)} %all_to_all.48.part_ref), channel_id=1, source_target_pairs={{0,1},{1,0},{2,3},{3,2},{4,5},{5,4},{6,7},{7,6},{8,9},{9,8},{10,11... | collective-permute-start | bytes 1572872 | tf_op jit(solution)/shard_map/ppermute | solution.py:442
  129.0 1.8 far.7
  130.8 19.0 %all_to_all.49.part_ref = bf16[16,128,256]{2,1,0:T(8,128)(2,1)S(1)} all-to-all(bf16[16,128,256]{2,1,0:T(8,128)(2,1)S(1)} %far.7), channel_id=1, replica_groups={{0,2,4,6,8,10,12,14,16,18,20,22,24,26,28,30},{1,3,5,7,9,11,13,15,17,19,..., dimensions={0} | all-to-all | bytes 2097152 | tf_op jit(solution)/shard_map/all_to_all | solution.py:438
  150.5 2.2 collective-permute-start.14
  154.5 5.8 %collective-permute-start.15 = (bf16[128,128]{1,0:T(8,128)(2,1)S(1)}, bf16[128,128]{1,0:T(8,128)(2,1)S(1)}, u32[]{:S(2)}, u32[]{:S(2)}) collective-permute-start(bf16[128,128]{1,0:T(8,128)(2,1)S(1)} %get-tuple-element.77), channel_id=1, source_target_pairs={{0,32},{32,64},{64,96},{1,33},{33,65},{65,97},{2,34},{34,66},{66,9... | collective-permute-start | bytes 98312 | tf_op jit(solution)/shard_map/ppermute | solution.py:493
  161.4 12.0 %all_to_all.50.part_ref = bf16[16,128,128]{2,1,0:T(8,128)(2,1)S(1)} all-to-all(bf16[16,128,128]{2,1,0:T(8,128)(2,1)S(1)} %broadcast_in_dim.64), channel_id=1, replica_groups={{0,2,4,6,8,10,12,14,16,18,20,22,24,26,28,30},{1,3,5,7,9,11,13,15,17,19,..., dimensions={0} | all-to-all | bytes 1048576 | tf_op jit(solution)/shard_map/all_to_all | solution.py:438
  173.4 3.4 %collective-permute-start.16 = (bf16[16,128,128]{2,1,0:T(8,128)(2,1)S(1)}, bf16[16,128,128]{2,1,0:T(8,128)(2,1)S(1)}, u32[]{:S(2)}, u32[]{:S(2)}) collective-permute-start(bf16[16,128,128]{2,1,0:T(8,128)(2,1)S(1)} %all_to_all.50.part_ref), channel_id=1, source_target_pairs={{0,1},{1,0},{2,3},{3,2},{4,5},{5,4},{6,7},{7,6},{8,9},{9,8},{10,11... | collective-permute-start | bytes 1572872 | tf_op jit(solution)/shard_map/ppermute | solution.py:442
  178.3 1.8 far.8
  180.1 19.0 %all_to_all.51.part_ref = bf16[16,128,256]{2,1,0:T(8,128)(2,1)S(1)} all-to-all(bf16[16,128,256]{2,1,0:T(8,128)(2,1)S(1)} %far.8), channel_id=1, replica_groups={{0,2,4,6,8,10,12,14,16,18,20,22,24,26,28,30},{1,3,5,7,9,11,13,15,17,19,..., dimensions={0} | all-to-all | bytes 2097152 | tf_op jit(solution)/shard_map/all_to_all | solution.py:438
  199.9 2.1 collective-permute-start.17
  203.8 5.8 %collective-permute-start.18 = (bf16[128,128]{1,0:T(8,128)(2,1)S(1)}, bf16[128,128]{1,0:T(8,128)(2,1)S(1)}, u32[]{:S(2)}, u32[]{:S(2)}) collective-permute-start(bf16[128,128]{1,0:T(8,128)(2,1)S(1)} %get-tuple-element.81), channel_id=1, source_target_pairs={{0,32},{32,64},{64,96},{1,33},{33,65},{65,97},{2,34},{34,66},{66,9... | collective-permute-start | bytes 98312 | tf_op jit(solution)/shard_map/ppermute | solution.py:493
  210.7 12.0 %all_to_all.52.part_ref = bf16[16,128,128]{2,1,0:T(8,128)(2,1)S(1)} all-to-all(bf16[16,128,128]{2,1,0:T(8,128)(2,1)S(1)} %broadcast_in_dim.65), channel_id=1, replica_groups={{0,2,4,6,8,10,12,14,16,18,20,22,24,26,28,30},{1,3,5,7,9,11,13,15,17,19,..., dimensions={0} | all-to-all | bytes 1048576 | tf_op jit(solution)/shard_map/all_to_all | solution.py:438
  222.7 3.4 %collective-permute-start.19 = (bf16[16,128,128]{2,1,0:T(8,128)(2,1)S(1)}, bf16[16,128,128]{2,1,0:T(8,128)(2,1)S(1)}, u32[]{:S(2)}, u32[]{:S(2)}) collective-permute-start(bf16[16,128,128]{2,1,0:T(8,128)(2,1)S(1)} %all_to_all.52.part_ref), channel_id=1, source_target_pairs={{0,1},{1,0},{2,3},{3,2},{4,5},{5,4},{6,7},{7,6},{8,9},{9,8},{10,11... | collective-permute-start | bytes 1572872 | tf_op jit(solution)/shard_map/ppermute | solution.py:442
  227.6 1.8 far.9
  229.4 19.0 %all_to_all.53.part_ref = bf16[16,128,256]{2,1,0:T(8,128)(2,1)S(1)} all-to-all(bf16[16,128,256]{2,1,0:T(8,128)(2,1)S(1)} %far.9), channel_id=1, replica_groups={{0,2,4,6,8,10,12,14,16,18,20,22,24,26,28,30},{1,3,5,7,9,11,13,15,17,19,..., dimensions={0} | all-to-all | bytes 2097152 | tf_op jit(solution)/shard_map/all_to_all | solution.py:438
  249.1 2.2 collective-permute-start.20
  (69 shorter events, 33.2 us)
Async XLA Ops:
  0.3 0.8 copy-start
  1.3 11.3 %collective-permute-start.2 = (bf16[128,128]{1,0:T(8,128)(2,1)S(1)}, bf16[128,128]{1,0:T(8,128)(2,1)S(1)}, u32[]{:S(2)}, u32[]{:S(2)}) collective-permute-start(bf16[128,128]{1,0:T(8,128)(2,1)S(1)} %get-tuple-element.52.refs_0_.taken_ref), channel_id=1, source_target_pairs={{0,24},{1,25},{2,26},{3,27},{4,28},{5,29},{6,30},{7,31},{8,0},{9,1... | collective-permute-start | bytes 98312 | tf_op jit(solution)/shard_map/ppermute | solution.py:355
  3.9 8.7 %collective-permute-start.1 = (bf16[128,128]{1,0:T(8,128)(2,1)S(1)}, bf16[128,128]{1,0:T(8,128)(2,1)S(1)}, u32[]{:S(2)}, u32[]{:S(2)}) collective-permute-start(bf16[128,128]{1,0:T(8,128)(2,1)S(1)} %get-tuple-element.52.refs_0_.taken_ref), channel_id=1, source_target_pairs={{0,16},{1,17},{2,18},{3,19},{4,20},{5,21},{6,22},{7,23},{8,24},{9,... | collective-permute-start | bytes 98312 | tf_op jit(solution)/shard_map/ppermute | solution.py:355
  4.4 8.2 %collective-permute-start = (bf16[128,128]{1,0:T(8,128)(2,1)S(1)}, bf16[128,128]{1,0:T(8,128)(2,1)S(1)}, u32[]{:S(2)}, u32[]{:S(2)}) collective-permute-start(bf16[128,128]{1,0:T(8,128)(2,1)S(1)} %get-tuple-element.52.refs_0_.taken_ref), channel_id=1, source_target_pairs={{0,8},{1,9},{2,10},{3,11},{4,12},{5,13},{6,14},{7,15},{8,16},{9,17... | collective-permute-start | bytes 98312 | tf_op jit(solution)/shard_map/ppermute | solution.py:355
  12.7 10.8 %collective-permute-start.5 = (bf16[4,128,128]{2,1,0:T(8,128)(2,1)S(1)}, bf16[4,128,128]{2,1,0:T(8,128)(2,1)S(1)}, u32[]{:S(2)}, u32[]{:S(2)}) collective-permute-start(bf16[4,128,128]{2,1,0:T(8,128)(2,1)S(1)} %placed.2.refs_0_), channel_id=1, source_target_pairs={{0,6},{1,7},{2,0},{3,1},{4,2},{5,3},{6,4},{7,5},{8,14},{9,15},{10,... | collective-permute-start | bytes 393224 | tf_op jit(solution)/shard_map/ppermute | solution.py:355
  15.5 8.0 %collective-permute-start.4 = (bf16[4,128,128]{2,1,0:T(8,128)(2,1)S(1)}, bf16[4,128,128]{2,1,0:T(8,128)(2,1)S(1)}, u32[]{:S(2)}, u32[]{:S(2)}) collective-permute-start(bf16[4,128,128]{2,1,0:T(8,128)(2,1)S(1)} %placed.2.refs_0_), channel_id=1, source_target_pairs={{0,4},{1,5},{2,6},{3,7},{4,0},{5,1},{6,2},{7,3},{8,12},{9,13},{10,... | collective-permute-start | bytes 393224 | tf_op jit(solution)/shard_map/ppermute | solution.py:355
  15.8 8.5 %collective-permute-start.3 = (bf16[4,128,128]{2,1,0:T(8,128)(2,1)S(1)}, bf16[4,128,128]{2,1,0:T(8,128)(2,1)S(1)}, u32[]{:S(2)}, u32[]{:S(2)}) collective-permute-start(bf16[4,128,128]{2,1,0:T(8,128)(2,1)S(1)} %placed.2.refs_0_), channel_id=1, source_target_pairs={{0,2},{1,3},{2,4},{3,5},{4,6},{5,7},{6,0},{7,1},{8,10},{9,11},{10,... | collective-permute-start | bytes 393224 | tf_op jit(solution)/shard_map/ppermute | solution.py:355
  23.4 2.5 copy-start.1
  24.3 3.2 %collective-permute-start.6 = (bf16[16,128,128]{2,1,0:T(8,128)(2,1)S(1)}, bf16[16,128,128]{2,1,0:T(8,128)(2,1)S(1)}, u32[]{:S(2)}, u32[]{:S(2)}) collective-permute-start(bf16[16,128,128]{2,1,0:T(8,128)(2,1)S(1)} %placed.3.part_ref), channel_id=1, source_target_pairs={{0,1},{1,0},{2,3},{3,2},{4,5},{5,4},{6,7},{7,6},{8,9},{9,8},{10,11... | collective-permute-start | bytes 1572872 | tf_op jit(solution)/shard_map/ppermute | solution.py:442
  29.2 21.3 %collective-permute-start.7 = (bf16[4128,512]{1,0:T(8,128)(2,1)S(1)}, bf16[4128,512]{1,0:T(8,128)(2,1)S(1)}, u32[]{:S(2)}, u32[]{:S(2)}) collective-permute-start(bf16[4128,512]{1,0:T(8,128)(2,1)S(1)} %get-tuple-element.64), channel_id=1, source_target_pairs={{0,1},{1,0},{2,3},{3,2},{4,5},{5,4},{6,7},{7,6},{8,9},{9,8},{10,11... | collective-permute-start | bytes 12681224 | tf_op jit(solution)/shard_map/ppermute | solution.py:442
  51.3 3.3 %collective-permute-start.8 = (f32[64,256]{1,0:T(8,128)S(1)}, f32[64,256]{1,0:T(8,128)S(1)}, u32[]{:S(2)}, u32[]{:S(2)}) collective-permute-start(f32[64,256]{1,0:T(8,128)S(1)} %send.5), channel_id=1, source_target_pairs={{0,1},{1,0},{2,3},{3,2},{4,5},{5,4},{6,7},{7,6},{8,9},{9,8},{10,11... | collective-permute-start | bytes 196616 | tf_op jit(solution)/shard_map/ppermute | solution.py:442
  55.5 7.1 %collective-permute-start.9 = (bf16[128,128]{1,0:T(8,128)(2,1)S(1)}, bf16[128,128]{1,0:T(8,128)(2,1)S(1)}, u32[]{:S(2)}, u32[]{:S(2)}) collective-permute-start(bf16[128,128]{1,0:T(8,128)(2,1)S(1)} %get-tuple-element.69), channel_id=1, source_target_pairs={{0,32},{32,64},{64,96},{1,33},{33,65},{65,97},{2,34},{34,66},{66,9... | collective-permute-start | bytes 98312 | tf_op jit(solution)/shard_map/ppermute | solution.py:493
  74.7 5.0 %collective-permute-start.10 = (bf16[16,128,128]{2,1,0:T(8,128)(2,1)S(1)}, bf16[16,128,128]{2,1,0:T(8,128)(2,1)S(1)}, u32[]{:S(2)}, u32[]{:S(2)}) collective-permute-start(bf16[16,128,128]{2,1,0:T(8,128)(2,1)S(1)} %all_to_all.46.part_ref), channel_id=1, source_target_pairs={{0,1},{1,0},{2,3},{3,2},{4,5},{5,4},{6,7},{7,6},{8,9},{9,8},{10,11... | collective-permute-start | bytes 1572872 | tf_op jit(solution)/shard_map/ppermute | solution.py:442
  101.2 3.1 %collective-permute-start.11 = (f32[64,256]{1,0:T(8,128)S(1)}, f32[64,256]{1,0:T(8,128)S(1)}, u32[]{:S(2)}, u32[]{:S(2)}) collective-permute-start(f32[64,256]{1,0:T(8,128)S(1)} %send.6), channel_id=1, source_target_pairs={{0,1},{1,0},{2,3},{3,2},{4,5},{5,4},{6,7},{7,6},{8,9},{9,8},{10,11... | collective-permute-start | bytes 196616 | tf_op jit(solution)/shard_map/ppermute | solution.py:442
  105.2 6.8 %collective-permute-start.12 = (bf16[128,128]{1,0:T(8,128)(2,1)S(1)}, bf16[128,128]{1,0:T(8,128)(2,1)S(1)}, u32[]{:S(2)}, u32[]{:S(2)}) collective-permute-start(bf16[128,128]{1,0:T(8,128)(2,1)S(1)} %get-tuple-element.73), channel_id=1, source_target_pairs={{0,32},{32,64},{64,96},{1,33},{33,65},{65,97},{2,34},{34,66},{66,9... | collective-permute-start | bytes 98312 | tf_op jit(solution)/shard_map/ppermute | solution.py:493
  124.0 5.0 %collective-permute-start.13 = (bf16[16,128,128]{2,1,0:T(8,128)(2,1)S(1)}, bf16[16,128,128]{2,1,0:T(8,128)(2,1)S(1)}, u32[]{:S(2)}, u32[]{:S(2)}) collective-permute-start(bf16[16,128,128]{2,1,0:T(8,128)(2,1)S(1)} %all_to_all.48.part_ref), channel_id=1, source_target_pairs={{0,1},{1,0},{2,3},{3,2},{4,5},{5,4},{6,7},{7,6},{8,9},{9,8},{10,11... | collective-permute-start | bytes 1572872 | tf_op jit(solution)/shard_map/ppermute | solution.py:442
  150.5 3.1 %collective-permute-start.14 = (f32[64,256]{1,0:T(8,128)S(1)}, f32[64,256]{1,0:T(8,128)S(1)}, u32[]{:S(2)}, u32[]{:S(2)}) collective-permute-start(f32[64,256]{1,0:T(8,128)S(1)} %send.7), channel_id=1, source_target_pairs={{0,1},{1,0},{2,3},{3,2},{4,5},{5,4},{6,7},{7,6},{8,9},{9,8},{10,11... | collective-permute-start | bytes 196616 | tf_op jit(solution)/shard_map/ppermute | solution.py:442
  154.5 6.8 %collective-permute-start.15 = (bf16[128,128]{1,0:T(8,128)(2,1)S(1)}, bf16[128,128]{1,0:T(8,128)(2,1)S(1)}, u32[]{:S(2)}, u32[]{:S(2)}) collective-permute-start(bf16[128,128]{1,0:T(8,128)(2,1)S(1)} %get-tuple-element.77), channel_id=1, source_target_pairs={{0,32},{32,64},{64,96},{1,33},{33,65},{65,97},{2,34},{34,66},{66,9... | collective-permute-start | bytes 98312 | tf_op jit(solution)/shard_map/ppermute | solution.py:493
  173.4 5.0 %collective-permute-start.16 = (bf16[16,128,128]{2,1,0:T(8,128)(2,1)S(1)}, bf16[16,128,128]{2,1,0:T(8,128)(2,1)S(1)}, u32[]{:S(2)}, u32[]{:S(2)}) collective-permute-start(bf16[16,128,128]{2,1,0:T(8,128)(2,1)S(1)} %all_to_all.50.part_ref), channel_id=1, source_target_pairs={{0,1},{1,0},{2,3},{3,2},{4,5},{5,4},{6,7},{7,6},{8,9},{9,8},{10,11... | collective-permute-start | bytes 1572872 | tf_op jit(solution)/shard_map/ppermute | solution.py:442
  199.9 3.1 %collective-permute-start.17 = (f32[64,256]{1,0:T(8,128)S(1)}, f32[64,256]{1,0:T(8,128)S(1)}, u32[]{:S(2)}, u32[]{:S(2)}) collective-permute-start(f32[64,256]{1,0:T(8,128)S(1)} %send.8), channel_id=1, source_target_pairs={{0,1},{1,0},{2,3},{3,2},{4,5},{5,4},{6,7},{7,6},{8,9},{9,8},{10,11... | collective-permute-start | bytes 196616 | tf_op jit(solution)/shard_map/ppermute | solution.py:442
  203.8 6.8 %collective-permute-start.18 = (bf16[128,128]{1,0:T(8,128)(2,1)S(1)}, bf16[128,128]{1,0:T(8,128)(2,1)S(1)}, u32[]{:S(2)}, u32[]{:S(2)}) collective-permute-start(bf16[128,128]{1,0:T(8,128)(2,1)S(1)} %get-tuple-element.81), channel_id=1, source_target_pairs={{0,32},{32,64},{64,96},{1,33},{33,65},{65,97},{2,34},{34,66},{66,9... | collective-permute-start | bytes 98312 | tf_op jit(solution)/shard_map/ppermute | solution.py:493
  222.7 5.0 %collective-permute-start.19 = (bf16[16,128,128]{2,1,0:T(8,128)(2,1)S(1)}, bf16[16,128,128]{2,1,0:T(8,128)(2,1)S(1)}, u32[]{:S(2)}, u32[]{:S(2)}) collective-permute-start(bf16[16,128,128]{2,1,0:T(8,128)(2,1)S(1)} %all_to_all.52.part_ref), channel_id=1, source_target_pairs={{0,1},{1,0},{2,3},{3,2},{4,5},{5,4},{6,7},{7,6},{8,9},{9,8},{10,11... | collective-permute-start | bytes 1572872 | tf_op jit(solution)/shard_map/ppermute | solution.py:442
  249.1 3.1 %collective-permute-start.20 = (f32[64,256]{1,0:T(8,128)S(1)}, f32[64,256]{1,0:T(8,128)S(1)}, u32[]{:S(2)}, u32[]{:S(2)}) collective-permute-start(f32[64,256]{1,0:T(8,128)S(1)} %send.9), channel_id=1, source_target_pairs={{0,1},{1,0},{2,3},{3,2},{4,5},{5,4},{6,7},{7,6},{8,9},{9,8},{10,11... | collective-permute-start | bytes 196616 | tf_op jit(solution)/shard_map/ppermute | solution.py:442

commit v5 on v4

--- a/solution.py
+++ b/solution.py
@@ -12,6 +12,7 @@
 BS = 64
 CHIPS = 16
 ROWS = 64
+KEPT = 112
 GU_ROWS = D // 2
 GU_COLS = 14 * 128
 DN_ROWS = 32 * 256
@@ -76,8 +77,8 @@
     lax.fori_loop(0, 2 * tiles, one, 0)
 
 
-def down_pack_kernel(goal_ref, source, near, far, buf, spread, sems):
-    tiles, slots = goal_ref.shape[0] // 2, goal_ref.shape[1]
+def down_pack_kernel(near_goal, far_goal, source, near, far, buf, spread, sems):
+    tiles, slots = near_goal.shape
     parts = 7
     size = slots // parts
     for part in range(parts):
@@ -104,8 +105,8 @@
                 for inner in range(2):
                     for tile in range(tiles):
                         piece = spread[half, pl.ds(inner * 4 + tile, 32, stride=8), :].astype(near.dtype)
-                        for which, target in enumerate((near, far)):
-                            goal = pl.multiple_of(goal_ref[which * tiles + tile, slot + inner], 32)
+                        for goal_ref, target in ((near_goal, near), (far_goal, far)):
+                            goal = pl.multiple_of(goal_ref[tile, slot + inner], 32)
                             target[pl.ds(goal, 32), tile * 128 : (tile + 1) * 128] = piece
             return 0
 
@@ -120,7 +121,7 @@
     return pl.pallas_call(
         kernel,
         out_shape=[pltpu.VMEM(shape, jnp.bfloat16)] * results,
-        in_specs=[pl.BlockSpec(memory_space=pltpu.SMEM)]
+        in_specs=[pl.BlockSpec(memory_space=pltpu.SMEM)] * len(goals)
         + [pl.BlockSpec(memory_space=pltpu.HBM)] * len(sources),
         out_specs=[pl.BlockSpec(memory_space=pltpu.VMEM)] * results,
         scratch_shapes=[
@@ -131,7 +132,7 @@
         compiler_params=pltpu.CompilerParams(vmem_limit_bytes=12 * MIB),
         cost_estimate=pl.CostEstimate(flops=0, bytes_accessed=40 * MIB, transcendentals=0),
         name=name,
-    )(goals, *sources)
+    )(*goals, *sources)
 
 
 def densify_wide(goals, gate_blocks, up_blocks):
@@ -139,7 +140,7 @@
     buf = (2 * tiles, slots, BS * BS)
     shape = (GU_ROWS + 32, GU_COLS)
     sources = (gate_blocks, up_blocks)
-    return pack(wide_pack_kernel, goals, sources, buf, (2, 512), 2 * tiles, shape, 1, "pack_wide")[0]
+    return pack(wide_pack_kernel, (goals,), sources, buf, (2, 512), 2 * tiles, shape, 1, "pack_wide")[0]
 
 
 def densify_down(goals, blocks):
@@ -160,13 +161,8 @@
     row = (device >> 1) * 256 + (index - device * 7) * 32
     near = (device & 1) == core
     trash = DN_ROWS // 2
-    return jnp.concatenate(
-        [
-            jnp.where((index >= 0) & near, row, trash),
-            jnp.where((index >= 0) & jnp.logical_not(near), row, trash),
-        ],
-        axis=0,
-    )
+    kept = index >= 0
+    return jnp.where(kept & near, row, trash), jnp.where(kept & jnp.logical_not(near), row, trash)
 
 
 def fold(even, odd, at):
@@ -227,14 +223,36 @@
     pieces.append(jnp.where(low, last, 0.0).astype(jnp.bfloat16))
     hidden = jnp.dot(
         jnp.concatenate(pieces, axis=1), order_ref[...], preferred_element_type=jnp.float32
-    ).astype(jnp.bfloat16)
+    )
     hidden = jnp.concatenate([hidden[:, :256], hidden[:, 256:]], axis=0)
+    extra = []
+    for slot in range(7):
+        half = slot // 4 * 128
+        piece = hidden[KEPT:, half : half + 128]
+        extra.append(pltpu.roll(piece, (96 - slot % 4 * 32) % 128, 1) if slot % 4 != 3 else piece)
+    spare = lax.broadcasted_iota(jnp.int32, (KEPT, 128), 1) >= 96
+    right = jnp.where(spare, jnp.concatenate(extra, axis=0), hidden[:KEPT, 128:])
+    hidden = jnp.concatenate([hidden[:KEPT, :128], right], axis=1).astype(jnp.bfloat16)
     for chip in range(CHIPS):
         out_ref[chip] = hidden
 
 
 def mixed_of(part_ref, weight_ref):
-    left = jnp.concatenate([part_ref[chip] for chip in range(CHIPS)], axis=1)
+    lane = lax.broadcasted_iota(jnp.int32, (16, 128), 1)
+    pieces = []
+    for chip in range(CHIPS):
+        tails = []
+        for half in range(2):
+            tail = jnp.zeros((16, 128), jnp.float32)
+            for slot in range(half * 4, min(half * 4 + 4, 7)):
+                piece = part_ref[chip, slot * 16 : slot * 16 + 16, 128:].astype(jnp.float32)
+                at = slot % 4 * 32
+                piece = pltpu.roll(piece, (at + 32) % 128, 1) if at != 96 else piece
+                tail = jnp.where((lane >= at) & (lane < at + 32), piece, tail)
+            tails.append(tail)
+        tail = jnp.concatenate(tails, axis=1).astype(jnp.bfloat16)
+        pieces.append(jnp.concatenate([part_ref[chip], tail], axis=0))
+    left = jnp.concatenate(pieces, axis=1)
     acc = jnp.dot(left, weight_ref[: DN_ROWS // 2, :], preferred_element_type=jnp.float32)
     even, odd = acc[:ROWS], acc[ROWS:]
     return jnp.concatenate([fold(even, odd, 0), fold(even, odd, 256)], axis=1)
@@ -244,10 +262,14 @@
     out_ref[...] = mixed_of(part_ref, weight_ref)
 
 
-def keep_kernel(part_ref, weight_ref, got_ref, taken_ref, order_ref, back_ref, out_ref, next_ref):
+def own_kernel(part_ref, weight_ref, taken_ref, back_ref, taken_out, out_ref):
     taken = jnp.concatenate([taken_ref[:ROWS], taken_ref[ROWS:]], axis=1)
-    taken = jnp.dot(taken, back_ref[...], preferred_element_type=jnp.float32)
-    produced = (taken + (mixed_of(part_ref, weight_ref) + got_ref[...])).astype(jnp.bfloat16)
+    taken_out[...] = jnp.dot(taken, back_ref[...], preferred_element_type=jnp.float32)
+    out_ref[...] = mixed_of(part_ref, weight_ref)
+
+
+def finish_kernel(taken_ref, own_ref, got_ref, order_ref, out_ref, next_ref):
+    produced = (taken_ref[...] + (own_ref[...] + got_ref[...])).astype(jnp.bfloat16)
     out_ref[...] = produced
     ordered = jnp.dot(produced, order_ref[...], preferred_element_type=jnp.float32).astype(jnp.bfloat16)
     next_ref[...] = jnp.concatenate([ordered[:, :128], ordered[:, 128:]], axis=0)
@@ -375,7 +397,7 @@
 def call_far(core, part, gain, weight, order, acc, square):
     return pl.pallas_call(
         far_kernel,
-        out_shape=jax.ShapeDtypeStruct((CHIPS, 2 * ROWS, 256), jnp.bfloat16),
+        out_shape=jax.ShapeDtypeStruct((CHIPS, KEPT, 256), jnp.bfloat16),
         in_specs=[SMEM] + [VMEM] * 6,
         out_specs=VMEM,
         scratch_shapes=[pltpu.VMEM((2 * ROWS, GU_ROWS // 2), jnp.bfloat16)],
@@ -397,19 +419,30 @@
     )(part, resident(weight))
 
 
-def call_keep(part, weight, got, taken, order, back):
-    return pl.pallas_call(
-        keep_kernel,
+def call_own(part, weight, taken, back):
+    return pl.pallas_call(
+        own_kernel,
+        out_shape=[jax.ShapeDtypeStruct((ROWS, 256), jnp.float32)] * 2,
+        in_specs=[VMEM] * 4,
+        out_specs=[VMEM] * 2,
+        compiler_params=pltpu.CompilerParams(vmem_limit_bytes=16 * MIB),
+        cost_estimate=cost(DN_ROWS * DN_COLS // 2),
+        name="own",
+    )(part, resident(weight), taken, back)
+
+
+def call_finish(taken, own, got, order):
+    return pl.pallas_call(
+        finish_kernel,
         out_shape=(
             jax.ShapeDtypeStruct((ROWS, 256), jnp.bfloat16),
             jax.ShapeDtypeStruct((2 * ROWS, 128), jnp.bfloat16),
         ),
-        in_specs=[VMEM] * 6,
+        in_specs=[VMEM] * 4,
         out_specs=(VMEM, VMEM),
-        compiler_params=pltpu.CompilerParams(vmem_limit_bytes=16 * MIB),
-        cost_estimate=cost(DN_ROWS * DN_COLS // 2),
-        name="keep",
-    )(part, resident(weight), got, taken, order, back)
+        compiler_params=pltpu.CompilerParams(vmem_limit_bytes=4 * MIB),
+        name="finish",
+    )(taken, own, got, order)
 
 
 def call_pick(place, made, groups):
@@ -472,8 +505,9 @@
             out_now, norm_gain, core = lax.optimization_barrier((out_index[0], norm_gain, core))
             gain = gains_of(norm_gain, x_order)
             down, lent = densify_down(out_goals(out_now, core[0]), down_blocks[0])
-            line = placed_by(line_kernel, x_at, parts + [resident(down)], 4)
-            in_now, line = lax.optimization_barrier((in_index[0], line))
+            line = placed_by(line_kernel, x_at, parts + [resident(down), gain], 4)
+            in_now, line, lent = lax.optimization_barrier((in_index[0], line, lent))
+            borrowed = swapped(lent)
             parts = shifted_all(line, False)
             wide = densify_wide(in_goals(in_now), gate_blocks[0], up_blocks[0])
             mine = placed_by(plane_kernel, y_at, parts + [resident(wide)], CHIPS)
@@ -482,12 +516,10 @@
         other = swapped(mine)
         acc, square = call_near(core, mine, gain, wide)
         hidden = call_far(core, other, gain, wide, h_order, acc, square)
-        if tick == 0:
-            hidden, lent = lax.optimization_barrier((hidden, lent))
-            borrowed = swapped(lent)
         mine = exchanged(hidden)
         got = swapped(call_send(mine, borrowed))
-        produced, ordered = call_keep(mine, down, got, taken, x_order, x_back)
+        residual, own = call_own(mine, down, taken, x_back)
+        produced, ordered = call_finish(residual, own, got, x_order)
         made.append(produced)
         if tick + 1 < tick_count:
             carried = lax.ppermute(ordered, "segment", hops)

time: 255 us -> 245 us (0.961)
  blocking collectives: 144 us -> 135 us
  waiting for transfers between devices: 10.6 us -> 7.74 us
    all_to_all x9, blocking collectives: 144 us -> 135 us  [exchanged(): return lax.all_to_all(value, 'tensor', 0, 0, axis_index_groups=same_core)]
    ppermute x11, waiting for transfers between devices: 5.78 us -> 1.97 us  [swapped(): return lax.ppermute(value, 'tensor', [(i, i ^ 1) for i in range(2 * CHIPS)])]
    pallas_call x10 -> x15, Pallas kernels: 13.9 us -> 14.5 us  [the longest x5 9.17 us: call_far(): pl.pallas_call(far_kernel, out_shape=jax.ShapeDtypeStruct((CHIPS, KEPT, 2...]
  transfers between devices with their start and end apart: 21 -> 21, of which waited for: 15 -> 15; matrix products, arithmetic and copies ran while one was open for 1% -> 1% of each run, Pallas kernels for 7% -> 10%
where the time goes in v5:
time: 245 us; the launch traced here: 244 us
  blocking collectives  135 us (55%)
  starting transfers between devices  58.8 us (24%)
  Pallas kernels  38.1 us (16%)
  waiting for transfers between devices  7.74 us (3%)
  local copies, waits for them, and re-layouts  2.66 us (1%)
    all_to_all x9, blocking collectives, exchanged(): return lax.all_to_all(value, 'tensor', 0, 0, axis_index_groups=same_core)  135 us
    ppermute x11, starting transfers between devices, swapped(): return lax.ppermute(value, 'tensor', [(i, i ^ 1) for i in range(2 * CHIPS)])  27.9 us
    ppermute x4, starting transfers between devices, local(): carried = lax.ppermute(ordered, 'segment', hops)  23.4 us
    pallas_call x2, Pallas kernels, pack(): pl.pallas_call(kernel, out_shape=[pltpu.VMEM(shape, jnp.bfloat16)] * resu...  12.4 us
    pallas_call x5, Pallas kernels, call_far(): pl.pallas_call(far_kernel, out_shape=jax.ShapeDtypeStruct((CHIPS, KEPT, 2...  9.17 us
    ppermute x6, starting transfers between devices, shifted_all(): parts.append(lax.ppermute(value, 'tensor', pairs))  7.46 us
    pallas_call x5, Pallas kernels, call_near(): pl.pallas_call(near_kernel, out_shape=(jax.ShapeDtypeStruct((2 * ROWS, GU...  6.17 us
  transfers between devices with their start and end apart: 21, of which 15 were waited for; matrix products, arithmetic and copies ran while one was open for 1% of the time, Pallas kernels for 10%

profile of v5, /device:TPU:65, one launch (start us, length us, event | category | flops | bytes accessed | tf_op | source)
XLA Modules:
  0.0 244.3 jit_solution(1876910747554478788)
XLA Ops:
  1.3 2.6 %collective-permute-start.2 = (bf16[128,128]{1,0:T(8,128)(2,1)S(1)}, bf16[128,128]{1,0:T(8,128)(2,1)S(1)}, u32[]{:S(2)}, u32[]{:S(2)}) collective-permute-start(bf16[128,128]{1,0:T(8,128)(2,1)S(1)} %get-tuple-element.61.refs_0_.taken_ref), channel_id=1, source_target_pairs={{0,24},{1,25},{2,26},{3,27},{4,28},{5,29},{6,30},{7,31},{8,0},{9,1... | collective-permute-start | bytes 98312 | tf_op jit(solution)/shard_map/ppermute | solution.py:377
  8.0 5.5 %pack_down.1 = (bf16[4128,512]{1,0:T(8,128)(2,1)S(1)}, bf16[4128,512]{1,0:T(8,128)(2,1)S(1)}) custom-call(s32[4,126]{1,0:T(4,128)S(1)} %and_select_fusion.1.near_goal, s32[4,126]{1,0:T(4,128)S(1)} %get-tuple-element.103.far_goal, bf16[126,4,4096]{2,1,0:T(4,128)(2,1)} %bitcast.20), custom_call_target="tpu_custom_call" | custom-call | bytes 41943040 | tf_op jit(solution)/shard_map/pack_down/pallas_call | solution.py:121
  15.2 2.7 %collective-permute-start.5 = (bf16[4,128,128]{2,1,0:T(8,128)(2,1)S(1)}, bf16[4,128,128]{2,1,0:T(8,128)(2,1)S(1)}, u32[]{:S(2)}, u32[]{:S(2)}) collective-permute-start(bf16[4,128,128]{2,1,0:T(8,128)(2,1)S(1)} %placed.2.refs_0_), channel_id=1, source_target_pairs={{0,6},{1,7},{2,0},{3,1},{4,2},{5,3},{6,4},{7,5},{8,14},{9,15},{10,... | collective-permute-start | bytes 393224 | tf_op jit(solution)/shard_map/ppermute | solution.py:377
  19.0 6.9 %pack_wide.1.refs_4_.weight_ref = bf16[4128,1792]{1,0:T(8,128)(2,1)S(1)} custom-call(s32[7,72]{1,0:T(8,128)S(1)} %add_select_fusion.goal_ref, bf16[7,72,4096]{2,1,0:T(8,128)(2,1)} %bitcast.21, bf16[7,72,4096]{2,1,0:T(8,128)(2,1)} %bitcast.22), custom_call_target="tpu_custom_call" | custom-call | bytes 41943040 | tf_op jit(solution)/shard_map/pack_wide/pallas_call | solution.py:121
  25.9 1.8 collective-permute-done.3.refs_1_
  29.8 1.8 far.5
  31.7 17.7 %all_to_all.45.part_ref = bf16[16,112,256]{2,1,0:T(8,128)(2,1)S(1)} all-to-all(bf16[16,112,256]{2,1,0:T(8,128)(2,1)S(1)} %far.5), channel_id=1, replica_groups={{0,2,4,6,8,10,12,14,16,18,20,22,24,26,28,30},{1,3,5,7,9,11,13,15,17,19,..., dimensions={0} | all-to-all | bytes 1835008 | tf_op jit(solution)/shard_map/all_to_all | solution.py:471
  50.2 2.4 collective-permute-start.8
  53.7 6.1 %collective-permute-start.9 = (bf16[128,128]{1,0:T(8,128)(2,1)S(1)}, bf16[128,128]{1,0:T(8,128)(2,1)S(1)}, u32[]{:S(2)}, u32[]{:S(2)}) collective-permute-start(bf16[128,128]{1,0:T(8,128)(2,1)S(1)} %get-tuple-element.79), channel_id=1, source_target_pairs={{0,32},{32,64},{64,96},{1,33},{33,65},{65,97},{2,34},{34,66},{66,9... | collective-permute-start | bytes 98312 | tf_op jit(solution)/shard_map/ppermute | solution.py:525
  60.9 12.2 %all_to_all.46.part_ref = bf16[16,128,128]{2,1,0:T(8,128)(2,1)S(1)} all-to-all(bf16[16,128,128]{2,1,0:T(8,128)(2,1)S(1)} %broadcast_in_dim.62), channel_id=1, replica_groups={{0,2,4,6,8,10,12,14,16,18,20,22,24,26,28,30},{1,3,5,7,9,11,13,15,17,19,..., dimensions={0} | all-to-all | bytes 1048576 | tf_op jit(solution)/shard_map/all_to_all | solution.py:471
  73.1 3.4 %collective-permute-start.10 = (bf16[16,128,128]{2,1,0:T(8,128)(2,1)S(1)}, bf16[16,128,128]{2,1,0:T(8,128)(2,1)S(1)}, u32[]{:S(2)}, u32[]{:S(2)}) collective-permute-start(bf16[16,128,128]{2,1,0:T(8,128)(2,1)S(1)} %all_to_all.46.part_ref), channel_id=1, source_target_pairs={{0,1},{1,0},{2,3},{3,2},{4,5},{5,4},{6,7},{7,6},{8,9},{9,8},{10,11... | collective-permute-start | bytes 1572872 | tf_op jit(solution)/shard_map/ppermute | solution.py:475
  78.1 1.8 far.6
  80.0 17.1 %all_to_all.47.part_ref = bf16[16,112,256]{2,1,0:T(8,128)(2,1)S(1)} all-to-all(bf16[16,112,256]{2,1,0:T(8,128)(2,1)S(1)} %far.6), channel_id=1, replica_groups={{0,2,4,6,8,10,12,14,16,18,20,22,24,26,28,30},{1,3,5,7,9,11,13,15,17,19,..., dimensions={0} | all-to-all | bytes 1835008 | tf_op jit(solution)/shard_map/all_to_all | solution.py:471
  97.8 2.4 collective-permute-start.11
  101.3 5.8 %collective-permute-start.12 = (bf16[128,128]{1,0:T(8,128)(2,1)S(1)}, bf16[128,128]{1,0:T(8,128)(2,1)S(1)}, u32[]{:S(2)}, u32[]{:S(2)}) collective-permute-start(bf16[128,128]{1,0:T(8,128)(2,1)S(1)} %get-tuple-element.85), channel_id=1, source_target_pairs={{0,32},{32,64},{64,96},{1,33},{33,65},{65,97},{2,34},{34,66},{66,9... | collective-permute-start | bytes 98312 | tf_op jit(solution)/shard_map/ppermute | solution.py:525
  108.2 12.2 %all_to_all.48.part_ref = bf16[16,128,128]{2,1,0:T(8,128)(2,1)S(1)} all-to-all(bf16[16,128,128]{2,1,0:T(8,128)(2,1)S(1)} %broadcast_in_dim.63), channel_id=1, replica_groups={{0,2,4,6,8,10,12,14,16,18,20,22,24,26,28,30},{1,3,5,7,9,11,13,15,17,19,..., dimensions={0} | all-to-all | bytes 1048576 | tf_op jit(solution)/shard_map/all_to_all | solution.py:471
  120.4 3.4 %collective-permute-start.13 = (bf16[16,128,128]{2,1,0:T(8,128)(2,1)S(1)}, bf16[16,128,128]{2,1,0:T(8,128)(2,1)S(1)}, u32[]{:S(2)}, u32[]{:S(2)}) collective-permute-start(bf16[16,128,128]{2,1,0:T(8,128)(2,1)S(1)} %all_to_all.48.part_ref), channel_id=1, source_target_pairs={{0,1},{1,0},{2,3},{3,2},{4,5},{5,4},{6,7},{7,6},{8,9},{9,8},{10,11... | collective-permute-start | bytes 1572872 | tf_op jit(solution)/shard_map/ppermute | solution.py:475
  125.4 1.8 far.7
  127.2 17.1 %all_to_all.49.part_ref = bf16[16,112,256]{2,1,0:T(8,128)(2,1)S(1)} all-to-all(bf16[16,112,256]{2,1,0:T(8,128)(2,1)S(1)} %far.7), channel_id=1, replica_groups={{0,2,4,6,8,10,12,14,16,18,20,22,24,26,28,30},{1,3,5,7,9,11,13,15,17,19,..., dimensions={0} | all-to-all | bytes 1835008 | tf_op jit(solution)/shard_map/all_to_all | solution.py:471
  145.1 2.4 collective-permute-start.14
  148.5 5.8 %collective-permute-start.15 = (bf16[128,128]{1,0:T(8,128)(2,1)S(1)}, bf16[128,128]{1,0:T(8,128)(2,1)S(1)}, u32[]{:S(2)}, u32[]{:S(2)}) collective-permute-start(bf16[128,128]{1,0:T(8,128)(2,1)S(1)} %get-tuple-element.91), channel_id=1, source_target_pairs={{0,32},{32,64},{64,96},{1,33},{33,65},{65,97},{2,34},{34,66},{66,9... | collective-permute-start | bytes 98312 | tf_op jit(solution)/shard_map/ppermute | solution.py:525
  155.4 12.2 %all_to_all.50.part_ref = bf16[16,128,128]{2,1,0:T(8,128)(2,1)S(1)} all-to-all(bf16[16,128,128]{2,1,0:T(8,128)(2,1)S(1)} %broadcast_in_dim.64), channel_id=1, replica_groups={{0,2,4,6,8,10,12,14,16,18,20,22,24,26,28,30},{1,3,5,7,9,11,13,15,17,19,..., dimensions={0} | all-to-all | bytes 1048576 | tf_op jit(solution)/shard_map/all_to_all | solution.py:471
  167.7 3.4 %collective-permute-start.16 = (bf16[16,128,128]{2,1,0:T(8,128)(2,1)S(1)}, bf16[16,128,128]{2,1,0:T(8,128)(2,1)S(1)}, u32[]{:S(2)}, u32[]{:S(2)}) collective-permute-start(bf16[16,128,128]{2,1,0:T(8,128)(2,1)S(1)} %all_to_all.50.part_ref), channel_id=1, source_target_pairs={{0,1},{1,0},{2,3},{3,2},{4,5},{5,4},{6,7},{7,6},{8,9},{9,8},{10,11... | collective-permute-start | bytes 1572872 | tf_op jit(solution)/shard_map/ppermute | solution.py:475
  172.7 1.8 far.8
  174.5 17.1 %all_to_all.51.part_ref = bf16[16,112,256]{2,1,0:T(8,128)(2,1)S(1)} all-to-all(bf16[16,112,256]{2,1,0:T(8,128)(2,1)S(1)} %far.8), channel_id=1, replica_groups={{0,2,4,6,8,10,12,14,16,18,20,22,24,26,28,30},{1,3,5,7,9,11,13,15,17,19,..., dimensions={0} | all-to-all | bytes 1835008 | tf_op jit(solution)/shard_map/all_to_all | solution.py:471
  192.4 2.4 collective-permute-start.17
  195.8 5.8 %collective-permute-start.18 = (bf16[128,128]{1,0:T(8,128)(2,1)S(1)}, bf16[128,128]{1,0:T(8,128)(2,1)S(1)}, u32[]{:S(2)}, u32[]{:S(2)}) collective-permute-start(bf16[128,128]{1,0:T(8,128)(2,1)S(1)} %get-tuple-element.97), channel_id=1, source_target_pairs={{0,32},{32,64},{64,96},{1,33},{33,65},{65,97},{2,34},{34,66},{66,9... | collective-permute-start | bytes 98312 | tf_op jit(solution)/shard_map/ppermute | solution.py:525
  202.7 12.2 %all_to_all.52.part_ref = bf16[16,128,128]{2,1,0:T(8,128)(2,1)S(1)} all-to-all(bf16[16,128,128]{2,1,0:T(8,128)(2,1)S(1)} %broadcast_in_dim.65), channel_id=1, replica_groups={{0,2,4,6,8,10,12,14,16,18,20,22,24,26,28,30},{1,3,5,7,9,11,13,15,17,19,..., dimensions={0} | all-to-all | bytes 1048576 | tf_op jit(solution)/shard_map/all_to_all | solution.py:471
  214.9 3.4 %collective-permute-start.19 = (bf16[16,128,128]{2,1,0:T(8,128)(2,1)S(1)}, bf16[16,128,128]{2,1,0:T(8,128)(2,1)S(1)}, u32[]{:S(2)}, u32[]{:S(2)}) collective-permute-start(bf16[16,128,128]{2,1,0:T(8,128)(2,1)S(1)} %all_to_all.52.part_ref), channel_id=1, source_target_pairs={{0,1},{1,0},{2,3},{3,2},{4,5},{5,4},{6,7},{7,6},{8,9},{9,8},{10,11... | collective-permute-start | bytes 1572872 | tf_op jit(solution)/shard_map/ppermute | solution.py:475
  219.9 1.8 far.9
  221.8 17.1 %all_to_all.53.part_ref = bf16[16,112,256]{2,1,0:T(8,128)(2,1)S(1)} all-to-all(bf16[16,112,256]{2,1,0:T(8,128)(2,1)S(1)} %far.9), channel_id=1, replica_groups={{0,2,4,6,8,10,12,14,16,18,20,22,24,26,28,30},{1,3,5,7,9,11,13,15,17,19,..., dimensions={0} | all-to-all | bytes 1835008 | tf_op jit(solution)/shard_map/all_to_all | solution.py:471
  239.6 2.4 collective-permute-start.20
  (73 shorter events, 31.3 us)
Async XLA Ops:
  0.3 0.8 copy-start
  1.3 12.2 %collective-permute-start.2 = (bf16[128,128]{1,0:T(8,128)(2,1)S(1)}, bf16[128,128]{1,0:T(8,128)(2,1)S(1)}, u32[]{:S(2)}, u32[]{:S(2)}) collective-permute-start(bf16[128,128]{1,0:T(8,128)(2,1)S(1)} %get-tuple-element.61.refs_0_.taken_ref), channel_id=1, source_target_pairs={{0,24},{1,25},{2,26},{3,27},{4,28},{5,29},{6,30},{7,31},{8,0},{9,1... | collective-permute-start | bytes 98312 | tf_op jit(solution)/shard_map/ppermute | solution.py:377
  3.9 9.7 %collective-permute-start.1 = (bf16[128,128]{1,0:T(8,128)(2,1)S(1)}, bf16[128,128]{1,0:T(8,128)(2,1)S(1)}, u32[]{:S(2)}, u32[]{:S(2)}) collective-permute-start(bf16[128,128]{1,0:T(8,128)(2,1)S(1)} %get-tuple-element.61.refs_0_.taken_ref), channel_id=1, source_target_pairs={{0,16},{1,17},{2,18},{3,19},{4,20},{5,21},{6,22},{7,23},{8,24},{9,... | collective-permute-start | bytes 98312 | tf_op jit(solution)/shard_map/ppermute | solution.py:377
  4.4 9.1 %collective-permute-start = (bf16[128,128]{1,0:T(8,128)(2,1)S(1)}, bf16[128,128]{1,0:T(8,128)(2,1)S(1)}, u32[]{:S(2)}, u32[]{:S(2)}) collective-permute-start(bf16[128,128]{1,0:T(8,128)(2,1)S(1)} %get-tuple-element.61.refs_0_.taken_ref), channel_id=1, source_target_pairs={{0,8},{1,9},{2,10},{3,11},{4,12},{5,13},{6,14},{7,15},{8,16},{9,17... | collective-permute-start | bytes 98312 | tf_op jit(solution)/shard_map/ppermute | solution.py:377
  7.1 0.8 copy-start.1
  13.6 35.8 %collective-permute-start.7 = (bf16[4128,512]{1,0:T(8,128)(2,1)S(1)}, bf16[4128,512]{1,0:T(8,128)(2,1)S(1)}, u32[]{:S(2)}, u32[]{:S(2)}) collective-permute-start(bf16[4128,512]{1,0:T(8,128)(2,1)S(1)} %get-tuple-element.75), channel_id=1, source_target_pairs={{0,1},{1,0},{2,3},{3,2},{4,5},{5,4},{6,7},{7,6},{8,9},{9,8},{10,11... | collective-permute-start | bytes 12681224 | tf_op jit(solution)/shard_map/ppermute | solution.py:475
  15.2 10.7 %collective-permute-start.5 = (bf16[4,128,128]{2,1,0:T(8,128)(2,1)S(1)}, bf16[4,128,128]{2,1,0:T(8,128)(2,1)S(1)}, u32[]{:S(2)}, u32[]{:S(2)}) collective-permute-start(bf16[4,128,128]{2,1,0:T(8,128)(2,1)S(1)} %placed.2.refs_0_), channel_id=1, source_target_pairs={{0,6},{1,7},{2,0},{3,1},{4,2},{5,3},{6,4},{7,5},{8,14},{9,15},{10,... | collective-permute-start | bytes 393224 | tf_op jit(solution)/shard_map/ppermute | solution.py:377
  17.9 8.0 %collective-permute-start.4 = (bf16[4,128,128]{2,1,0:T(8,128)(2,1)S(1)}, bf16[4,128,128]{2,1,0:T(8,128)(2,1)S(1)}, u32[]{:S(2)}, u32[]{:S(2)}) collective-permute-start(bf16[4,128,128]{2,1,0:T(8,128)(2,1)S(1)} %placed.2.refs_0_), channel_id=1, source_target_pairs={{0,4},{1,5},{2,6},{3,7},{4,0},{5,1},{6,2},{7,3},{8,12},{9,13},{10,... | collective-permute-start | bytes 393224 | tf_op jit(solution)/shard_map/ppermute | solution.py:377
  18.3 9.4 %collective-permute-start.3 = (bf16[4,128,128]{2,1,0:T(8,128)(2,1)S(1)}, bf16[4,128,128]{2,1,0:T(8,128)(2,1)S(1)}, u32[]{:S(2)}, u32[]{:S(2)}) collective-permute-start(bf16[4,128,128]{2,1,0:T(8,128)(2,1)S(1)} %placed.2.refs_0_), channel_id=1, source_target_pairs={{0,2},{1,3},{2,4},{3,5},{4,6},{5,7},{6,0},{7,1},{8,10},{9,11},{10,... | collective-permute-start | bytes 393224 | tf_op jit(solution)/shard_map/ppermute | solution.py:377
  27.7 2.1 collective-permute-start.6
  50.2 3.3 %collective-permute-start.8 = (f32[64,256]{1,0:T(8,128)S(1)}, f32[64,256]{1,0:T(8,128)S(1)}, u32[]{:S(2)}, u32[]{:S(2)}) collective-permute-start(f32[64,256]{1,0:T(8,128)S(1)} %send.5), channel_id=1, source_target_pairs={{0,1},{1,0},{2,3},{3,2},{4,5},{5,4},{6,7},{7,6},{8,9},{9,8},{10,11... | collective-permute-start | bytes 196616 | tf_op jit(solution)/shard_map/ppermute | solution.py:475
  53.7 7.1 %collective-permute-start.9 = (bf16[128,128]{1,0:T(8,128)(2,1)S(1)}, bf16[128,128]{1,0:T(8,128)(2,1)S(1)}, u32[]{:S(2)}, u32[]{:S(2)}) collective-permute-start(bf16[128,128]{1,0:T(8,128)(2,1)S(1)} %get-tuple-element.79), channel_id=1, source_target_pairs={{0,32},{32,64},{64,96},{1,33},{33,65},{65,97},{2,34},{34,66},{66,9... | collective-permute-start | bytes 98312 | tf_op jit(solution)/shard_map/ppermute | solution.py:525
  73.1 5.0 %collective-permute-start.10 = (bf16[16,128,128]{2,1,0:T(8,128)(2,1)S(1)}, bf16[16,128,128]{2,1,0:T(8,128)(2,1)S(1)}, u32[]{:S(2)}, u32[]{:S(2)}) collective-permute-start(bf16[16,128,128]{2,1,0:T(8,128)(2,1)S(1)} %all_to_all.46.part_ref), channel_id=1, source_target_pairs={{0,1},{1,0},{2,3},{3,2},{4,5},{5,4},{6,7},{7,6},{8,9},{9,8},{10,11... | collective-permute-start | bytes 1572872 | tf_op jit(solution)/shard_map/ppermute | solution.py:475
  97.8 3.3 %collective-permute-start.11 = (f32[64,256]{1,0:T(8,128)S(1)}, f32[64,256]{1,0:T(8,128)S(1)}, u32[]{:S(2)}, u32[]{:S(2)}) collective-permute-start(f32[64,256]{1,0:T(8,128)S(1)} %send.6), channel_id=1, source_target_pairs={{0,1},{1,0},{2,3},{3,2},{4,5},{5,4},{6,7},{7,6},{8,9},{9,8},{10,11... | collective-permute-start | bytes 196616 | tf_op jit(solution)/shard_map/ppermute | solution.py:475
  101.3 6.8 %collective-permute-start.12 = (bf16[128,128]{1,0:T(8,128)(2,1)S(1)}, bf16[128,128]{1,0:T(8,128)(2,1)S(1)}, u32[]{:S(2)}, u32[]{:S(2)}) collective-permute-start(bf16[128,128]{1,0:T(8,128)(2,1)S(1)} %get-tuple-element.85), channel_id=1, source_target_pairs={{0,32},{32,64},{64,96},{1,33},{33,65},{65,97},{2,34},{34,66},{66,9... | collective-permute-start | bytes 98312 | tf_op jit(solution)/shard_map/ppermute | solution.py:525
  120.4 5.0 %collective-permute-start.13 = (bf16[16,128,128]{2,1,0:T(8,128)(2,1)S(1)}, bf16[16,128,128]{2,1,0:T(8,128)(2,1)S(1)}, u32[]{:S(2)}, u32[]{:S(2)}) collective-permute-start(bf16[16,128,128]{2,1,0:T(8,128)(2,1)S(1)} %all_to_all.48.part_ref), channel_id=1, source_target_pairs={{0,1},{1,0},{2,3},{3,2},{4,5},{5,4},{6,7},{7,6},{8,9},{9,8},{10,11... | collective-permute-start | bytes 1572872 | tf_op jit(solution)/shard_map/ppermute | solution.py:475
  145.1 3.3 %collective-permute-start.14 = (f32[64,256]{1,0:T(8,128)S(1)}, f32[64,256]{1,0:T(8,128)S(1)}, u32[]{:S(2)}, u32[]{:S(2)}) collective-permute-start(f32[64,256]{1,0:T(8,128)S(1)} %send.7), channel_id=1, source_target_pairs={{0,1},{1,0},{2,3},{3,2},{4,5},{5,4},{6,7},{7,6},{8,9},{9,8},{10,11... | collective-permute-start | bytes 196616 | tf_op jit(solution)/shard_map/ppermute | solution.py:475
  148.5 6.8 %collective-permute-start.15 = (bf16[128,128]{1,0:T(8,128)(2,1)S(1)}, bf16[128,128]{1,0:T(8,128)(2,1)S(1)}, u32[]{:S(2)}, u32[]{:S(2)}) collective-permute-start(bf16[128,128]{1,0:T(8,128)(2,1)S(1)} %get-tuple-element.91), channel_id=1, source_target_pairs={{0,32},{32,64},{64,96},{1,33},{33,65},{65,97},{2,34},{34,66},{66,9... | collective-permute-start | bytes 98312 | tf_op jit(solution)/shard_map/ppermute | solution.py:525
  167.7 5.0 %collective-permute-start.16 = (bf16[16,128,128]{2,1,0:T(8,128)(2,1)S(1)}, bf16[16,128,128]{2,1,0:T(8,128)(2,1)S(1)}, u32[]{:S(2)}, u32[]{:S(2)}) collective-permute-start(bf16[16,128,128]{2,1,0:T(8,128)(2,1)S(1)} %all_to_all.50.part_ref), channel_id=1, source_target_pairs={{0,1},{1,0},{2,3},{3,2},{4,5},{5,4},{6,7},{7,6},{8,9},{9,8},{10,11... | collective-permute-start | bytes 1572872 | tf_op jit(solution)/shard_map/ppermute | solution.py:475
  192.4 3.3 %collective-permute-start.17 = (f32[64,256]{1,0:T(8,128)S(1)}, f32[64,256]{1,0:T(8,128)S(1)}, u32[]{:S(2)}, u32[]{:S(2)}) collective-permute-start(f32[64,256]{1,0:T(8,128)S(1)} %send.8), channel_id=1, source_target_pairs={{0,1},{1,0},{2,3},{3,2},{4,5},{5,4},{6,7},{7,6},{8,9},{9,8},{10,11... | collective-permute-start | bytes 196616 | tf_op jit(solution)/shard_map/ppermute | solution.py:475
  195.8 6.8 %collective-permute-start.18 = (bf16[128,128]{1,0:T(8,128)(2,1)S(1)}, bf16[128,128]{1,0:T(8,128)(2,1)S(1)}, u32[]{:S(2)}, u32[]{:S(2)}) collective-permute-start(bf16[128,128]{1,0:T(8,128)(2,1)S(1)} %get-tuple-element.97), channel_id=1, source_target_pairs={{0,32},{32,64},{64,96},{1,33},{33,65},{65,97},{2,34},{34,66},{66,9... | collective-permute-start | bytes 98312 | tf_op jit(solution)/shard_map/ppermute | solution.py:525
  214.9 5.0 %collective-permute-start.19 = (bf16[16,128,128]{2,1,0:T(8,128)(2,1)S(1)}, bf16[16,128,128]{2,1,0:T(8,128)(2,1)S(1)}, u32[]{:S(2)}, u32[]{:S(2)}) collective-permute-start(bf16[16,128,128]{2,1,0:T(8,128)(2,1)S(1)} %all_to_all.52.part_ref), channel_id=1, source_target_pairs={{0,1},{1,0},{2,3},{3,2},{4,5},{5,4},{6,7},{7,6},{8,9},{9,8},{10,11... | collective-permute-start | bytes 1572872 | tf_op jit(solution)/shard_map/ppermute | solution.py:475
  239.6 3.3 %collective-permute-start.20 = (f32[64,256]{1,0:T(8,128)S(1)}, f32[64,256]{1,0:T(8,128)S(1)}, u32[]{:S(2)}, u32[]{:S(2)}) collective-permute-start(f32[64,256]{1,0:T(8,128)S(1)} %send.9), channel_id=1, source_target_pairs={{0,1},{1,0},{2,3},{3,2},{4,5},{5,4},{6,7},{7,6},{8,9},{9,8},{10,11... | collective-permute-start | bytes 196616 | tf_op jit(solution)/shard_map/ppermute | solution.py:475

commit v6 on v5

--- a/solution.py
+++ b/solution.py
@@ -31,7 +31,7 @@
 
 
 def wide_pack_kernel(goal_ref, gate_hbm, up_hbm, target, buf, spread, sems):
-    tiles, slots = goal_ref.shape
+    tiles, _, slots = goal_ref.shape
     for which, source in enumerate((gate_hbm, up_hbm)):
         for tile in range(tiles):
             at = which * tiles + tile
@@ -45,7 +45,7 @@
                     group : group + 8, part * 128 : (part + 1) * 128
                 ]
         for row in range(count):
-            goal = pl.multiple_of(goal_ref[tile, first + row], 32)
+            goal = pl.multiple_of(goal_ref[tile, 0, first + row], 32)
             piece = spread[half, pl.ds(row // 8 * 256 + row % 8, 32, stride=8), :]
             target[pl.ds(goal, 32), pl.ds(column, 128)] = piece.astype(target.dtype)
 
@@ -77,8 +77,8 @@
     lax.fori_loop(0, 2 * tiles, one, 0)
 
 
-def down_pack_kernel(near_goal, far_goal, source, near, far, buf, spread, sems):
-    tiles, slots = near_goal.shape
+def down_pack_kernel(goal_ref, source, near, far, buf, spread, sems):
+    _, tiles, slots = goal_ref.shape
     parts = 7
     size = slots // parts
     for part in range(parts):
@@ -105,8 +105,8 @@
                 for inner in range(2):
                     for tile in range(tiles):
                         piece = spread[half, pl.ds(inner * 4 + tile, 32, stride=8), :].astype(near.dtype)
-                        for goal_ref, target in ((near_goal, near), (far_goal, far)):
-                            goal = pl.multiple_of(goal_ref[tile, slot + inner], 32)
+                        for side, target in enumerate((near, far)):
+                            goal = pl.multiple_of(goal_ref[side, tile, slot + inner], 32)
                             target[pl.ds(goal, 32), tile * 128 : (tile + 1) * 128] = piece
             return 0
 
@@ -121,7 +121,7 @@
     return pl.pallas_call(
         kernel,
         out_shape=[pltpu.VMEM(shape, jnp.bfloat16)] * results,
-        in_specs=[pl.BlockSpec(memory_space=pltpu.SMEM)] * len(goals)
+        in_specs=[pl.BlockSpec(memory_space=pltpu.SMEM)]
         + [pl.BlockSpec(memory_space=pltpu.HBM)] * len(sources),
         out_specs=[pl.BlockSpec(memory_space=pltpu.VMEM)] * results,
         scratch_shapes=[
@@ -132,15 +132,15 @@
         compiler_params=pltpu.CompilerParams(vmem_limit_bytes=12 * MIB),
         cost_estimate=pl.CostEstimate(flops=0, bytes_accessed=40 * MIB, transcendentals=0),
         name=name,
-    )(*goals, *sources)
+    )(goals, *sources)
 
 
 def densify_wide(goals, gate_blocks, up_blocks):
-    tiles, slots = goals.shape
+    tiles, _, slots = goals.shape
     buf = (2 * tiles, slots, BS * BS)
     shape = (GU_ROWS + 32, GU_COLS)
     sources = (gate_blocks, up_blocks)
-    return pack(wide_pack_kernel, (goals,), sources, buf, (2, 512), 2 * tiles, shape, 1, "pack_wide")[0]
+    return pack(wide_pack_kernel, goals, sources, buf, (2, 512), 2 * tiles, shape, 1, "pack_wide")[0]
 
 
 def densify_down(goals, blocks):
@@ -157,12 +157,13 @@
 
 
 def out_goals(index, core):
-    device = lax.div(index, jnp.int32(7))
+    device = (index * 9363) >> 16
     row = (device >> 1) * 256 + (index - device * 7) * 32
     near = (device & 1) == core
     trash = DN_ROWS // 2
-    kept = index >= 0
-    return jnp.where(kept & near, row, trash), jnp.where(kept & jnp.logical_not(near), row, trash)
+    near_row = jnp.where(near, row, trash)
+    far_row = jnp.where(near, trash, row)
+    return jnp.where(index >= 0, near_row, trash), jnp.where(index >= 0, far_row, trash)
 
 
 def fold(even, odd, at):
@@ -275,7 +276,19 @@
     next_ref[...] = jnp.concatenate([ordered[:, :128], ordered[:, 128:]], axis=0)
 
 
-def gain_kernel(norm_ref, order_ref, gain_ref, rows_ref):
+def prepare_kernel(groups, core_ref, x_hbm, norm_hbm, in_hbm, out_hbm, order_ref, *refs):
+    firsts = refs[:groups]
+    gain_ref, wide_goal, down_goal, x_ref, norm_ref, in_ref, out_ref, rows_ref, sems = refs[groups:]
+    pairs = ((x_hbm, x_ref), (norm_hbm, norm_ref), (in_hbm, in_ref), (out_hbm, out_ref))
+    copies = [pltpu.make_async_copy(a, b, sems.at[at]) for at, (a, b) in enumerate(pairs)]
+    for copy in copies:
+        copy.start()
+    for copy in copies:
+        copy.wait()
+    ordered = jnp.dot(x_ref[...], order_ref[...], preferred_element_type=jnp.float32).astype(jnp.bfloat16)
+    for group, ref in enumerate(firsts):
+        part = ordered[group * ROWS : (group + 1) * ROWS]
+        ref[...] = jnp.concatenate([part[:, :128], part[:, 128:]], axis=0)
     for device in range(2 * CHIPS):
         rows_ref[device : device + 1, :] = norm_ref[:, device * 256 : (device + 1) * 256]
     left = rows_ref[...]
@@ -288,13 +301,10 @@
         at = 2 * (device % 2 * CHIPS + device // 2)
         for p in range(2):
             gain_ref[at + p : at + p + 1, :] = gain[device : device + 1, p * 128 : (p + 1) * 128]
-
-
-def prepare_kernel(x_ref, order_ref, *firsts):
-    ordered = jnp.dot(x_ref[...], order_ref[...], preferred_element_type=jnp.float32).astype(jnp.bfloat16)
-    for group, ref in enumerate(firsts):
-        part = ordered[group * ROWS : (group + 1) * ROWS]
-        ref[...] = jnp.concatenate([part[:, :128], part[:, 128:]], axis=0)
+    wide_goal[...] = in_goals(in_ref[...])
+    near, far = out_goals(out_ref[...], core_ref[0])
+    down_goal[0] = near
+    down_goal[1] = far
 
 
 def line_kernel(at_ref, *refs):
@@ -308,7 +318,7 @@
             refs[-1][line * 4 + ((at_ref[0] - shift) & 3)] = ref[line]
 
 
-def pick_kernel(place_ref, *refs):
+def last_kernel(place_ref, taken_ref, own_ref, got_ref, *refs):
     made, out_ref = refs[:-1], refs[-1]
     groups = out_ref.shape[0] // ROWS
     for segment in range(len(made) - groups + 1):
@@ -318,6 +328,14 @@
             for group in range(groups):
                 out_ref[group * ROWS : (group + 1) * ROWS, :] = made[group + segment][...]
 
+    @pl.when(place_ref[0] == len(made) - groups + 1)
+    def _():
+        for group in range(groups - 1):
+            at = len(made) - groups + 1 + group
+            out_ref[group * ROWS : (group + 1) * ROWS, :] = made[at][...]
+        produced = (taken_ref[...] + (own_ref[...] + got_ref[...])).astype(jnp.bfloat16)
+        out_ref[(groups - 1) * ROWS :, :] = produced
+
 
 VMEM = pl.BlockSpec(memory_space=pltpu.VMEM)
 SMEM = pl.BlockSpec(memory_space=pltpu.SMEM)
@@ -331,28 +349,24 @@
     return pl.CostEstimate(flops=2 * 128 * products, bytes_accessed=2 * MIB, transcendentals=0)
 
 
-def prepare(x_in, x_order):
+def prepare(core, x_in, norm_gain, in_index, out_index, x_order):
     groups = x_in.shape[0] // ROWS
-    return pl.pallas_call(
-        prepare_kernel,
-        out_shape=[jax.ShapeDtypeStruct((2 * ROWS, 128), jnp.bfloat16)] * groups,
-        in_specs=[VMEM] * 2,
-        out_specs=[VMEM] * groups,
+    hbm = [pltpu.with_memory_space_constraint(v, pltpu.HBM) for v in (x_in, norm_gain, in_index, out_index)]
+    return pl.pallas_call(
+        functools.partial(prepare_kernel, groups),
+        out_shape=[jax.ShapeDtypeStruct((2 * ROWS, 128), jnp.bfloat16)] * groups
+        + [
+            jax.ShapeDtypeStruct((4 * CHIPS, 128), jnp.float32),
+            jax.ShapeDtypeStruct(in_index.shape, jnp.int32),
+            jax.ShapeDtypeStruct((2,) + out_index.shape, jnp.int32),
+        ],
+        in_specs=[SMEM] + [pl.BlockSpec(memory_space=pltpu.HBM)] * 4 + [VMEM],
+        out_specs=[VMEM] * (groups + 3),
+        scratch_shapes=[pltpu.VMEM(v.shape, v.dtype) for v in (x_in, norm_gain, in_index, out_index)]
+        + [pltpu.VMEM((2 * CHIPS, 256), jnp.float32), pltpu.SemaphoreType.DMA((4,))],
         compiler_params=pltpu.CompilerParams(vmem_limit_bytes=4 * MIB),
         name="prepare",
-    )(x_in, x_order)
-
-
-def gains_of(norm_gain, x_order):
-    return pl.pallas_call(
-        gain_kernel,
-        out_shape=jax.ShapeDtypeStruct((4 * CHIPS, 128), jnp.float32),
-        in_specs=[VMEM] * 2,
-        out_specs=VMEM,
-        scratch_shapes=[pltpu.VMEM((2 * CHIPS, 256), jnp.float32)],
-        compiler_params=pltpu.CompilerParams(vmem_limit_bytes=4 * MIB),
-        name="gains",
-    )(norm_gain, x_order)
+    )(core, *hbm, x_order)
 
 
 def placed_by(kernel, at, parts, count):
@@ -445,15 +459,15 @@
     )(taken, own, got, order)
 
 
-def call_pick(place, made, groups):
-    return pl.pallas_call(
-        pick_kernel,
+def call_last(place, taken, own, got, made, groups):
+    return pl.pallas_call(
+        last_kernel,
         out_shape=jax.ShapeDtypeStruct((groups * ROWS, 256), jnp.bfloat16),
-        in_specs=[SMEM] + [VMEM] * len(made),
+        in_specs=[SMEM] + [VMEM] * (3 + len(made)),
         out_specs=VMEM,
         compiler_params=pltpu.CompilerParams(vmem_limit_bytes=4 * MIB),
-        name="pick",
-    )(place, *made)
+        name="last",
+    )(place, taken, own, got, *made)
 
 
 def orders():
@@ -485,12 +499,13 @@
     tick_count = group_count + segment_count - 1
     x_order, h_order = orders()
     x_back = x_order.T
-    firsts = prepare(x_in, x_order)
+    in_index = jnp.transpose(in_index, (1, 0, 2))
+    *firsts, gain, to_wide, to_down = prepare(core, x_in, norm_gain, in_index, out_index[0], x_order)
     is_first = jnp.broadcast_to(segment_at == 0, (8, 128)).astype(jnp.bfloat16)
     place = segment_at.astype(jnp.int32)[None]
     x_at, y_at = (tensor_at >> 3)[None], ((tensor_at >> 1) & 3)[None]
-    core, place, x_at, y_at, x_order, x_back, h_order, firsts, is_first = lax.optimization_barrier(
-        (core, place, x_at, y_at, x_order, x_back, h_order, firsts, is_first)
+    core, place, x_at, y_at, x_order, x_back, h_order, firsts, gain, is_first = lax.optimization_barrier(
+        (core, place, x_at, y_at, x_order, x_back, h_order, firsts, gain, is_first)
     )
 
     carried = None
@@ -502,14 +517,12 @@
             taken = jnp.where(jnp.tile(is_first, (2 * ROWS // 8, 1)) > 0, taken, carried)
         if tick == 0:
             parts = shifted_all(taken, True)
-            out_now, norm_gain, core = lax.optimization_barrier((out_index[0], norm_gain, core))
-            gain = gains_of(norm_gain, x_order)
-            down, lent = densify_down(out_goals(out_now, core[0]), down_blocks[0])
-            line = placed_by(line_kernel, x_at, parts + [resident(down), gain], 4)
-            in_now, line, lent = lax.optimization_barrier((in_index[0], line, lent))
+            down, lent = densify_down(to_down, down_blocks[0])
+            line = placed_by(line_kernel, x_at, parts + [resident(down)], 4)
+            to_wide, line, lent = lax.optimization_barrier((to_wide, line, lent))
             borrowed = swapped(lent)
             parts = shifted_all(line, False)
-            wide = densify_wide(in_goals(in_now), gate_blocks[0], up_blocks[0])
+            wide = densify_wide(to_wide, gate_blocks[0], up_blocks[0])
             mine = placed_by(plane_kernel, y_at, parts + [resident(wide)], CHIPS)
         else:
             mine = exchanged(jnp.broadcast_to(taken[None], (CHIPS, 2 * ROWS, 128)))
@@ -519,11 +532,11 @@
         mine = exchanged(hidden)
         got = swapped(call_send(mine, borrowed))
         residual, own = call_own(mine, down, taken, x_back)
+        if tick + 1 == tick_count:
+            return call_last(place, residual, own, got, made, group_count)[None]
         produced, ordered = call_finish(residual, own, got, x_order)
         made.append(produced)
-        if tick + 1 < tick_count:
-            carried = lax.ppermute(ordered, "segment", hops)
-    return call_pick(place, made, group_count)[None]
+        carried = lax.ppermute(ordered, "segment", hops)
 
 
 def solution(mesh):

time: 245 us -> 241 us (0.984)
  transfers between devices with their start and end apart: 21 -> 21, of which waited for: 15 -> 15; matrix products, arithmetic and copies ran while one was open for 1% -> 0% of each run, Pallas kernels for 10% -> 10%
where the time goes in v6:
time: 241 us
  blocking collectives  135 us (56%)
  starting transfers between devices  58.8 us (24%)
  Pallas kernels  38.1 us (16%)
  waiting for transfers between devices  7.76 us (3%)
    all_to_all x9, blocking collectives, exchanged(): return lax.all_to_all(value, 'tensor', 0, 0, axis_index_groups=same_core)  135 us
    ppermute x11, starting transfers between devices, swapped(): return lax.ppermute(value, 'tensor', [(i, i ^ 1) for i in range(2 * CHIPS)])  27.9 us
    ppermute x4, starting transfers between devices, local(): carried = lax.ppermute(ordered, 'segment', hops)  23.4 us
    pallas_call x2, Pallas kernels, pack(): pl.pallas_call(kernel, out_shape=[pltpu.VMEM(shape, jnp.bfloat16)] * resu...  12.3 us
    pallas_call x5, Pallas kernels, call_far(): pl.pallas_call(far_kernel, out_shape=jax.ShapeDtypeStruct((CHIPS, KEPT, 2...  9.21 us
    ppermute x6, starting transfers between devices, shifted_all(): parts.append(lax.ppermute(value, 'tensor', pairs))  7.46 us
    pallas_call x5, Pallas kernels, call_near(): pl.pallas_call(near_kernel, out_shape=(jax.ShapeDtypeStruct((2 * ROWS, GU...  6.17 us
  transfers between devices with their start and end apart: 21, of which 15 were waited for; matrix products, arithmetic and copies ran while one was open for 0% of the time, Pallas kernels for 10%

profile of v6, /device:TPU:65, one launch (start us, length us, event | category | flops | bytes accessed | tf_op | source)
XLA Modules:
  0.0 240.7 jit_solution(1935598505406702510)
XLA Ops:
  1.4 2.6 %collective-permute-start.2 = (bf16[128,128]{1,0:T(8,128)(2,1)S(1)}, bf16[128,128]{1,0:T(8,128)(2,1)S(1)}, u32[]{:S(2)}, u32[]{:S(2)}) collective-permute-start(bf16[128,128]{1,0:T(8,128)(2,1)S(1)} %get-tuple-element.64.refs_0_.taken_ref), channel_id=1, source_target_pairs={{0,24},{1,25},{2,26},{3,27},{4,28},{5,29},{6,30},{7,31},{8,0},{9,1... | collective-permute-start | bytes 98312 | tf_op jit(solution)/shard_map/ppermute | solution.py:391
  5.1 5.5 %pack_down.1 = (bf16[4128,512]{1,0:T(8,128)(2,1)S(1)}, bf16[4128,512]{1,0:T(8,128)(2,1)S(1)}) custom-call(s32[2,4,126]{2,1,0:T(4,128)S(1)} %get-tuple-element.65.goal_ref, bf16[126,4,4096]{2,1,0:T(4,128)(2,1)} %bitcast.17), custom_call_target="tpu_custom_call" | custom-call | bytes 41943040 | tf_op jit(solution)/shard_map/pack_down/pallas_call | solution.py:121
  12.2 2.7 %collective-permute-start.5 = (bf16[4,128,128]{2,1,0:T(8,128)(2,1)S(1)}, bf16[4,128,128]{2,1,0:T(8,128)(2,1)S(1)}, u32[]{:S(2)}, u32[]{:S(2)}) collective-permute-start(bf16[4,128,128]{2,1,0:T(8,128)(2,1)S(1)} %placed.2.refs_0_), channel_id=1, source_target_pairs={{0,6},{1,7},{2,0},{3,1},{4,2},{5,3},{6,4},{7,5},{8,14},{9,15},{10,... | collective-permute-start | bytes 393224 | tf_op jit(solution)/shard_map/ppermute | solution.py:391
  16.0 6.9 %pack_wide.1.refs_4_.weight_ref = bf16[4128,1792]{1,0:T(8,128)(2,1)S(1)} custom-call(s32[7,1,72]{2,1,0:T(1,128)S(1)} %get-tuple-element.69.goal_ref, bf16[7,72,4096]{2,1,0:T(8,128)(2,1)} %bitcast.18, bf16[7,72,4096]{2,1,0:T(8,128)(2,1)} %bitcast.19), custom_call_target="tpu_custom_call" | custom-call | bytes 41943040 | tf_op jit(solution)/shard_map/pack_wide/pallas_call | solution.py:121
  22.9 1.8 collective-permute-done.3.refs_1_
  26.9 1.8 far.5
  28.7 17.7 %all_to_all.45.part_ref = bf16[16,112,256]{2,1,0:T(8,128)(2,1)S(1)} all-to-all(bf16[16,112,256]{2,1,0:T(8,128)(2,1)S(1)} %far.5), channel_id=1, replica_groups={{0,2,4,6,8,10,12,14,16,18,20,22,24,26,28,30},{1,3,5,7,9,11,13,15,17,19,..., dimensions={0} | all-to-all | bytes 1835008 | tf_op jit(solution)/shard_map/all_to_all | solution.py:485
  47.2 2.4 collective-permute-start.8
  50.7 6.1 %collective-permute-start.9 = (bf16[128,128]{1,0:T(8,128)(2,1)S(1)}, bf16[128,128]{1,0:T(8,128)(2,1)S(1)}, u32[]{:S(2)}, u32[]{:S(2)}) collective-permute-start(bf16[128,128]{1,0:T(8,128)(2,1)S(1)} %get-tuple-element.79), channel_id=1, source_target_pairs={{0,32},{32,64},{64,96},{1,33},{33,65},{65,97},{2,34},{34,66},{66,9... | collective-permute-start | bytes 98312 | tf_op jit(solution)/shard_map/ppermute | solution.py:539
  57.9 12.3 %all_to_all.46.part_ref = bf16[16,128,128]{2,1,0:T(8,128)(2,1)S(1)} all-to-all(bf16[16,128,128]{2,1,0:T(8,128)(2,1)S(1)} %broadcast_in_dim.25), channel_id=1, replica_groups={{0,2,4,6,8,10,12,14,16,18,20,22,24,26,28,30},{1,3,5,7,9,11,13,15,17,19,..., dimensions={0} | all-to-all | bytes 1048576 | tf_op jit(solution)/shard_map/all_to_all | solution.py:485
  70.2 3.4 %collective-permute-start.10 = (bf16[16,128,128]{2,1,0:T(8,128)(2,1)S(1)}, bf16[16,128,128]{2,1,0:T(8,128)(2,1)S(1)}, u32[]{:S(2)}, u32[]{:S(2)}) collective-permute-start(bf16[16,128,128]{2,1,0:T(8,128)(2,1)S(1)} %all_to_all.46.part_ref), channel_id=1, source_target_pairs={{0,1},{1,0},{2,3},{3,2},{4,5},{5,4},{6,7},{7,6},{8,9},{9,8},{10,11... | collective-permute-start | bytes 1572872 | tf_op jit(solution)/shard_map/ppermute | solution.py:489
  75.2 1.8 far.6
  77.0 17.1 %all_to_all.47.part_ref = bf16[16,112,256]{2,1,0:T(8,128)(2,1)S(1)} all-to-all(bf16[16,112,256]{2,1,0:T(8,128)(2,1)S(1)} %far.6), channel_id=1, replica_groups={{0,2,4,6,8,10,12,14,16,18,20,22,24,26,28,30},{1,3,5,7,9,11,13,15,17,19,..., dimensions={0} | all-to-all | bytes 1835008 | tf_op jit(solution)/shard_map/all_to_all | solution.py:485
  94.9 2.4 collective-permute-start.11
  98.3 5.8 %collective-permute-start.12 = (bf16[128,128]{1,0:T(8,128)(2,1)S(1)}, bf16[128,128]{1,0:T(8,128)(2,1)S(1)}, u32[]{:S(2)}, u32[]{:S(2)}) collective-permute-start(bf16[128,128]{1,0:T(8,128)(2,1)S(1)} %get-tuple-element.84), channel_id=1, source_target_pairs={{0,32},{32,64},{64,96},{1,33},{33,65},{65,97},{2,34},{34,66},{66,9... | collective-permute-start | bytes 98312 | tf_op jit(solution)/shard_map/ppermute | solution.py:539
  105.2 12.2 %all_to_all.48.part_ref = bf16[16,128,128]{2,1,0:T(8,128)(2,1)S(1)} all-to-all(bf16[16,128,128]{2,1,0:T(8,128)(2,1)S(1)} %broadcast_in_dim.52), channel_id=1, replica_groups={{0,2,4,6,8,10,12,14,16,18,20,22,24,26,28,30},{1,3,5,7,9,11,13,15,17,19,..., dimensions={0} | all-to-all | bytes 1048576 | tf_op jit(solution)/shard_map/all_to_all | solution.py:485
  117.5 3.4 %collective-permute-start.13 = (bf16[16,128,128]{2,1,0:T(8,128)(2,1)S(1)}, bf16[16,128,128]{2,1,0:T(8,128)(2,1)S(1)}, u32[]{:S(2)}, u32[]{:S(2)}) collective-permute-start(bf16[16,128,128]{2,1,0:T(8,128)(2,1)S(1)} %all_to_all.48.part_ref), channel_id=1, source_target_pairs={{0,1},{1,0},{2,3},{3,2},{4,5},{5,4},{6,7},{7,6},{8,9},{9,8},{10,11... | collective-permute-start | bytes 1572872 | tf_op jit(solution)/shard_map/ppermute | solution.py:489
  122.4 1.8 far.7
  124.3 17.1 %all_to_all.49.part_ref = bf16[16,112,256]{2,1,0:T(8,128)(2,1)S(1)} all-to-all(bf16[16,112,256]{2,1,0:T(8,128)(2,1)S(1)} %far.7), channel_id=1, replica_groups={{0,2,4,6,8,10,12,14,16,18,20,22,24,26,28,30},{1,3,5,7,9,11,13,15,17,19,..., dimensions={0} | all-to-all | bytes 1835008 | tf_op jit(solution)/shard_map/all_to_all | solution.py:485
  142.2 2.4 collective-permute-start.14
  145.6 5.8 %collective-permute-start.15 = (bf16[128,128]{1,0:T(8,128)(2,1)S(1)}, bf16[128,128]{1,0:T(8,128)(2,1)S(1)}, u32[]{:S(2)}, u32[]{:S(2)}) collective-permute-start(bf16[128,128]{1,0:T(8,128)(2,1)S(1)} %get-tuple-element.89), channel_id=1, source_target_pairs={{0,32},{32,64},{64,96},{1,33},{33,65},{65,97},{2,34},{34,66},{66,9... | collective-permute-start | bytes 98312 | tf_op jit(solution)/shard_map/ppermute | solution.py:539
  152.5 12.2 %all_to_all.50.part_ref = bf16[16,128,128]{2,1,0:T(8,128)(2,1)S(1)} all-to-all(bf16[16,128,128]{2,1,0:T(8,128)(2,1)S(1)} %broadcast_in_dim.53), channel_id=1, replica_groups={{0,2,4,6,8,10,12,14,16,18,20,22,24,26,28,30},{1,3,5,7,9,11,13,15,17,19,..., dimensions={0} | all-to-all | bytes 1048576 | tf_op jit(solution)/shard_map/all_to_all | solution.py:485
  164.7 3.4 %collective-permute-start.16 = (bf16[16,128,128]{2,1,0:T(8,128)(2,1)S(1)}, bf16[16,128,128]{2,1,0:T(8,128)(2,1)S(1)}, u32[]{:S(2)}, u32[]{:S(2)}) collective-permute-start(bf16[16,128,128]{2,1,0:T(8,128)(2,1)S(1)} %all_to_all.50.part_ref), channel_id=1, source_target_pairs={{0,1},{1,0},{2,3},{3,2},{4,5},{5,4},{6,7},{7,6},{8,9},{9,8},{10,11... | collective-permute-start | bytes 1572872 | tf_op jit(solution)/shard_map/ppermute | solution.py:489
  169.7 1.8 far.8
  171.6 17.1 %all_to_all.51.part_ref = bf16[16,112,256]{2,1,0:T(8,128)(2,1)S(1)} all-to-all(bf16[16,112,256]{2,1,0:T(8,128)(2,1)S(1)} %far.8), channel_id=1, replica_groups={{0,2,4,6,8,10,12,14,16,18,20,22,24,26,28,30},{1,3,5,7,9,11,13,15,17,19,..., dimensions={0} | all-to-all | bytes 1835008 | tf_op jit(solution)/shard_map/all_to_all | solution.py:485
  189.5 2.4 collective-permute-start.17
  192.9 5.8 %collective-permute-start.18 = (bf16[128,128]{1,0:T(8,128)(2,1)S(1)}, bf16[128,128]{1,0:T(8,128)(2,1)S(1)}, u32[]{:S(2)}, u32[]{:S(2)}) collective-permute-start(bf16[128,128]{1,0:T(8,128)(2,1)S(1)} %get-tuple-element.94), channel_id=1, source_target_pairs={{0,32},{32,64},{64,96},{1,33},{33,65},{65,97},{2,34},{34,66},{66,9... | collective-permute-start | bytes 98312 | tf_op jit(solution)/shard_map/ppermute | solution.py:539
  199.8 12.2 %all_to_all.52.part_ref = bf16[16,128,128]{2,1,0:T(8,128)(2,1)S(1)} all-to-all(bf16[16,128,128]{2,1,0:T(8,128)(2,1)S(1)} %broadcast_in_dim.54), channel_id=1, replica_groups={{0,2,4,6,8,10,12,14,16,18,20,22,24,26,28,30},{1,3,5,7,9,11,13,15,17,19,..., dimensions={0} | all-to-all | bytes 1048576 | tf_op jit(solution)/shard_map/all_to_all | solution.py:485
  212.0 3.4 %collective-permute-start.19 = (bf16[16,128,128]{2,1,0:T(8,128)(2,1)S(1)}, bf16[16,128,128]{2,1,0:T(8,128)(2,1)S(1)}, u32[]{:S(2)}, u32[]{:S(2)}) collective-permute-start(bf16[16,128,128]{2,1,0:T(8,128)(2,1)S(1)} %all_to_all.52.part_ref), channel_id=1, source_target_pairs={{0,1},{1,0},{2,3},{3,2},{4,5},{5,4},{6,7},{7,6},{8,9},{9,8},{10,11... | collective-permute-start | bytes 1572872 | tf_op jit(solution)/shard_map/ppermute | solution.py:489
  217.0 1.8 far.9
  218.9 17.1 %all_to_all.53.part_ref = bf16[16,112,256]{2,1,0:T(8,128)(2,1)S(1)} all-to-all(bf16[16,112,256]{2,1,0:T(8,128)(2,1)S(1)} %far.9), channel_id=1, replica_groups={{0,2,4,6,8,10,12,14,16,18,20,22,24,26,28,30},{1,3,5,7,9,11,13,15,17,19,..., dimensions={0} | all-to-all | bytes 1835008 | tf_op jit(solution)/shard_map/all_to_all | solution.py:485
  236.7 2.4 collective-permute-start.20
  (63 shorter events, 27.6 us)
Async XLA Ops:
  1.4 9.2 %collective-permute-start.2 = (bf16[128,128]{1,0:T(8,128)(2,1)S(1)}, bf16[128,128]{1,0:T(8,128)(2,1)S(1)}, u32[]{:S(2)}, u32[]{:S(2)}) collective-permute-start(bf16[128,128]{1,0:T(8,128)(2,1)S(1)} %get-tuple-element.64.refs_0_.taken_ref), channel_id=1, source_target_pairs={{0,24},{1,25},{2,26},{3,27},{4,28},{5,29},{6,30},{7,31},{8,0},{9,1... | collective-permute-start | bytes 98312 | tf_op jit(solution)/shard_map/ppermute | solution.py:391
  4.0 6.6 %collective-permute-start.1 = (bf16[128,128]{1,0:T(8,128)(2,1)S(1)}, bf16[128,128]{1,0:T(8,128)(2,1)S(1)}, u32[]{:S(2)}, u32[]{:S(2)}) collective-permute-start(bf16[128,128]{1,0:T(8,128)(2,1)S(1)} %get-tuple-element.64.refs_0_.taken_ref), channel_id=1, source_target_pairs={{0,16},{1,17},{2,18},{3,19},{4,20},{5,21},{6,22},{7,23},{8,24},{9,... | collective-permute-start | bytes 98312 | tf_op jit(solution)/shard_map/ppermute | solution.py:391
  4.5 6.1 %collective-permute-start = (bf16[128,128]{1,0:T(8,128)(2,1)S(1)}, bf16[128,128]{1,0:T(8,128)(2,1)S(1)}, u32[]{:S(2)}, u32[]{:S(2)}) collective-permute-start(bf16[128,128]{1,0:T(8,128)(2,1)S(1)} %get-tuple-element.64.refs_0_.taken_ref), channel_id=1, source_target_pairs={{0,8},{1,9},{2,10},{3,11},{4,12},{5,13},{6,14},{7,15},{8,16},{9,17... | collective-permute-start | bytes 98312 | tf_op jit(solution)/shard_map/ppermute | solution.py:391
  10.6 35.8 %collective-permute-start.7 = (bf16[4128,512]{1,0:T(8,128)(2,1)S(1)}, bf16[4128,512]{1,0:T(8,128)(2,1)S(1)}, u32[]{:S(2)}, u32[]{:S(2)}) collective-permute-start(bf16[4128,512]{1,0:T(8,128)(2,1)S(1)} %get-tuple-element.77), channel_id=1, source_target_pairs={{0,1},{1,0},{2,3},{3,2},{4,5},{5,4},{6,7},{7,6},{8,9},{9,8},{10,11... | collective-permute-start | bytes 12681224 | tf_op jit(solution)/shard_map/ppermute | solution.py:489
  12.2 10.7 %collective-permute-start.5 = (bf16[4,128,128]{2,1,0:T(8,128)(2,1)S(1)}, bf16[4,128,128]{2,1,0:T(8,128)(2,1)S(1)}, u32[]{:S(2)}, u32[]{:S(2)}) collective-permute-start(bf16[4,128,128]{2,1,0:T(8,128)(2,1)S(1)} %placed.2.refs_0_), channel_id=1, source_target_pairs={{0,6},{1,7},{2,0},{3,1},{4,2},{5,3},{6,4},{7,5},{8,14},{9,15},{10,... | collective-permute-start | bytes 393224 | tf_op jit(solution)/shard_map/ppermute | solution.py:391
  15.0 7.9 %collective-permute-start.4 = (bf16[4,128,128]{2,1,0:T(8,128)(2,1)S(1)}, bf16[4,128,128]{2,1,0:T(8,128)(2,1)S(1)}, u32[]{:S(2)}, u32[]{:S(2)}) collective-permute-start(bf16[4,128,128]{2,1,0:T(8,128)(2,1)S(1)} %placed.2.refs_0_), channel_id=1, source_target_pairs={{0,4},{1,5},{2,6},{3,7},{4,0},{5,1},{6,2},{7,3},{8,12},{9,13},{10,... | collective-permute-start | bytes 393224 | tf_op jit(solution)/shard_map/ppermute | solution.py:391
  15.3 9.4 %collective-permute-start.3 = (bf16[4,128,128]{2,1,0:T(8,128)(2,1)S(1)}, bf16[4,128,128]{2,1,0:T(8,128)(2,1)S(1)}, u32[]{:S(2)}, u32[]{:S(2)}) collective-permute-start(bf16[4,128,128]{2,1,0:T(8,128)(2,1)S(1)} %placed.2.refs_0_), channel_id=1, source_target_pairs={{0,2},{1,3},{2,4},{3,5},{4,6},{5,7},{6,0},{7,1},{8,10},{9,11},{10,... | collective-permute-start | bytes 393224 | tf_op jit(solution)/shard_map/ppermute | solution.py:391
  24.7 2.1 collective-permute-start.6
  47.2 3.3 %collective-permute-start.8 = (f32[64,256]{1,0:T(8,128)S(1)}, f32[64,256]{1,0:T(8,128)S(1)}, u32[]{:S(2)}, u32[]{:S(2)}) collective-permute-start(f32[64,256]{1,0:T(8,128)S(1)} %send.5), channel_id=1, source_target_pairs={{0,1},{1,0},{2,3},{3,2},{4,5},{5,4},{6,7},{7,6},{8,9},{9,8},{10,11... | collective-permute-start | bytes 196616 | tf_op jit(solution)/shard_map/ppermute | solution.py:489
  50.7 7.1 %collective-permute-start.9 = (bf16[128,128]{1,0:T(8,128)(2,1)S(1)}, bf16[128,128]{1,0:T(8,128)(2,1)S(1)}, u32[]{:S(2)}, u32[]{:S(2)}) collective-permute-start(bf16[128,128]{1,0:T(8,128)(2,1)S(1)} %get-tuple-element.79), channel_id=1, source_target_pairs={{0,32},{32,64},{64,96},{1,33},{33,65},{65,97},{2,34},{34,66},{66,9... | collective-permute-start | bytes 98312 | tf_op jit(solution)/shard_map/ppermute | solution.py:539
  70.2 5.0 %collective-permute-start.10 = (bf16[16,128,128]{2,1,0:T(8,128)(2,1)S(1)}, bf16[16,128,128]{2,1,0:T(8,128)(2,1)S(1)}, u32[]{:S(2)}, u32[]{:S(2)}) collective-permute-start(bf16[16,128,128]{2,1,0:T(8,128)(2,1)S(1)} %all_to_all.46.part_ref), channel_id=1, source_target_pairs={{0,1},{1,0},{2,3},{3,2},{4,5},{5,4},{6,7},{7,6},{8,9},{9,8},{10,11... | collective-permute-start | bytes 1572872 | tf_op jit(solution)/shard_map/ppermute | solution.py:489
  94.9 3.3 %collective-permute-start.11 = (f32[64,256]{1,0:T(8,128)S(1)}, f32[64,256]{1,0:T(8,128)S(1)}, u32[]{:S(2)}, u32[]{:S(2)}) collective-permute-start(f32[64,256]{1,0:T(8,128)S(1)} %send.6), channel_id=1, source_target_pairs={{0,1},{1,0},{2,3},{3,2},{4,5},{5,4},{6,7},{7,6},{8,9},{9,8},{10,11... | collective-permute-start | bytes 196616 | tf_op jit(solution)/shard_map/ppermute | solution.py:489
  98.3 6.8 %collective-permute-start.12 = (bf16[128,128]{1,0:T(8,128)(2,1)S(1)}, bf16[128,128]{1,0:T(8,128)(2,1)S(1)}, u32[]{:S(2)}, u32[]{:S(2)}) collective-permute-start(bf16[128,128]{1,0:T(8,128)(2,1)S(1)} %get-tuple-element.84), channel_id=1, source_target_pairs={{0,32},{32,64},{64,96},{1,33},{33,65},{65,97},{2,34},{34,66},{66,9... | collective-permute-start | bytes 98312 | tf_op jit(solution)/shard_map/ppermute | solution.py:539
  117.5 5.0 %collective-permute-start.13 = (bf16[16,128,128]{2,1,0:T(8,128)(2,1)S(1)}, bf16[16,128,128]{2,1,0:T(8,128)(2,1)S(1)}, u32[]{:S(2)}, u32[]{:S(2)}) collective-permute-start(bf16[16,128,128]{2,1,0:T(8,128)(2,1)S(1)} %all_to_all.48.part_ref), channel_id=1, source_target_pairs={{0,1},{1,0},{2,3},{3,2},{4,5},{5,4},{6,7},{7,6},{8,9},{9,8},{10,11... | collective-permute-start | bytes 1572872 | tf_op jit(solution)/shard_map/ppermute | solution.py:489
  142.2 3.3 %collective-permute-start.14 = (f32[64,256]{1,0:T(8,128)S(1)}, f32[64,256]{1,0:T(8,128)S(1)}, u32[]{:S(2)}, u32[]{:S(2)}) collective-permute-start(f32[64,256]{1,0:T(8,128)S(1)} %send.7), channel_id=1, source_target_pairs={{0,1},{1,0},{2,3},{3,2},{4,5},{5,4},{6,7},{7,6},{8,9},{9,8},{10,11... | collective-permute-start | bytes 196616 | tf_op jit(solution)/shard_map/ppermute | solution.py:489
  145.6 6.8 %collective-permute-start.15 = (bf16[128,128]{1,0:T(8,128)(2,1)S(1)}, bf16[128,128]{1,0:T(8,128)(2,1)S(1)}, u32[]{:S(2)}, u32[]{:S(2)}) collective-permute-start(bf16[128,128]{1,0:T(8,128)(2,1)S(1)} %get-tuple-element.89), channel_id=1, source_target_pairs={{0,32},{32,64},{64,96},{1,33},{33,65},{65,97},{2,34},{34,66},{66,9... | collective-permute-start | bytes 98312 | tf_op jit(solution)/shard_map/ppermute | solution.py:539
  164.7 5.0 %collective-permute-start.16 = (bf16[16,128,128]{2,1,0:T(8,128)(2,1)S(1)}, bf16[16,128,128]{2,1,0:T(8,128)(2,1)S(1)}, u32[]{:S(2)}, u32[]{:S(2)}) collective-permute-start(bf16[16,128,128]{2,1,0:T(8,128)(2,1)S(1)} %all_to_all.50.part_ref), channel_id=1, source_target_pairs={{0,1},{1,0},{2,3},{3,2},{4,5},{5,4},{6,7},{7,6},{8,9},{9,8},{10,11... | collective-permute-start | bytes 1572872 | tf_op jit(solution)/shard_map/ppermute | solution.py:489
  189.5 3.3 %collective-permute-start.17 = (f32[64,256]{1,0:T(8,128)S(1)}, f32[64,256]{1,0:T(8,128)S(1)}, u32[]{:S(2)}, u32[]{:S(2)}) collective-permute-start(f32[64,256]{1,0:T(8,128)S(1)} %send.8), channel_id=1, source_target_pairs={{0,1},{1,0},{2,3},{3,2},{4,5},{5,4},{6,7},{7,6},{8,9},{9,8},{10,11... | collective-permute-start | bytes 196616 | tf_op jit(solution)/shard_map/ppermute | solution.py:489
  192.9 6.8 %collective-permute-start.18 = (bf16[128,128]{1,0:T(8,128)(2,1)S(1)}, bf16[128,128]{1,0:T(8,128)(2,1)S(1)}, u32[]{:S(2)}, u32[]{:S(2)}) collective-permute-start(bf16[128,128]{1,0:T(8,128)(2,1)S(1)} %get-tuple-element.94), channel_id=1, source_target_pairs={{0,32},{32,64},{64,96},{1,33},{33,65},{65,97},{2,34},{34,66},{66,9... | collective-permute-start | bytes 98312 | tf_op jit(solution)/shard_map/ppermute | solution.py:539
  212.0 5.0 %collective-permute-start.19 = (bf16[16,128,128]{2,1,0:T(8,128)(2,1)S(1)}, bf16[16,128,128]{2,1,0:T(8,128)(2,1)S(1)}, u32[]{:S(2)}, u32[]{:S(2)}) collective-permute-start(bf16[16,128,128]{2,1,0:T(8,128)(2,1)S(1)} %all_to_all.52.part_ref), channel_id=1, source_target_pairs={{0,1},{1,0},{2,3},{3,2},{4,5},{5,4},{6,7},{7,6},{8,9},{9,8},{10,11... | collective-permute-start | bytes 1572872 | tf_op jit(solution)/shard_map/ppermute | solution.py:489
  236.7 3.3 %collective-permute-start.20 = (f32[64,256]{1,0:T(8,128)S(1)}, f32[64,256]{1,0:T(8,128)S(1)}, u32[]{:S(2)}, u32[]{:S(2)}) collective-permute-start(f32[64,256]{1,0:T(8,128)S(1)} %send.9), channel_id=1, source_target_pairs={{0,1},{1,0},{2,3},{3,2},{4,5},{5,4},{6,7},{7,6},{8,9},{9,8},{10,11... | collective-permute-start | bytes 196616 | tf_op jit(solution)/shard_map/ppermute | solution.py:489

commit v7 on v6

--- a/solution.py
+++ b/solution.py
@@ -63,7 +63,7 @@
                 place(chunk, 16, first, half, tile, column)
             return 0
 
-        lax.fori_loop(0, slots // 32, pair, 0)
+        lax.fori_loop(0, slots // 32, pair, 0, unroll=True)
         done = slots // 32 * 32
         half = 0
         while done < slots:
@@ -110,7 +110,7 @@
                             target[pl.ds(goal, 32), tile * 128 : (tile + 1) * 128] = piece
             return 0
 
-        lax.fori_loop(0, size // 6, step, 0)
+        lax.fori_loop(0, size // 6, step, 0, unroll=True)
         return 0
 
     lax.fori_loop(0, parts, one, 0)

time: 241 us -> 241 us (level)
  no operation moved by 1% of the time
where the time goes in v7:
time: 241 us; the launch traced here: 240 us
  blocking collectives  135 us (56%)
  starting transfers between devices  58.8 us (24%)
  Pallas kernels  37.1 us (15%)
  waiting for transfers between devices  8.65 us (4%)
    all_to_all x9, blocking collectives, exchanged(): return lax.all_to_all(value, 'tensor', 0, 0, axis_index_groups=same_core)  135 us
    ppermute x11, starting transfers between devices, swapped(): return lax.ppermute(value, 'tensor', [(i, i ^ 1) for i in range(2 * CHIPS)])  27.9 us
    ppermute x4, starting transfers between devices, local(): carried = lax.ppermute(ordered, 'segment', hops)  23.4 us
    pallas_call x2, Pallas kernels, pack(): pl.pallas_call(kernel, out_shape=[pltpu.VMEM(shape, jnp.bfloat16)] * resu...  11.3 us
    pallas_call x5, Pallas kernels, call_far(): pl.pallas_call(far_kernel, out_shape=jax.ShapeDtypeStruct((CHIPS, KEPT, 2...  9.21 us
    ppermute x6, starting transfers between devices, shifted_all(): parts.append(lax.ppermute(value, 'tensor', pairs))  7.46 us
    pallas_call x5, Pallas kernels, call_near(): pl.pallas_call(near_kernel, out_shape=(jax.ShapeDtypeStruct((2 * ROWS, GU...  6.17 us
  transfers between devices with their start and end apart: 21, of which 15 were waited for; matrix products, arithmetic and copies ran while one was open for 0% of the time, Pallas kernels for 10%

profile of v7, /device:TPU:65, one launch (start us, length us, event | category | flops | bytes accessed | tf_op | source)
XLA Modules:
  0.0 240.2 jit_solution(4179242328507215893)
XLA Ops:
  1.4 2.6 %collective-permute-start.2 = (bf16[128,128]{1,0:T(8,128)(2,1)S(1)}, bf16[128,128]{1,0:T(8,128)(2,1)S(1)}, u32[]{:S(2)}, u32[]{:S(2)}) collective-permute-start(bf16[128,128]{1,0:T(8,128)(2,1)S(1)} %get-tuple-element.64.refs_0_.taken_ref), channel_id=1, source_target_pairs={{0,24},{1,25},{2,26},{3,27},{4,28},{5,29},{6,30},{7,31},{8,0},{9,1... | collective-permute-start | bytes 98312 | tf_op jit(solution)/shard_map/ppermute | solution.py:391
  5.1 5.4 %pack_down.1 = (bf16[4128,512]{1,0:T(8,128)(2,1)S(1)}, bf16[4128,512]{1,0:T(8,128)(2,1)S(1)}) custom-call(s32[2,4,126]{2,1,0:T(4,128)S(1)} %get-tuple-element.65.goal_ref, bf16[126,4,4096]{2,1,0:T(4,128)(2,1)} %bitcast.17), custom_call_target="tpu_custom_call" | custom-call | bytes 41943040 | tf_op jit(solution)/shard_map/pack_down/pallas_call | solution.py:121
  12.1 2.7 %collective-permute-start.5 = (bf16[4,128,128]{2,1,0:T(8,128)(2,1)S(1)}, bf16[4,128,128]{2,1,0:T(8,128)(2,1)S(1)}, u32[]{:S(2)}, u32[]{:S(2)}) collective-permute-start(bf16[4,128,128]{2,1,0:T(8,128)(2,1)S(1)} %placed.2.refs_0_), channel_id=1, source_target_pairs={{0,6},{1,7},{2,0},{3,1},{4,2},{5,3},{6,4},{7,5},{8,14},{9,15},{10,... | collective-permute-start | bytes 393224 | tf_op jit(solution)/shard_map/ppermute | solution.py:391
  15.9 6.0 %pack_wide.1.refs_4_.weight_ref = bf16[4128,1792]{1,0:T(8,128)(2,1)S(1)} custom-call(s32[7,1,72]{2,1,0:T(1,128)S(1)} %get-tuple-element.69.goal_ref, bf16[7,72,4096]{2,1,0:T(8,128)(2,1)} %bitcast.18, bf16[7,72,4096]{2,1,0:T(8,128)(2,1)} %bitcast.19), custom_call_target="tpu_custom_call" | custom-call | bytes 41943040 | tf_op jit(solution)/shard_map/pack_wide/pallas_call | solution.py:121
  21.9 2.7 %collective-permute-done.3.refs_1_ = bf16[4,128,128]{2,1,0:T(8,128)(2,1)S(1)} collective-permute-done((bf16[4,128,128]{2,1,0:T(8,128)(2,1)S(1)}, bf16[4,128,128]{2,1,0:T(8,128)(2,1)S(1)}, u32[]{:S(2)}, u32[]{:S(2)}) %collective-permute-start.3) | collective-permute-done | bytes 131104 | tf_op jit(solution)/shard_map/ppermute | solution.py:391
  26.7 1.8 far.5
  28.6 17.4 %all_to_all.45.part_ref = bf16[16,112,256]{2,1,0:T(8,128)(2,1)S(1)} all-to-all(bf16[16,112,256]{2,1,0:T(8,128)(2,1)S(1)} %far.5), channel_id=1, replica_groups={{0,2,4,6,8,10,12,14,16,18,20,22,24,26,28,30},{1,3,5,7,9,11,13,15,17,19,..., dimensions={0} | all-to-all | bytes 1835008 | tf_op jit(solution)/shard_map/all_to_all | solution.py:485
  46.8 2.4 collective-permute-start.8
  50.3 6.1 %collective-permute-start.9 = (bf16[128,128]{1,0:T(8,128)(2,1)S(1)}, bf16[128,128]{1,0:T(8,128)(2,1)S(1)}, u32[]{:S(2)}, u32[]{:S(2)}) collective-permute-start(bf16[128,128]{1,0:T(8,128)(2,1)S(1)} %get-tuple-element.79), channel_id=1, source_target_pairs={{0,32},{32,64},{64,96},{1,33},{33,65},{65,97},{2,34},{34,66},{66,9... | collective-permute-start | bytes 98312 | tf_op jit(solution)/shard_map/ppermute | solution.py:539
  57.5 12.2 %all_to_all.46.part_ref = bf16[16,128,128]{2,1,0:T(8,128)(2,1)S(1)} all-to-all(bf16[16,128,128]{2,1,0:T(8,128)(2,1)S(1)} %broadcast_in_dim.25), channel_id=1, replica_groups={{0,2,4,6,8,10,12,14,16,18,20,22,24,26,28,30},{1,3,5,7,9,11,13,15,17,19,..., dimensions={0} | all-to-all | bytes 1048576 | tf_op jit(solution)/shard_map/all_to_all | solution.py:485
  69.8 3.4 %collective-permute-start.10 = (bf16[16,128,128]{2,1,0:T(8,128)(2,1)S(1)}, bf16[16,128,128]{2,1,0:T(8,128)(2,1)S(1)}, u32[]{:S(2)}, u32[]{:S(2)}) collective-permute-start(bf16[16,128,128]{2,1,0:T(8,128)(2,1)S(1)} %all_to_all.46.part_ref), channel_id=1, source_target_pairs={{0,1},{1,0},{2,3},{3,2},{4,5},{5,4},{6,7},{7,6},{8,9},{9,8},{10,11... | collective-permute-start | bytes 1572872 | tf_op jit(solution)/shard_map/ppermute | solution.py:489
  74.7 1.8 far.6
  76.6 17.1 %all_to_all.47.part_ref = bf16[16,112,256]{2,1,0:T(8,128)(2,1)S(1)} all-to-all(bf16[16,112,256]{2,1,0:T(8,128)(2,1)S(1)} %far.6), channel_id=1, replica_groups={{0,2,4,6,8,10,12,14,16,18,20,22,24,26,28,30},{1,3,5,7,9,11,13,15,17,19,..., dimensions={0} | all-to-all | bytes 1835008 | tf_op jit(solution)/shard_map/all_to_all | solution.py:485
  94.5 2.4 collective-permute-start.11
  97.9 5.8 %collective-permute-start.12 = (bf16[128,128]{1,0:T(8,128)(2,1)S(1)}, bf16[128,128]{1,0:T(8,128)(2,1)S(1)}, u32[]{:S(2)}, u32[]{:S(2)}) collective-permute-start(bf16[128,128]{1,0:T(8,128)(2,1)S(1)} %get-tuple-element.84), channel_id=1, source_target_pairs={{0,32},{32,64},{64,96},{1,33},{33,65},{65,97},{2,34},{34,66},{66,9... | collective-permute-start | bytes 98312 | tf_op jit(solution)/shard_map/ppermute | solution.py:539
  104.8 12.2 %all_to_all.48.part_ref = bf16[16,128,128]{2,1,0:T(8,128)(2,1)S(1)} all-to-all(bf16[16,128,128]{2,1,0:T(8,128)(2,1)S(1)} %broadcast_in_dim.52), channel_id=1, replica_groups={{0,2,4,6,8,10,12,14,16,18,20,22,24,26,28,30},{1,3,5,7,9,11,13,15,17,19,..., dimensions={0} | all-to-all | bytes 1048576 | tf_op jit(solution)/shard_map/all_to_all | solution.py:485
  117.0 3.4 %collective-permute-start.13 = (bf16[16,128,128]{2,1,0:T(8,128)(2,1)S(1)}, bf16[16,128,128]{2,1,0:T(8,128)(2,1)S(1)}, u32[]{:S(2)}, u32[]{:S(2)}) collective-permute-start(bf16[16,128,128]{2,1,0:T(8,128)(2,1)S(1)} %all_to_all.48.part_ref), channel_id=1, source_target_pairs={{0,1},{1,0},{2,3},{3,2},{4,5},{5,4},{6,7},{7,6},{8,9},{9,8},{10,11... | collective-permute-start | bytes 1572872 | tf_op jit(solution)/shard_map/ppermute | solution.py:489
  122.0 1.8 far.7
  123.9 17.1 %all_to_all.49.part_ref = bf16[16,112,256]{2,1,0:T(8,128)(2,1)S(1)} all-to-all(bf16[16,112,256]{2,1,0:T(8,128)(2,1)S(1)} %far.7), channel_id=1, replica_groups={{0,2,4,6,8,10,12,14,16,18,20,22,24,26,28,30},{1,3,5,7,9,11,13,15,17,19,..., dimensions={0} | all-to-all | bytes 1835008 | tf_op jit(solution)/shard_map/all_to_all | solution.py:485
  141.8 2.4 collective-permute-start.14
  145.2 5.8 %collective-permute-start.15 = (bf16[128,128]{1,0:T(8,128)(2,1)S(1)}, bf16[128,128]{1,0:T(8,128)(2,1)S(1)}, u32[]{:S(2)}, u32[]{:S(2)}) collective-permute-start(bf16[128,128]{1,0:T(8,128)(2,1)S(1)} %get-tuple-element.89), channel_id=1, source_target_pairs={{0,32},{32,64},{64,96},{1,33},{33,65},{65,97},{2,34},{34,66},{66,9... | collective-permute-start | bytes 98312 | tf_op jit(solution)/shard_map/ppermute | solution.py:539
  152.1 12.2 %all_to_all.50.part_ref = bf16[16,128,128]{2,1,0:T(8,128)(2,1)S(1)} all-to-all(bf16[16,128,128]{2,1,0:T(8,128)(2,1)S(1)} %broadcast_in_dim.53), channel_id=1, replica_groups={{0,2,4,6,8,10,12,14,16,18,20,22,24,26,28,30},{1,3,5,7,9,11,13,15,17,19,..., dimensions={0} | all-to-all | bytes 1048576 | tf_op jit(solution)/shard_map/all_to_all | solution.py:485
  164.3 3.4 %collective-permute-start.16 = (bf16[16,128,128]{2,1,0:T(8,128)(2,1)S(1)}, bf16[16,128,128]{2,1,0:T(8,128)(2,1)S(1)}, u32[]{:S(2)}, u32[]{:S(2)}) collective-permute-start(bf16[16,128,128]{2,1,0:T(8,128)(2,1)S(1)} %all_to_all.50.part_ref), channel_id=1, source_target_pairs={{0,1},{1,0},{2,3},{3,2},{4,5},{5,4},{6,7},{7,6},{8,9},{9,8},{10,11... | collective-permute-start | bytes 1572872 | tf_op jit(solution)/shard_map/ppermute | solution.py:489
  169.3 1.8 far.8
  171.2 17.1 %all_to_all.51.part_ref = bf16[16,112,256]{2,1,0:T(8,128)(2,1)S(1)} all-to-all(bf16[16,112,256]{2,1,0:T(8,128)(2,1)S(1)} %far.8), channel_id=1, replica_groups={{0,2,4,6,8,10,12,14,16,18,20,22,24,26,28,30},{1,3,5,7,9,11,13,15,17,19,..., dimensions={0} | all-to-all | bytes 1835008 | tf_op jit(solution)/shard_map/all_to_all | solution.py:485
  189.0 2.4 collective-permute-start.17
  192.5 5.8 %collective-permute-start.18 = (bf16[128,128]{1,0:T(8,128)(2,1)S(1)}, bf16[128,128]{1,0:T(8,128)(2,1)S(1)}, u32[]{:S(2)}, u32[]{:S(2)}) collective-permute-start(bf16[128,128]{1,0:T(8,128)(2,1)S(1)} %get-tuple-element.94), channel_id=1, source_target_pairs={{0,32},{32,64},{64,96},{1,33},{33,65},{65,97},{2,34},{34,66},{66,9... | collective-permute-start | bytes 98312 | tf_op jit(solution)/shard_map/ppermute | solution.py:539
  199.4 12.2 %all_to_all.52.part_ref = bf16[16,128,128]{2,1,0:T(8,128)(2,1)S(1)} all-to-all(bf16[16,128,128]{2,1,0:T(8,128)(2,1)S(1)} %broadcast_in_dim.54), channel_id=1, replica_groups={{0,2,4,6,8,10,12,14,16,18,20,22,24,26,28,30},{1,3,5,7,9,11,13,15,17,19,..., dimensions={0} | all-to-all | bytes 1048576 | tf_op jit(solution)/shard_map/all_to_all | solution.py:485
  211.6 3.4 %collective-permute-start.19 = (bf16[16,128,128]{2,1,0:T(8,128)(2,1)S(1)}, bf16[16,128,128]{2,1,0:T(8,128)(2,1)S(1)}, u32[]{:S(2)}, u32[]{:S(2)}) collective-permute-start(bf16[16,128,128]{2,1,0:T(8,128)(2,1)S(1)} %all_to_all.52.part_ref), channel_id=1, source_target_pairs={{0,1},{1,0},{2,3},{3,2},{4,5},{5,4},{6,7},{7,6},{8,9},{9,8},{10,11... | collective-permute-start | bytes 1572872 | tf_op jit(solution)/shard_map/ppermute | solution.py:489
  216.6 1.8 far.9
  218.4 17.1 %all_to_all.53.part_ref = bf16[16,112,256]{2,1,0:T(8,128)(2,1)S(1)} all-to-all(bf16[16,112,256]{2,1,0:T(8,128)(2,1)S(1)} %far.9), channel_id=1, replica_groups={{0,2,4,6,8,10,12,14,16,18,20,22,24,26,28,30},{1,3,5,7,9,11,13,15,17,19,..., dimensions={0} | all-to-all | bytes 1835008 | tf_op jit(solution)/shard_map/all_to_all | solution.py:485
  236.3 2.4 collective-permute-start.20
  (63 shorter events, 27.6 us)
Async XLA Ops:
  1.4 9.0 %collective-permute-start.2 = (bf16[128,128]{1,0:T(8,128)(2,1)S(1)}, bf16[128,128]{1,0:T(8,128)(2,1)S(1)}, u32[]{:S(2)}, u32[]{:S(2)}) collective-permute-start(bf16[128,128]{1,0:T(8,128)(2,1)S(1)} %get-tuple-element.64.refs_0_.taken_ref), channel_id=1, source_target_pairs={{0,24},{1,25},{2,26},{3,27},{4,28},{5,29},{6,30},{7,31},{8,0},{9,1... | collective-permute-start | bytes 98312 | tf_op jit(solution)/shard_map/ppermute | solution.py:391
  4.0 6.5 %collective-permute-start.1 = (bf16[128,128]{1,0:T(8,128)(2,1)S(1)}, bf16[128,128]{1,0:T(8,128)(2,1)S(1)}, u32[]{:S(2)}, u32[]{:S(2)}) collective-permute-start(bf16[128,128]{1,0:T(8,128)(2,1)S(1)} %get-tuple-element.64.refs_0_.taken_ref), channel_id=1, source_target_pairs={{0,16},{1,17},{2,18},{3,19},{4,20},{5,21},{6,22},{7,23},{8,24},{9,... | collective-permute-start | bytes 98312 | tf_op jit(solution)/shard_map/ppermute | solution.py:391
  4.5 6.0 %collective-permute-start = (bf16[128,128]{1,0:T(8,128)(2,1)S(1)}, bf16[128,128]{1,0:T(8,128)(2,1)S(1)}, u32[]{:S(2)}, u32[]{:S(2)}) collective-permute-start(bf16[128,128]{1,0:T(8,128)(2,1)S(1)} %get-tuple-element.64.refs_0_.taken_ref), channel_id=1, source_target_pairs={{0,8},{1,9},{2,10},{3,11},{4,12},{5,13},{6,14},{7,15},{8,16},{9,17... | collective-permute-start | bytes 98312 | tf_op jit(solution)/shard_map/ppermute | solution.py:391
  10.5 35.5 %collective-permute-start.7 = (bf16[4128,512]{1,0:T(8,128)(2,1)S(1)}, bf16[4128,512]{1,0:T(8,128)(2,1)S(1)}, u32[]{:S(2)}, u32[]{:S(2)}) collective-permute-start(bf16[4128,512]{1,0:T(8,128)(2,1)S(1)} %get-tuple-element.77), channel_id=1, source_target_pairs={{0,1},{1,0},{2,3},{3,2},{4,5},{5,4},{6,7},{7,6},{8,9},{9,8},{10,11... | collective-permute-start | bytes 12681224 | tf_op jit(solution)/shard_map/ppermute | solution.py:489
  12.1 9.8 %collective-permute-start.5 = (bf16[4,128,128]{2,1,0:T(8,128)(2,1)S(1)}, bf16[4,128,128]{2,1,0:T(8,128)(2,1)S(1)}, u32[]{:S(2)}, u32[]{:S(2)}) collective-permute-start(bf16[4,128,128]{2,1,0:T(8,128)(2,1)S(1)} %placed.2.refs_0_), channel_id=1, source_target_pairs={{0,6},{1,7},{2,0},{3,1},{4,2},{5,3},{6,4},{7,5},{8,14},{9,15},{10,... | collective-permute-start | bytes 393224 | tf_op jit(solution)/shard_map/ppermute | solution.py:391
  14.9 7.1 %collective-permute-start.4 = (bf16[4,128,128]{2,1,0:T(8,128)(2,1)S(1)}, bf16[4,128,128]{2,1,0:T(8,128)(2,1)S(1)}, u32[]{:S(2)}, u32[]{:S(2)}) collective-permute-start(bf16[4,128,128]{2,1,0:T(8,128)(2,1)S(1)} %placed.2.refs_0_), channel_id=1, source_target_pairs={{0,4},{1,5},{2,6},{3,7},{4,0},{5,1},{6,2},{7,3},{8,12},{9,13},{10,... | collective-permute-start | bytes 393224 | tf_op jit(solution)/shard_map/ppermute | solution.py:391
  15.2 9.4 %collective-permute-start.3 = (bf16[4,128,128]{2,1,0:T(8,128)(2,1)S(1)}, bf16[4,128,128]{2,1,0:T(8,128)(2,1)S(1)}, u32[]{:S(2)}, u32[]{:S(2)}) collective-permute-start(bf16[4,128,128]{2,1,0:T(8,128)(2,1)S(1)} %placed.2.refs_0_), channel_id=1, source_target_pairs={{0,2},{1,3},{2,4},{3,5},{4,6},{5,7},{6,0},{7,1},{8,10},{9,11},{10,... | collective-permute-start | bytes 393224 | tf_op jit(solution)/shard_map/ppermute | solution.py:391
  24.6 2.1 collective-permute-start.6
  46.8 3.3 %collective-permute-start.8 = (f32[64,256]{1,0:T(8,128)S(1)}, f32[64,256]{1,0:T(8,128)S(1)}, u32[]{:S(2)}, u32[]{:S(2)}) collective-permute-start(f32[64,256]{1,0:T(8,128)S(1)} %send.5), channel_id=1, source_target_pairs={{0,1},{1,0},{2,3},{3,2},{4,5},{5,4},{6,7},{7,6},{8,9},{9,8},{10,11... | collective-permute-start | bytes 196616 | tf_op jit(solution)/shard_map/ppermute | solution.py:489
  50.3 7.1 %collective-permute-start.9 = (bf16[128,128]{1,0:T(8,128)(2,1)S(1)}, bf16[128,128]{1,0:T(8,128)(2,1)S(1)}, u32[]{:S(2)}, u32[]{:S(2)}) collective-permute-start(bf16[128,128]{1,0:T(8,128)(2,1)S(1)} %get-tuple-element.79), channel_id=1, source_target_pairs={{0,32},{32,64},{64,96},{1,33},{33,65},{65,97},{2,34},{34,66},{66,9... | collective-permute-start | bytes 98312 | tf_op jit(solution)/shard_map/ppermute | solution.py:539
  69.8 5.0 %collective-permute-start.10 = (bf16[16,128,128]{2,1,0:T(8,128)(2,1)S(1)}, bf16[16,128,128]{2,1,0:T(8,128)(2,1)S(1)}, u32[]{:S(2)}, u32[]{:S(2)}) collective-permute-start(bf16[16,128,128]{2,1,0:T(8,128)(2,1)S(1)} %all_to_all.46.part_ref), channel_id=1, source_target_pairs={{0,1},{1,0},{2,3},{3,2},{4,5},{5,4},{6,7},{7,6},{8,9},{9,8},{10,11... | collective-permute-start | bytes 1572872 | tf_op jit(solution)/shard_map/ppermute | solution.py:489
  94.5 3.3 %collective-permute-start.11 = (f32[64,256]{1,0:T(8,128)S(1)}, f32[64,256]{1,0:T(8,128)S(1)}, u32[]{:S(2)}, u32[]{:S(2)}) collective-permute-start(f32[64,256]{1,0:T(8,128)S(1)} %send.6), channel_id=1, source_target_pairs={{0,1},{1,0},{2,3},{3,2},{4,5},{5,4},{6,7},{7,6},{8,9},{9,8},{10,11... | collective-permute-start | bytes 196616 | tf_op jit(solution)/shard_map/ppermute | solution.py:489
  97.9 6.8 %collective-permute-start.12 = (bf16[128,128]{1,0:T(8,128)(2,1)S(1)}, bf16[128,128]{1,0:T(8,128)(2,1)S(1)}, u32[]{:S(2)}, u32[]{:S(2)}) collective-permute-start(bf16[128,128]{1,0:T(8,128)(2,1)S(1)} %get-tuple-element.84), channel_id=1, source_target_pairs={{0,32},{32,64},{64,96},{1,33},{33,65},{65,97},{2,34},{34,66},{66,9... | collective-permute-start | bytes 98312 | tf_op jit(solution)/shard_map/ppermute | solution.py:539
  117.0 5.0 %collective-permute-start.13 = (bf16[16,128,128]{2,1,0:T(8,128)(2,1)S(1)}, bf16[16,128,128]{2,1,0:T(8,128)(2,1)S(1)}, u32[]{:S(2)}, u32[]{:S(2)}) collective-permute-start(bf16[16,128,128]{2,1,0:T(8,128)(2,1)S(1)} %all_to_all.48.part_ref), channel_id=1, source_target_pairs={{0,1},{1,0},{2,3},{3,2},{4,5},{5,4},{6,7},{7,6},{8,9},{9,8},{10,11... | collective-permute-start | bytes 1572872 | tf_op jit(solution)/shard_map/ppermute | solution.py:489
  141.8 3.3 %collective-permute-start.14 = (f32[64,256]{1,0:T(8,128)S(1)}, f32[64,256]{1,0:T(8,128)S(1)}, u32[]{:S(2)}, u32[]{:S(2)}) collective-permute-start(f32[64,256]{1,0:T(8,128)S(1)} %send.7), channel_id=1, source_target_pairs={{0,1},{1,0},{2,3},{3,2},{4,5},{5,4},{6,7},{7,6},{8,9},{9,8},{10,11... | collective-permute-start | bytes 196616 | tf_op jit(solution)/shard_map/ppermute | solution.py:489
  145.2 6.8 %collective-permute-start.15 = (bf16[128,128]{1,0:T(8,128)(2,1)S(1)}, bf16[128,128]{1,0:T(8,128)(2,1)S(1)}, u32[]{:S(2)}, u32[]{:S(2)}) collective-permute-start(bf16[128,128]{1,0:T(8,128)(2,1)S(1)} %get-tuple-element.89), channel_id=1, source_target_pairs={{0,32},{32,64},{64,96},{1,33},{33,65},{65,97},{2,34},{34,66},{66,9... | collective-permute-start | bytes 98312 | tf_op jit(solution)/shard_map/ppermute | solution.py:539
  164.3 5.0 %collective-permute-start.16 = (bf16[16,128,128]{2,1,0:T(8,128)(2,1)S(1)}, bf16[16,128,128]{2,1,0:T(8,128)(2,1)S(1)}, u32[]{:S(2)}, u32[]{:S(2)}) collective-permute-start(bf16[16,128,128]{2,1,0:T(8,128)(2,1)S(1)} %all_to_all.50.part_ref), channel_id=1, source_target_pairs={{0,1},{1,0},{2,3},{3,2},{4,5},{5,4},{6,7},{7,6},{8,9},{9,8},{10,11... | collective-permute-start | bytes 1572872 | tf_op jit(solution)/shard_map/ppermute | solution.py:489
  189.0 3.3 %collective-permute-start.17 = (f32[64,256]{1,0:T(8,128)S(1)}, f32[64,256]{1,0:T(8,128)S(1)}, u32[]{:S(2)}, u32[]{:S(2)}) collective-permute-start(f32[64,256]{1,0:T(8,128)S(1)} %send.8), channel_id=1, source_target_pairs={{0,1},{1,0},{2,3},{3,2},{4,5},{5,4},{6,7},{7,6},{8,9},{9,8},{10,11... | collective-permute-start | bytes 196616 | tf_op jit(solution)/shard_map/ppermute | solution.py:489
  192.5 6.8 %collective-permute-start.18 = (bf16[128,128]{1,0:T(8,128)(2,1)S(1)}, bf16[128,128]{1,0:T(8,128)(2,1)S(1)}, u32[]{:S(2)}, u32[]{:S(2)}) collective-permute-start(bf16[128,128]{1,0:T(8,128)(2,1)S(1)} %get-tuple-element.94), channel_id=1, source_target_pairs={{0,32},{32,64},{64,96},{1,33},{33,65},{65,97},{2,34},{34,66},{66,9... | collective-permute-start | bytes 98312 | tf_op jit(solution)/shard_map/ppermute | solution.py:539
  211.6 5.0 %collective-permute-start.19 = (bf16[16,128,128]{2,1,0:T(8,128)(2,1)S(1)}, bf16[16,128,128]{2,1,0:T(8,128)(2,1)S(1)}, u32[]{:S(2)}, u32[]{:S(2)}) collective-permute-start(bf16[16,128,128]{2,1,0:T(8,128)(2,1)S(1)} %all_to_all.52.part_ref), channel_id=1, source_target_pairs={{0,1},{1,0},{2,3},{3,2},{4,5},{5,4},{6,7},{7,6},{8,9},{9,8},{10,11... | collective-permute-start | bytes 1572872 | tf_op jit(solution)/shard_map/ppermute | solution.py:489
  236.3 3.3 %collective-permute-start.20 = (f32[64,256]{1,0:T(8,128)S(1)}, f32[64,256]{1,0:T(8,128)S(1)}, u32[]{:S(2)}, u32[]{:S(2)}) collective-permute-start(f32[64,256]{1,0:T(8,128)S(1)} %send.9), channel_id=1, source_target_pairs={{0,1},{1,0},{2,3},{3,2},{4,5},{5,4},{6,7},{7,6},{8,9},{9,8},{10,11... | collective-permute-start | bytes 196616 | tf_op jit(solution)/shard_map/ppermute | solution.py:489
